TPU v7x, 32 devices: a whole 2x2x4 slice. The times are simulated.
32 devices in a mesh: fsdp: 4 (over y, x), ctx: 4 (over z), tp: 2 (over core).
Axes of the slice: x: 2, y: 2, z: 4, core: 2. Of those that a mesh axis runs over, the one named last changes fastest.
Arguments:
- tokens: bfloat16 [4, 2048, 1024], P('fsdp', 'ctx'), may hold values from -6 to 6
- segment_ids: int32 [4, 2048], P('fsdp', 'ctx'), may hold values from 0 to 10, as said below
- positions: int32 [4, 2048], P('fsdp', 'ctx'), may hold values from 0 to 2047, as said below
- attention_gain: bfloat16 [1024], P('fsdp'), may hold values from 0.099609375 to 1.8984375
- attention_shift: bfloat16 [1024], P('fsdp'), may hold values from -1.75 to 1.75
- feedforward_gain: bfloat16 [1024], P('fsdp'), may hold values from 0.099609375 to 1.8984375
- feedforward_shift: bfloat16 [1024], P('fsdp'), may hold values from -1.75 to 1.75
- joint_weight: bfloat16 [1024, 3, 1024], P('fsdp', None, 'tp'), may hold values from -8 to 8
- joint_bias: bfloat16 [3, 1024], P(None, ('tp', 'fsdp')), may hold values from -3 to 3
- output_weight: bfloat16 [1024, 1024], P('tp', 'fsdp'), may hold values from -1.5 to 1.5
- output_bias: bfloat16 [1024], P('fsdp'), may hold values from -1.75 to 1.75
- up_weight: bfloat16 [1024, 4096], P('fsdp', 'tp'), may hold values from -0.1875 to 0.1875
- up_bias: bfloat16 [4096], P(('tp', 'fsdp')), may hold values from -3 to 3
- down_weight: bfloat16 [4096, 1024], P('tp', 'fsdp'), may hold values from -0.09375 to 0.09375
- down_bias: bfloat16 [1024], P('fsdp'), may hold values from -1.75 to 1.75
- cotangent: float32 [4, 2048, 1024], P('fsdp', 'ctx'), may hold values from -6 to 6
Outputs:
- result: float32 [4, 2048, 1024], P('fsdp', 'ctx')
- tokens_grad: float32 [4, 2048, 1024], P('fsdp', 'ctx')
- attention_gain_grad: float32 [1024], P('fsdp')
- attention_shift_grad: float32 [1024], P('fsdp')
- feedforward_gain_grad: float32 [1024], P('fsdp')
- feedforward_shift_grad: float32 [1024], P('fsdp')
- joint_weight_grad: float32 [1024, 3, 1024], P('fsdp', None, 'tp')
- joint_bias_grad: float32 [3, 1024], P(None, ('tp', 'fsdp'))
- output_weight_grad: float32 [1024, 1024], P('tp', 'fsdp')
- output_bias_grad: float32 [1024], P('fsdp')
- up_weight_grad: float32 [1024, 4096], P('fsdp', 'tp')
- up_bias_grad: float32 [4096], P(('tp', 'fsdp'))
- down_weight_grad: float32 [4096, 1024], P('tp', 'fsdp')
- down_bias_grad: float32 [1024], P('fsdp')
Inputs may be any that keep to these rules, and one draw needn't show every extreme that they name: `segment_ids`: along each sequence the ids start at 0 and rise by one at each document's first token; a document holds 204 to 2048 tokens, the last one cut at the sequence's end. The first sequence is one document; the last sequence is documents of 204 tokens. `positions`: each token's offset from the first token of its document; the first sequence is one document.
All inputs are finite; a program needn't handle non-finite values.
Results may differ from a plain program's by a relative error of at most 0.011.
Values may be sent and summed in bfloat16 or wider, within the bound.
No kernel may reach another device: no remote copies, remote signals or barrier semaphores. Data moves between devices by JAX's collectives and lax.ppermute only.
A program may use at most 192 MiB of HBM per device.

v0:
```python
import jax
import jax.numpy as jnp
from jax import lax
from jax.sharding import PartitionSpec as P

HD = 64
ROT = 16


EPS = 1e-05
ROPE_BASE = 10000.0


def rope_tables(offsets):
    half_dim = ROT // 2
    freq = ROPE_BASE ** (-(jnp.arange(half_dim, dtype=jnp.float32) * 2.0 / ROT))
    angle = offsets.astype(jnp.float32)[:, None] * freq[None, :]
    return (jnp.cos(angle)[:, None, :], jnp.sin(angle)[:, None, :])


def rotate(tensor, cosine, sine):
    half_dim = ROT // 2
    front = tensor[..., :half_dim]
    middle = tensor[..., half_dim:ROT]
    return jnp.concatenate(
        [front * cosine - middle * sine, middle * cosine + front * sine, tensor[..., ROT:]], axis=-1
    )


def unrotate(grads, cosine, sine):
    half_dim = ROT // 2
    front = grads[..., :half_dim]
    middle = grads[..., half_dim:ROT]
    return jnp.concatenate(
        [front * cosine + middle * sine, middle * cosine - front * sine, grads[..., ROT:]], axis=-1
    )


def normalize(rows):
    center = jnp.mean(rows, -1, keepdims=True)
    centred = rows - center
    spread = jnp.mean(centred * centred, -1, keepdims=True)
    rstd = lax.rsqrt(spread + EPS)
    return (centred * rstd, rstd)


def norm_back(upstream, normed, rstd, gain):
    scaled = upstream * gain
    return rstd * (
        scaled
        - jnp.mean(scaled, -1, keepdims=True)
        - normed * jnp.mean(scaled * normed, -1, keepdims=True)
    )


def masked_scores(query_blk, query_index, query_seg, keys, key_seg):
    scores = jnp.einsum(
        "qhe,khe->hqk", query_blk, keys, preferred_element_type=jnp.float32
    ) * HD ** (-0.5)
    key_index = jnp.arange(keys.shape[0], dtype=jnp.int32)
    allowed = (key_seg[None, :] == query_seg[:, None]) & (
        key_index[None, :] <= query_index[:, None]
    )
    return jnp.where(allowed[None], scores, -jnp.inf)


def local(
    tokens,
    segment_ids,
    positions,
    attention_gain,
    attention_shift,
    feedforward_gain,
    feedforward_shift,
    joint_weight,
    joint_bias,
    output_weight,
    output_bias,
    up_weight,
    up_bias,
    down_weight,
    down_bias,
    cotangent,
):
    f32 = jnp.float32
    bf16 = jnp.bfloat16
    scale = HD ** (-0.5)
    small = jnp.stack(
        [
            attention_gain,
            attention_shift,
            feedforward_gain,
            feedforward_shift,
            output_bias,
            down_bias,
        ]
    )
    full_joint, full_output, full_up, full_down, full_small, full_jbias, full_upbias = (
        lax.all_gather(joint_weight, "fsdp", axis=0, tiled=True),
        lax.all_gather(output_weight, "fsdp", axis=1, tiled=True),
        lax.all_gather(up_weight, "fsdp", axis=0, tiled=True),
        lax.all_gather(down_weight, "fsdp", axis=1, tiled=True),
        lax.all_gather(small, "fsdp", axis=1, tiled=True),
        lax.all_gather(joint_bias, "fsdp", axis=1, tiled=True),
        lax.all_gather(up_bias, "fsdp", axis=0, tiled=True),
    )
    params = full_small.astype(f32)
    gain_one = params[0]
    shift_one = params[1]
    gain_two = params[2]
    shift_two = params[3]
    rows = tokens[0].astype(f32)
    count_rows = rows.shape[0]
    local_width = joint_weight.shape[2]
    heads_here = local_width // HD
    normed, rstd = normalize(rows)
    first = (normed * gain_one + shift_one).astype(bf16)
    second = (normed * gain_two + shift_two).astype(bf16)
    joint = (
        jnp.einsum("nd,dpe->npe", first, full_joint, preferred_element_type=f32)
        + full_jbias.astype(f32)[None]
    )
    cosine, sine = rope_tables(positions[0])
    queries = rotate(joint[:, 0].reshape(count_rows, heads_here, HD), cosine, sine).astype(bf16)
    keys_here = rotate(joint[:, 1].reshape(count_rows, heads_here, HD), cosine, sine).astype(bf16)
    values_here = joint[:, 2].reshape(count_rows, heads_here, HD).astype(bf16)
    seg_here = segment_ids[0]
    all_keys, all_values, all_segs = (
        lax.all_gather(keys_here, "ctx", axis=0, tiled=True),
        lax.all_gather(values_here, "ctx", axis=0, tiled=True),
        lax.all_gather(seg_here.astype(bf16), "ctx", axis=0, tiled=True),
    )
    key_seg = all_segs.astype(f32)
    query_seg = seg_here.astype(f32)
    query_index = lax.axis_index("ctx") * count_rows + jnp.arange(count_rows, dtype=jnp.int32)
    block = min(512, count_rows)
    count_blocks = count_rows // block
    query_blocks = queries.reshape(count_blocks, block, heads_here, HD)
    index_blocks = query_index.reshape(count_blocks, block)
    seg_blocks = query_seg.reshape(count_blocks, block)

    def forward_block(args):
        query_blk, block_index, block_seg = args
        scores = masked_scores(query_blk, block_index, block_seg, all_keys, key_seg)
        top = jnp.max(scores, -1, keepdims=True)
        lse = top + jnp.log(jnp.sum(jnp.exp(scores - top), -1, keepdims=True))
        probs = jnp.exp(scores - lse).astype(bf16)
        mixed = jnp.einsum("hqk,khe->qhe", probs, all_values, preferred_element_type=f32)
        return (mixed, lse[..., 0])

    context32, lse_all = lax.map(forward_block, (query_blocks, index_blocks, seg_blocks))
    context32 = context32.reshape(count_rows, local_width)
    context = context32.astype(bf16)
    upper = jnp.dot(second, full_up, preferred_element_type=f32) + full_upbias.astype(f32)
    activated = jax.nn.gelu(upper, approximate=False).astype(bf16)
    partial_value = jnp.dot(context, full_output, preferred_element_type=f32) + jnp.dot(
        activated, full_down, preferred_element_type=f32
    )
    mixed_all = lax.psum(partial_value, "tp")
    result = rows + mixed_all + params[4] + params[5]
    back_joint, back_output, back_up, back_down = (
        lax.all_gather(joint_weight, "fsdp", axis=0, tiled=True),
        lax.all_gather(output_weight, "fsdp", axis=1, tiled=True),
        lax.all_gather(up_weight, "fsdp", axis=0, tiled=True),
        lax.all_gather(down_weight, "fsdp", axis=1, tiled=True),
    )
    cot = cotangent[0]
    cot_b = cot.astype(bf16)
    grad_output_w = jnp.dot(context.T, cot_b, preferred_element_type=f32)
    bias_sum = jnp.sum(cot, 0)
    grad_down_w = jnp.dot(activated.T, cot_b, preferred_element_type=f32)
    d_act = jnp.einsum("nd,fd->nf", cot_b, back_down, preferred_element_type=f32)
    unused, gelu_back = jax.vjp(lambda value: jax.nn.gelu(value, approximate=False), upper)
    d_upper = gelu_back(d_act)[0]
    d_upper_b = d_upper.astype(bf16)
    grad_up_w = jnp.dot(second.T, d_upper_b, preferred_element_type=f32)
    grad_up_b = jnp.sum(d_upper, 0)
    d_second_part = jnp.einsum("nf,df->nd", d_upper_b, back_up, preferred_element_type=f32)
    d_context = (
        jnp.einsum("nd,wd->nw", cot_b, back_output, preferred_element_type=f32)
        .astype(bf16)
        .reshape(count_rows, heads_here, HD)
    )
    delta = jnp.sum(d_context.astype(f32) * context32.reshape(count_rows, heads_here, HD), -1)
    dctx_blocks = d_context.reshape(count_blocks, block, heads_here, HD)

    def backward_block(args):
        query_blk, block_index, block_seg, dctx_blk, delta_blk, lse_blk = args
        scores = masked_scores(query_blk, block_index, block_seg, all_keys, key_seg)
        probs = jnp.exp(scores - lse_blk[..., None]).astype(bf16)
        d_probs = jnp.einsum("qhe,khe->hqk", dctx_blk, all_values, preferred_element_type=f32)
        d_scores = (probs.astype(f32) * (d_probs - jnp.transpose(delta_blk)[..., None])).astype(
            bf16
        )
        d_query_blk = (
            jnp.einsum("hqk,khe->qhe", d_scores, all_keys, preferred_element_type=f32) * scale
        )
        return (probs, d_scores, d_query_blk)

    probs_all, dscores_all, d_queries = lax.map(
        backward_block,
        (
            query_blocks,
            index_blocks,
            seg_blocks,
            dctx_blocks,
            delta.reshape(count_blocks, block, heads_here),
            lse_all,
        ),
    )
    d_queries = d_queries.reshape(count_rows, heads_here, HD)
    key_part = (
        jnp.einsum("bhqk,bqhe->khe", dscores_all, query_blocks, preferred_element_type=f32) * scale
    )
    value_part = jnp.einsum("bhqk,bqhe->khe", probs_all, dctx_blocks, preferred_element_type=f32)
    key_value = lax.psum_scatter(
        jnp.concatenate(
            [
                key_part.reshape(count_rows * lax.axis_size("ctx"), local_width),
                value_part.reshape(count_rows * lax.axis_size("ctx"), local_width),
            ],
            axis=1,
        ),
        "ctx",
        scatter_dimension=0,
        tiled=True,
    )
    d_keys = key_value[:, :local_width].reshape(count_rows, heads_here, HD)
    d_values = key_value[:, local_width:]
    d_joint = jnp.stack(
        [
            unrotate(d_queries, cosine, sine).reshape(count_rows, local_width),
            unrotate(d_keys, cosine, sine).reshape(count_rows, local_width),
            d_values,
        ],
        axis=1,
    )
    d_joint_b = d_joint.astype(bf16)
    grad_joint_w = jnp.einsum("nd,npe->dpe", first, d_joint_b, preferred_element_type=f32)
    grad_joint_b = jnp.sum(d_joint, 0)
    d_first_part = jnp.einsum("npe,dpe->nd", d_joint_b, back_joint, preferred_element_type=f32)
    d_first, d_second = lax.psum((d_first_part, d_second_part), "tp")
    norm_stats = jnp.stack(
        [
            jnp.sum(d_first * normed, 0),
            jnp.sum(d_first, 0),
            jnp.sum(d_second * normed, 0),
            jnp.sum(d_second, 0),
        ]
    )
    tokens_grad = (
        cot
        + norm_back(d_first, normed, rstd, gain_one)
        + norm_back(d_second, normed, rstd, gain_two)
    )
    grad_small = jnp.concatenate([norm_stats, bias_sum[None], bias_sum[None]], axis=0)
    share_joint, share_output, share_up, share_down, share_small, share_jbias, share_upbias = (
        lax.psum_scatter(grad_joint_w, ("fsdp", "ctx"), scatter_dimension=0, tiled=True),
        lax.psum_scatter(grad_output_w, ("fsdp", "ctx"), scatter_dimension=1, tiled=True),
        lax.psum_scatter(grad_up_w, ("fsdp", "ctx"), scatter_dimension=0, tiled=True),
        lax.psum_scatter(grad_down_w, ("fsdp", "ctx"), scatter_dimension=1, tiled=True),
        lax.psum_scatter(grad_small, ("fsdp", "ctx"), scatter_dimension=1, tiled=True),
        lax.psum_scatter(grad_joint_b, ("fsdp", "ctx"), scatter_dimension=1, tiled=True),
        lax.psum_scatter(grad_up_b, ("fsdp", "ctx"), scatter_dimension=0, tiled=True),
    )
    owned = (
        lax.all_gather(share_joint, "ctx", axis=0, tiled=True),
        lax.all_gather(share_output, "ctx", axis=1, tiled=True),
        lax.all_gather(share_up, "ctx", axis=0, tiled=True),
        lax.all_gather(share_down, "ctx", axis=1, tiled=True),
        lax.all_gather(share_small, "ctx", axis=1, tiled=True),
        lax.all_gather(share_jbias, "ctx", axis=1, tiled=True),
        lax.all_gather(share_upbias, "ctx", axis=0, tiled=True),
    )
    owned_joint, owned_output, owned_up, owned_down, owned_small, owned_jbias, owned_upbias = owned
    return (
        result[None],
        tokens_grad[None],
        owned_small[0],
        owned_small[1],
        owned_small[2],
        owned_small[3],
        owned_joint,
        owned_jbias,
        owned_output,
        owned_small[4],
        owned_up,
        owned_upbias,
        owned_down,
        owned_small[5],
    )


def solution(mesh):
    placed = (
        P("fsdp", "ctx", None),
        P("fsdp", "ctx"),
        P("fsdp", "ctx"),
        P("fsdp"),
        P("fsdp"),
        P("fsdp"),
        P("fsdp"),
        P("fsdp", None, "tp"),
        P(None, ("tp", "fsdp")),
        P("tp", "fsdp"),
        P("fsdp"),
        P("fsdp", "tp"),
        P(("tp", "fsdp")),
        P("tp", "fsdp"),
        P("fsdp"),
        P("fsdp", "ctx", None),
    )
    return jax.shard_map(
        local,
        mesh=mesh,
        in_specs=placed,
        out_specs=(
            P("fsdp", "ctx", None),
            P("fsdp", "ctx", None),
            P("fsdp"),
            P("fsdp"),
            P("fsdp"),
            P("fsdp"),
            P("fsdp", None, "tp"),
            P(None, ("tp", "fsdp")),
            P("tp", "fsdp"),
            P("fsdp"),
            P("fsdp", "tp"),
            P(("tp", "fsdp")),
            P("tp", "fsdp"),
            P("fsdp"),
        ),
        check_vma=False,
    )
```

profile of v0, /device:TPU:8, one launch (start us, length us, event | category | flops | bytes accessed | tf_op | source)
XLA Modules:
  0.0 1350.0 jit_solution(17469226401049093940)
XLA Ops:
  12.7 8.1 all_gather.57
  20.8 8.3 all_gather.55
  29.8 25.9 %all-gather.15.cloned.1.call-done = bf16[1024,3,512]{0,2,1:T(8,128)(2,1)} async-done(((bf16[256,3,512]{0,2,1:T(8,128)(2,1)}), bf16[1024,3,512]{0,2,1:T(8,128)(2,1)}) %all-gather.15.cloned.1.call-update) | async-done | bytes 3145744 | tf_op jit(solution)/shard_map/all_gather | solution.py:99
  65.9 11.9 all-gather
  87.9 42.5 %all-gather.19.cloned.1.call-done = bf16[2048,8,64]{0,2,1:T(8,128)(2,1)} async-done(((bf16[512,8,64]{0,2,1:T(8,128)(2,1)}), bf16[2048,8,64]{0,2,1:T(8,128)(2,1)}) %all-gather.19.cloned.1.call-update) | async-done | bytes 2097168 | tf_op jit(solution)/shard_map/all_gather | solution.py:129
  130.5 16.1 %fusion = (f32[8,512]{1,0:T(8,128)S(1)}, f32[8,512,2048]{2,1,0:T(8,128)}) fusion(pred[512,2048]{1,0:T(8,128)(4,1)S(1)} %fusion.7, bf16[2048,8,64]{0,2,1:T(8,128)(2,1)} %all-gather.19.cloned.1.call-done, bf16[512,8,48]{0,2,1:T(8,128)(2,1)S(1)} %slice.170, bf16[512,8,8]{0,2,1:T(8,128)(2,1)} %get-tuple-element.148, bf16[512,8,8]{0,2,1:T(8,128)(2,1)} %get-tuple-element.147), kind=kOutput, calls=%fused_computation.4 | convolution fusion | flops 1100476416 | bytes 37240832 | tf_op jit(solution)/shard_map/while/body/eval_jaxpr/qhe,khe->hqk/dot_general | solution.py:57
  146.6 15.8 %exponential_reduce_fusion = f32[8,512]{1,0:T(8,128)S(1)} fusion(f32[8,512,2048]{2,1,0:T(8,128)} %get-tuple-element.176, f32[8,512]{1,0:T(8,128)S(1)} %get-tuple-element.175, pred[512,2048]{1,0:T(8,128)(4,1)S(1)} %fusion.7), kind=kLoop, calls=%fused_computation.2 | loop fusion | flops 33550336 | bytes 34635776 | tf_op jit(solution)/shard_map/while/body/eval_jaxpr/reduce_sum | solution.py:146
  167.0 9.4 exponential_convert_fusion
  177.1 12.4 multiply_reduce_fusion.2
  189.6 25.3 %multiply_convert_fusion = bf16[8,512,2048]{2,1,0:T(8,128)(2,1)} fusion(bf16[8,512,2048]{2,1,0:T(8,128)(2,1)} %exponential_convert_fusion, bf16[512,8,64]{0,2,1:T(8,128)(2,1)S(1)} %bitcast.212, bf16[2048,8,64]{0,2,1:T(8,128)(2,1)} %all-gather.17.cloned.1.call-done, f32[8,512]{1,0:T(8,128)S(1)} %bitcast.227), kind=kOutput, calls=%fused_computation | convolution fusion | flops 1107296256 | bytes 36192256 | tf_op jit(solution)/shard_map/while/body/eval_jaxpr/qhe,khe->hqk/dot_general | solution.py:191
  214.9 10.9 convolution_multiply_fusion
  231.1 10.9 fusion.82
  247.4 8.2 pad_maximum_fusion
  256.3 8.0 all-gather.1
  264.4 15.2 %multiply_convert_fusion.1 = (bf16[512,2048]{1,0:T(8,128)(2,1)}, f32[512,2048]{1,0:T(8,128)}, f32[512,2048]{1,0:T(8,128)}) fusion(f32[2048]{0:T(1024)S(1)} %bitcast.253, bf16[1024,2048]{1,0:T(8,128)(2,1)} %all-gather.23.cloned.1.call-done, bf16[1,512,1024]{2,1,0:T(8,128)(2,1)S(1)} %copy-done.3, f32[1024]{0:T(1024)S(1)} %bitcast.257, f32[1024]{0:T(1024)S(1)} %bitcast.234, ...), kind=kOutput, calls=%fused_computation.9 | convolution fusion | flops 2219835392 | bytes 15749120 | tf_op jit(solution)/shard_map/dot_general | solution.py:154
  319.0 12.7 fusion.41
  338.0 94.8 %reduce-scatter.12.cloned.1.call-done = f32[512,1024]{1,0:T(8,128)} async-done(((f32[2048,1024]{1,0:T(8,128)}), f32[512,1024]{1,0:T(8,128)}) %reduce-scatter.12.cloned.1.call-update) | async-done | bytes 2097168 | tf_op jit(solution)/shard_map/reduce_scatter | solution.py:216
  468.1 145.7 %reduce-scatter.18.cloned.1.call-done = f32[64,2048]{1,0:T(8,128)} async-done(((f32[1024,2048]{1,0:T(8,128)}), f32[64,2048]{1,0:T(8,128)}) %reduce-scatter.18.cloned.1.call-update) | async-done | bytes 524304 | tf_op jit(solution)/shard_map/reduce_scatter | solution.py:260
  613.9 182.1 %reduce-scatter.20.cloned.1.call-done = f32[2048,64]{0,1:T(8,128)} async-done(((f32[2048,1024]{0,1:T(8,128)}), f32[2048,64]{0,1:T(8,128)}) %reduce-scatter.20.cloned.1.call-update) | async-done | bytes 524304 | tf_op jit(solution)/shard_map/reduce_scatter | solution.py:261
  796.1 38.2 %all-reduce.4.cloned.1.call-done = (f32[512,1024]{1,0:T(8,128)}, f32[512,1024]{1,0:T(8,128)}, f32[512,1024]{1,0:T(8,128)}) async-done(((f32[512,1024]{1,0:T(8,128)}, f32[512,1024]{1,0:T(8,128)}, f32[512,1024]{1,0:T(8,128)}), (f32[512,1024]{1,0:T(8,128)}, f32[512,1024]{1,0:T(8,128)}, f32[512,1024]{1,0:T(8,128)})) %all-reduce.4.cloned.1.call-update) | async-done | bytes 6291472 | tf_op jit(solution)/shard_map/psum | solution.py:159
  839.0 134.1 %reduce-scatter.14.cloned.1.call-done = f32[64,3,512]{2,0,1:T(8,128)} async-done(((f32[1024,3,512]{2,0,1:T(8,128)}), f32[64,3,512]{2,0,1:T(8,128)}) %reduce-scatter.14.cloned.1.call-update) | async-done | bytes 393232 | tf_op jit(solution)/shard_map/reduce_scatter | solution.py:258
  974.3 41.2 %all-reduce = f32[2048]{0:T(1024)S(1)} all-reduce(f32[2048]{0:T(1024)S(1)} %get-tuple-element.179), channel_id=9, replica_groups=mesh['fsdp'=4,'ctx'=4,'tp'=2] {'fsdp','ctx'}, use_global_device_ids=true, to_apply=%region_25.26.clone | all-reduce | flops 2048 | bytes 16384
  1015.6 9.2 all-gather.4
  1024.9 31.5 %reduce-scatter.16.cloned.1.call-done = f32[512,64]{0,1:T(8,128)} async-done(((f32[512,1024]{0,1:T(8,128)}), f32[512,64]{0,1:T(8,128)}) %reduce-scatter.16.cloned.1.call-update) | async-done | bytes 131088 | tf_op jit(solution)/shard_map/reduce_scatter | solution.py:259
  1056.4 18.7 %all_gather.68 = f32[512,256]{0,1:T(8,128)} all-gather(f32[512,64]{0,1:T(8,128)} %reduce-scatter.16.cloned.1.call-done), channel_id=1, replica_groups=mesh['fsdp'=4,'ctx'=4,'tp'=2] {'ctx'}, dimensions={1}, use_global_device_ids=true | all-gather | bytes 655360 | tf_op jit(solution)/shard_map/all_gather | solution.py:268
  1077.2 54.6 %reduce-scatter.24.cloned.1.call-done = f32[32,3]{1,0:T(8,128)} async-done(((f32[512,3]{1,0:T(8,128)}), f32[32,3]{1,0:T(8,128)}) %reduce-scatter.24.cloned.1.call-update) | async-done | bytes 400
  1132.6 14.2 %all-gather.3 = f32[4,32,3]{1,2,0:T(4,128)S(1)} all-gather(f32[1,32,3]{1,2,0:T(4,128)S(1)} %bitcast.250), channel_id=1, replica_groups=mesh['fsdp'=4,'ctx'=4,'tp'=2] {'ctx'}, dimensions={0}, use_global_device_ids=true | all-gather | bytes 1920 | tf_op jit(solution)/shard_map/all_gather | solution.py:272
  1147.4 31.1 %all-gather.29.cloned.1.call-done = f32[256,2048]{1,0:T(8,128)} async-done(((f32[64,2048]{1,0:T(8,128)}), f32[256,2048]{1,0:T(8,128)}) %all-gather.29.cloned.1.call-update) | async-done | bytes 2097168 | tf_op jit(solution)/shard_map/all_gather | solution.py:269
  1178.6 46.1 %all-gather.31.cloned.1.call-done = f32[2048,256]{0,1:T(8,128)} async-done(((f32[2048,64]{0,1:T(8,128)}), f32[2048,256]{0,1:T(8,128)}) %all-gather.31.cloned.1.call-update) | async-done | bytes 2097168 | tf_op jit(solution)/shard_map/all_gather | solution.py:270
  1232.4 67.6 %reduce-scatter.22.cloned.1.call-done = f32[64,6]{1,0:T(8,128)} async-done(((f32[1024,6]{1,0:T(8,128)}), f32[64,6]{1,0:T(8,128)}) %reduce-scatter.22.cloned.1.call-update) | async-done | bytes 1552
  1300.9 14.5 %all-gather.2 = f32[4,64,6]{1,2,0:T(8,128)S(1)} all-gather(f32[1,64,6]{1,2,0:T(8,128)S(1)} %bitcast.243), channel_id=1, replica_groups=mesh['fsdp'=4,'ctx'=4,'tp'=2] {'ctx'}, dimensions={0}, use_global_device_ids=true | all-gather | bytes 7680 | tf_op jit(solution)/shard_map/all_gather | solution.py:271
  1316.0 22.7 %all-gather.27.cloned.1.call-done = f32[256,3,512]{2,0,1:T(8,128)} async-done(((f32[64,3,512]{2,0,1:T(8,128)}), f32[256,3,512]{2,0,1:T(8,128)}) %all-gather.27.cloned.1.call-update) | async-done | bytes 1572880 | tf_op jit(solution)/shard_map/all_gather | solution.py:267
  (182 shorter events, 146.8 us)
Async XLA Ops:
  7.3 48.4 %all-gather.15.cloned.1.call-start = ((), (), s32[]{:S(2)}) async-start(), calls=%async_computation.7 | async-start | bytes 3932160 | tf_op jit(solution)/shard_map/all_gather | solution.py:99
  9.7 74.3 %all-gather.21.cloned.1.call-start = ((), (), s32[]{:S(2)}) async-start(), calls=%async_computation.10 | async-start | bytes 1310720 | tf_op jit(solution)/shard_map/all_gather | solution.py:100
  10.5 120.0 %all-gather.19.cloned.1.call-start = ((), (), s32[]{:S(2)}) async-start(), calls=%async_computation.9 | async-start | bytes 2621440 | tf_op jit(solution)/shard_map/all_gather | solution.py:129
  12.5 47.3 %copy-start.10 = (f32[512,8]{0,1:T(8,128)}, f32[512,8]{0,1:T(8,128)S(1)}, u32[]{:S(2)}) copy-start(f32[512,8]{0,1:T(8,128)S(1)} %get-tuple-element.171) | copy-start | bytes 49156
  12.6 47.3 %copy-start.12 = (f32[512,8]{0,1:T(8,128)}, f32[512,8]{0,1:T(8,128)S(1)}, u32[]{:S(2)}) copy-start(f32[512,8]{0,1:T(8,128)S(1)} %get-tuple-element.172) | copy-start | bytes 49156
  29.8 29.8 %copy-start.14 = (f32[1,1024]{1,0:T(1,128)}, f32[1,1024]{1,0:T(1,128)S(1)}, u32[]{:S(2)}) copy-start(f32[1,1024]{1,0:T(1,128)S(1)} %get-tuple-element.161) | copy-start | bytes 12292
  29.8 29.8 %copy-start.18 = (f32[1,1024]{1,0:T(1,128)}, f32[1,1024]{1,0:T(1,128)S(1)}, u32[]{:S(2)}) copy-start(f32[1,1024]{1,0:T(1,128)S(1)} %get-tuple-element.162) | copy-start | bytes 12292
  59.8 24.2 %copy-start.1 = (f32[1,512,1024]{2,1,0:T(8,128)S(1)}, f32[1,512,1024]{2,1,0:T(8,128)}, u32[]{:S(2)}) copy-start(f32[1,512,1024]{2,1,0:T(8,128)} %param.31) | copy-start | bytes 6291460
  62.5 114.6 %all-gather.17.cloned.1.call-start = ((), (), s32[]{:S(2)}) async-start(), calls=%async_computation.8 | async-start | bytes 2621440 | tf_op jit(solution)/shard_map/all_gather | solution.py:130
  64.7 199.7 %all-gather.23.cloned.1.call-start = ((), (), s32[]{:S(2)}) async-start(), calls=%async_computation.11 | async-start | bytes 5242880 | tf_op jit(solution)/shard_map/all_gather | solution.py:101
  65.3 221.0 %all-gather.25.cloned.1.call-start = ((), (), s32[]{:S(2)}) async-start(), calls=%async_computation.12 | async-start | bytes 5242880 | tf_op jit(solution)/shard_map/all_gather | solution.py:102
  65.8 366.9 %reduce-scatter.12.cloned.1.call-start = ((), (), s32[]{:S(2)}) async-start(), calls=%async_computation.13 | async-start | bytes 10485760 | tf_op jit(solution)/shard_map/reduce_scatter | solution.py:216
  146.6 20.5 %copy-start = (f32[8,512,2048]{2,1,0:T(8,128)S(1)}, f32[8,512,2048]{2,1,0:T(8,128)}, u32[]{:S(2)}) copy-start(f32[8,512,2048]{2,1,0:T(8,128)} %get-tuple-element.176) | copy-start | bytes 100663296
  176.4 13.2 copy-start.4
  189.5 25.3 %copy-start.8 = (bf16[512,8,8]{0,2,1:T(8,128)(2,1)S(1)}, bf16[512,8,8]{0,2,1:T(8,128)(2,1)}, u32[]{:S(2)}) copy-start(bf16[512,8,8]{0,2,1:T(8,128)(2,1)} %get-tuple-element.147) | copy-start | bytes 196612
  189.6 25.3 %copy-start.9 = (bf16[512,8,8]{0,2,1:T(8,128)(2,1)S(1)}, bf16[512,8,8]{0,2,1:T(8,128)(2,1)}, u32[]{:S(2)}) copy-start(bf16[512,8,8]{0,2,1:T(8,128)(2,1)} %get-tuple-element.148) | copy-start | bytes 196612
  255.7 358.1 %reduce-scatter.18.cloned.1.call-start = ((), (), s32[]{:S(2)}) async-start(), calls=%async_computation.17 | async-start | bytes 8912896 | tf_op jit(solution)/shard_map/reduce_scatter | solution.py:260
  300.9 495.0 %reduce-scatter.20.cloned.1.call-start = ((), (), s32[]{:S(2)}) async-start(), calls=%async_computation.19 | async-start | bytes 8912896 | tf_op jit(solution)/shard_map/reduce_scatter | solution.py:261
  308.2 526.2 %all-reduce.4.cloned.1.call-start = ((), (), s32[]{:S(2)}) async-start(), calls=%async_computation.23 | async-start | bytes 12582912 | tf_op jit(solution)/shard_map/psum | solution.py:159
  338.0 101.6 %copy-start.11 = (f32[512,8]{0,1:T(8,128)S(1)}, f32[512,8]{0,1:T(8,128)}, u32[]{:S(2)}) copy-start(f32[512,8]{0,1:T(8,128)} %copy-done.10) | copy-start | bytes 49156
  338.0 101.6 %copy-start.13 = (f32[512,8]{0,1:T(8,128)S(1)}, f32[512,8]{0,1:T(8,128)}, u32[]{:S(2)}) copy-start(f32[512,8]{0,1:T(8,128)} %copy-done.12) | copy-start | bytes 49156
  454.6 518.5 %reduce-scatter.14.cloned.1.call-start = ((), (), s32[]{:S(2)}) async-start(), calls=%async_computation.14 | async-start | bytes 6684672 | tf_op jit(solution)/shard_map/reduce_scatter | solution.py:258
  461.8 594.6 %reduce-scatter.16.cloned.1.call-start = ((), (), s32[]{:S(2)}) async-start(), calls=%async_computation.16 | async-start | bytes 2228224 | tf_op jit(solution)/shard_map/reduce_scatter | solution.py:259
  465.0 666.8 %reduce-scatter.24.cloned.1.call-start = ((), (), s32[]{:S(2)}) async-start(), calls=%async_computation.22 | async-start | bytes 278528
  468.0 710.5 %all-gather.29.cloned.1.call-start = ((), (), s32[]{:S(2)}) async-start(), calls=%async_computation.18 | async-start | bytes 2621440 | tf_op jit(solution)/shard_map/all_gather | solution.py:269
  613.8 610.9 %all-gather.31.cloned.1.call-start = ((), (), s32[]{:S(2)}) async-start(), calls=%async_computation.20 | async-start | bytes 2621440 | tf_op jit(solution)/shard_map/all_gather | solution.py:270
  795.9 177.1 %copy-start.31 = (u32[32]{0:T(128)S(1)}, u32[32]{0:T(128)}, u32[]{:S(2)}) copy-start(u32[32]{0:T(128)} %constant.141) | copy-start | bytes 388
  795.9 504.1 %reduce-scatter.22.cloned.1.call-start = ((), (), s32[]{:S(2)}) async-start(), calls=%async_computation.21 | async-start | bytes 557056
  837.8 389.8 %copy-start.16 = (f32[1,1024]{1,0:T(1,128)S(1)}, f32[1,1024]{1,0:T(1,128)}, u32[]{:S(2)}) copy-start(f32[1,1024]{1,0:T(1,128)} %get-tuple-element.159) | copy-start | bytes 12292
  837.8 389.8 %copy-start.17 = (f32[1,1024]{1,0:T(1,128)S(1)}, f32[1,1024]{1,0:T(1,128)}, u32[]{:S(2)}) copy-start(f32[1,1024]{1,0:T(1,128)} %get-tuple-element.160) | copy-start | bytes 12292
  838.9 499.8 %all-gather.27.cloned.1.call-start = ((), (), s32[]{:S(2)}) async-start(), calls=%async_computation.15 | async-start | bytes 1966080 | tf_op jit(solution)/shard_map/all_gather | solution.py:267
  1232.4 109.0 %copy-start.7 = (f32[256,2048]{1,0:T(8,128)S(1)}, f32[256,2048]{1,0:T(8,128)}, u32[]{:S(2)}) copy-start(f32[256,2048]{1,0:T(8,128)} %all-gather.29.cloned.1.call-done) | copy-start | bytes 6291460
  (19 other events, 82.7 us)
Sparse Core Ops, SparseCore 0:
  10.5 45.0 all-gather.14
  57.4 26.4 all-gather.20
  86.1 44.2 all-gather.18
  132.5 44.6 all-gather.16
  178.8 53.0 all-gather.22
  233.6 52.5 all-gather.24
  288.6 144.1 reduce-scatter.11
  435.1 178.6 reduce-scatter.17
  616.1 179.7 reduce-scatter.19
  799.6 34.6 all-reduce.3
  836.8 136.2 reduce-scatter.13
  975.8 80.4 reduce-scatter.15
  1058.7 73.0 reduce-scatter.23
  1133.2 45.3 all-gather.28
  1180.0 44.6 all-gather.30
  1227.3 72.7 reduce-scatter.21
  1301.6 37.1 all-gather.26
where the time goes:
time: 1360 us; the launch traced here: 1350 us
  waiting for transfers between devices  931 us (68%)
  matrix products  161 us (12%)
  blocking collectives  134 us (10%)
  local copies, waits for them, and re-layouts  54.6 us (4%)
  other arithmetic  52.5 us (4%)
  between operations  15.4 us (1%)
    reduce_scatter x1, waiting for transfers between devices, local(): lax.psum_scatter(grad_down_w, ('fsdp', 'ctx'), scatter_dimension=1, tiled...  182 us
    reduce_scatter x1, waiting for transfers between devices, local(): lax.psum_scatter(grad_up_w, ('fsdp', 'ctx'), scatter_dimension=0, tiled=T...  146 us
    reduce_scatter x1, waiting for transfers between devices, local(): lax.psum_scatter(grad_joint_w, ('fsdp', 'ctx'), scatter_dimension=0, tile...  134 us
    unnamed x19, waiting for transfers between devices  124 us
    reduce_scatter x1, waiting for transfers between devices, local(): lax.psum_scatter(jnp.concatenate([key_part.reshape(count_rows * lax.axis_...  94.8 us
    all_gather x1, waiting for transfers between devices, local(): lax.all_gather(share_down, 'ctx', axis=1, tiled=True)  46.1 us
    all_gather x1, waiting for transfers between devices, local(): lax.all_gather(keys_here, 'ctx', axis=0, tiled=True)  42.5 us
    unnamed x1, blocking collectives  41.2 us
  transfers between devices with their start and end apart: 17, of which 16 were waited for; matrix products, arithmetic and copies ran while one was open for 19% of the time, Pallas kernels for 0%

commit v1 on v0

--- a/solution.py
+++ b/solution.py
@@ -1,6 +1,8 @@
 import jax
 import jax.numpy as jnp
 from jax import lax
+from jax.experimental import pallas as pl
+from jax.experimental.pallas import tpu as pltpu
 from jax.sharding import PartitionSpec as P
 
 HD = 64
@@ -64,7 +66,7 @@
     return jnp.where(allowed[None], scores, -jnp.inf)
 
 
-def local(
+def gathered_local(
     tokens,
     segment_ids,
     positions,
@@ -291,6 +293,494 @@
     )
 
 
+NEG = -1e30
+
+
+def attention_body(
+    heads, q_ref, k_ref, v_ref, dc_ref, qseg_ref, kseg_ref, ctx_ref, dq_ref, dkv_ref,
+    kt_ref, vt_ref, s_ref, e_ref, dk_acc, dv_acc,
+):
+    f32 = jnp.float32
+    bf16 = jnp.bfloat16
+    step = pl.program_id(0)
+    rows, width = q_ref.shape
+    chunks, _, chunk = kt_ref.shape
+    hd = width // heads
+
+    @pl.when(step == 0)
+    def _():
+        for c in range(chunks):
+            part = pl.ds(c * chunk, chunk)
+            kt_ref[c] = k_ref[part, :].astype(f32).T.astype(bf16)
+            vt_ref[c] = v_ref[part, :].astype(f32).T.astype(bf16)
+        dk_acc[...] = jnp.zeros_like(dk_acc)
+        dv_acc[...] = jnp.zeros_like(dv_acc)
+
+    used = ((step + 1) * rows + chunk - 1) // chunk
+    q = q_ref[...]
+    q_t = q.astype(f32).T
+    dc_t = dc_ref[...].astype(f32).T
+    row_head = lax.broadcasted_iota(jnp.int32, (width, rows), 0) // hd
+    lane_head = lax.broadcasted_iota(jnp.int32, (rows, width), 1) // hd
+    q_heads_t = [jnp.where(row_head == h, q_t, 0.0).astype(bf16) for h in range(heads)]
+    q_heads = [jnp.where(lane_head == h, q, jnp.zeros_like(q)) for h in range(heads)]
+    qseg = qseg_ref[...]
+    query = step * rows + lax.broadcasted_iota(jnp.int32, (1, rows), 1)
+    key_base = lax.broadcasted_iota(jnp.int32, (chunk, 1), 0)
+
+    def score(j, tops):
+        part = pl.ds(pl.multiple_of(j * chunk, chunk), chunk)
+        keys = k_ref[part, :]
+        allowed = (kseg_ref[part, :] == qseg) & (key_base + j * chunk <= query)
+        out = []
+        for h in range(heads):
+            s = jnp.dot(keys, q_heads_t[h], preferred_element_type=f32)
+            s = jnp.where(allowed, s, NEG)
+            s_ref[h, part, :] = s
+            out.append(jnp.maximum(tops[h], jnp.max(s, 0, keepdims=True)))
+        return tuple(out)
+
+    tops = lax.fori_loop(
+        0, used, score, tuple(jnp.full((1, rows), NEG, f32) for _ in range(heads))
+    )
+
+    def mix(j, carry):
+        part = pl.ds(pl.multiple_of(j * chunk, chunk), chunk)
+        values_t = vt_ref[j]
+        out = []
+        for h in range(heads):
+            total, acc = carry[h]
+            e = jnp.exp(s_ref[h, part, :] - tops[h])
+            total = total + jnp.sum(e, 0, keepdims=True)
+            e = e.astype(bf16)
+            e_ref[h, part, :] = e
+            acc = acc + jnp.dot(
+                values_t[h * hd : (h + 1) * hd, :], e, preferred_element_type=f32
+            )
+            out.append((total, acc))
+        return tuple(out)
+
+    mixed = lax.fori_loop(
+        0,
+        used,
+        mix,
+        tuple((jnp.zeros((1, rows), f32), jnp.zeros((hd, rows), f32)) for _ in range(heads)),
+    )
+    ctx_parts, dcn_parts, deltas = [], [], []
+    for h in range(heads):
+        total, acc = mixed[h]
+        inv = 1.0 / total
+        ctx_h = acc * inv
+        dc_h = dc_t[h * hd : (h + 1) * hd, :]
+        deltas.append(jnp.sum(ctx_h * dc_h, 0, keepdims=True) * inv)
+        ctx_parts.append(ctx_h)
+        dcn_parts.append(dc_h * inv)
+    ctx_ref[...] = jnp.concatenate(ctx_parts, 0).T.astype(bf16)
+    dcn_t = jnp.concatenate(dcn_parts, 0)
+    dcn = dcn_t.T
+    dcn_heads_t = [jnp.where(row_head == h, dcn_t, 0.0).astype(bf16) for h in range(heads)]
+    dcn_heads = [jnp.where(lane_head == h, dcn, 0.0).astype(bf16) for h in range(heads)]
+
+    def back(j, carry):
+        part = pl.ds(pl.multiple_of(j * chunk, chunk), chunk)
+        values = v_ref[part, :]
+        keys_t = kt_ref[j]
+        dk = dk_acc[part, :]
+        dv = dv_acc[part, :]
+        out = []
+        for h in range(heads):
+            e = e_ref[h, part, :]
+            dp = jnp.dot(values, dcn_heads_t[h], preferred_element_type=f32)
+            ds = (e.astype(f32) * (dp - deltas[h])).astype(bf16)
+            out.append(
+                carry[h]
+                + jnp.dot(keys_t[h * hd : (h + 1) * hd, :], ds, preferred_element_type=f32)
+            )
+            dk = dk + jnp.dot(ds, q_heads[h], preferred_element_type=f32)
+            dv = dv + jnp.dot(e, dcn_heads[h], preferred_element_type=f32)
+        dk_acc[part, :] = dk
+        dv_acc[part, :] = dv
+        return tuple(out)
+
+    dq = lax.fori_loop(
+        0, used, back, tuple(jnp.zeros((hd, rows), f32) for _ in range(heads))
+    )
+    dq_ref[...] = (jnp.concatenate(dq, 0).T * HD ** (-0.5)).astype(bf16)
+
+    @pl.when(step == pl.num_programs(0) - 1)
+    def _():
+        dkv_ref[:, :width] = dk_acc[...].astype(bf16)
+        dkv_ref[:, width:] = dv_acc[...].astype(bf16)
+
+
+def attention(qkv, dctx, seg, block=256, chunk=256):
+    count, width = dctx.shape
+    heads = width // HD
+    bf16 = jnp.bfloat16
+    f32 = jnp.float32
+    pairs = count * (count + block) // 2 * heads
+    return pl.pallas_call(
+        lambda *refs: attention_body(heads, *refs),
+        grid=(count // block,),
+        in_specs=[
+            pl.BlockSpec((block, width), lambda i: (i, 0)),
+            pl.BlockSpec((count, width), lambda i: (0, 1)),
+            pl.BlockSpec((count, width), lambda i: (0, 2)),
+            pl.BlockSpec((block, width), lambda i: (i, 0)),
+            pl.BlockSpec((1, block), lambda i: (0, i)),
+            pl.BlockSpec((count, 1), lambda i: (0, 0)),
+        ],
+        out_specs=[
+            pl.BlockSpec((block, width), lambda i: (i, 0)),
+            pl.BlockSpec((block, width), lambda i: (i, 0)),
+            pl.BlockSpec((count, 2 * width), lambda i: (0, 0)),
+        ],
+        out_shape=[
+            jax.ShapeDtypeStruct((count, width), bf16),
+            jax.ShapeDtypeStruct((count, width), bf16),
+            jax.ShapeDtypeStruct((count, 2 * width), bf16),
+        ],
+        scratch_shapes=[
+            pltpu.VMEM((count // chunk, width, chunk), bf16),
+            pltpu.VMEM((count // chunk, width, chunk), bf16),
+            pltpu.VMEM((heads, count, block), f32),
+            pltpu.VMEM((heads, count, block), bf16),
+            pltpu.VMEM((count, width), f32),
+            pltpu.VMEM((count, width), f32),
+        ],
+        compiler_params=pltpu.CompilerParams(vmem_limit_bytes=40 * 1024 * 1024),
+        cost_estimate=pl.CostEstimate(
+            flops=10 * pairs * HD * 3, bytes_accessed=count * width * 16, transcendentals=pairs
+        ),
+        name="attention",
+    )(qkv, qkv, qkv, dctx, seg[None, :], seg[:, None])
+
+
+def partner(tensor, axis, flip):
+    size = lax.axis_size(axis)
+    return lax.ppermute(tensor, axis, [(s, s ^ flip) for s in range(size)])
+
+
+def pick(tensor, index, size, dim=0):
+    return lax.dynamic_slice_in_dim(tensor, index * size, size, dim)
+
+
+def put(buffer, block, index, dim=0):
+    return lax.dynamic_update_slice_in_dim(buffer, block, index * block.shape[dim], dim)
+
+
+def exchange(tensor, axis, dim_from, dim_to):
+    size = lax.axis_size(axis)
+    me = lax.axis_index(axis)
+    part = tensor.shape[dim_from] // size
+    shape = list(tensor.shape)
+    shape[dim_from] = part
+    shape[dim_to] *= size
+    out = jnp.zeros(shape, tensor.dtype)
+    for flip in range(size):
+        block = pick(tensor, me ^ flip, part, dim_from)
+        if flip:
+            block = partner(block, axis, flip)
+        out = put(out, block, me ^ flip, dim_to)
+    return out
+
+
+def plane_gather(block, axis="fsdp"):
+    return [block] + [partner(block, axis, flip) for flip in range(1, lax.axis_size(axis))]
+
+
+def chip_gather(rows):
+    core = lax.axis_index("tp")
+    half = rows.shape[0] // 2
+    mine = pick(rows, core, half)
+    out = [rows]
+    for block in plane_gather(mine)[1:]:
+        other = partner(block, "tp", 1)
+        out.append(jnp.where(core == 0, block, other))
+        out.append(jnp.where(core == 0, other, block))
+    return jnp.concatenate(out, 0)
+
+
+def chip_scatter(partial, count):
+    f32 = jnp.float32
+    bf16 = jnp.bfloat16
+    core = lax.axis_index("tp")
+    size = partial.shape[0] // count
+    halves = partial.reshape(size, 2, count // 2, partial.shape[1])
+    away = lax.dynamic_index_in_dim(halves, 1 - core, 1, keepdims=False).astype(bf16)
+    kept = lax.dynamic_index_in_dim(halves, core, 1, keepdims=False)
+    summed = kept + partner(away, "tp", 1).astype(f32)
+    sending = summed.astype(bf16)
+    total = summed[0]
+    for flip in range(1, size):
+        total = total + partner(sending[flip], "fsdp", flip).astype(f32)
+    other = partner(total, "tp", 1)
+    low = jnp.where(core == 0, total, other)
+    high = jnp.where(core == 0, other, total)
+    return jnp.concatenate([low, high], 0)
+
+
+def spread_sum(parts, axis):
+    size = lax.axis_size(axis)
+    me = lax.axis_index(axis)
+    total = lax.dynamic_index_in_dim(parts, me, 1, keepdims=False).astype(jnp.float32)
+    for flip in range(1, size):
+        block = lax.dynamic_index_in_dim(parts, me ^ flip, 1, keepdims=False)
+        total = total + partner(block, axis, flip).astype(jnp.float32)
+    return total
+
+
+def share_rows(grad):
+    size, depth = lax.axis_size("fsdp"), lax.axis_size("ctx")
+    rows, cols = grad.shape
+    part = rows // size // depth
+    quarter = spread_sum(grad.reshape(size, depth, part, cols), "ctx").astype(jnp.bfloat16)
+    me, place = lax.axis_index("fsdp"), lax.axis_index("ctx")
+    held = jnp.zeros((part, size, cols), jnp.bfloat16)
+    for flip in range(size):
+        block = lax.dynamic_index_in_dim(quarter, me ^ flip, 0, keepdims=False)
+        if flip:
+            block = partner(block, "fsdp", flip)
+        held = lax.dynamic_update_slice(held, block[:, None], (0, me ^ flip, 0))
+    out = jnp.zeros((depth, part, size, cols), jnp.float32)
+    for flip in range(depth):
+        block = partner(held, "ctx", flip) if flip else held
+        out = lax.dynamic_update_slice(
+            out, block.astype(jnp.float32)[None], (place ^ flip, 0, 0, 0)
+        )
+    return out.reshape(rows // size, size, cols)
+
+
+def share_cols(grad):
+    size, depth = lax.axis_size("fsdp"), lax.axis_size("ctx")
+    rows, cols = grad.shape
+    part = rows // depth
+    width = cols // size
+    quarter = spread_sum(grad.reshape(1, depth, part, cols), "ctx")[0].astype(jnp.bfloat16)
+    me, place = lax.axis_index("fsdp"), lax.axis_index("ctx")
+    held = jnp.zeros((size, part, width), jnp.bfloat16)
+    for flip in range(size):
+        block = pick(quarter, me ^ flip, width, 1)
+        if flip:
+            block = partner(block, "fsdp", flip)
+        held = lax.dynamic_update_slice(held, block[None], (me ^ flip, 0, 0))
+    out = jnp.zeros((size, depth, part, width), jnp.float32)
+    for flip in range(depth):
+        block = partner(held, "ctx", flip) if flip else held
+        out = lax.dynamic_update_slice(
+            out, block.astype(jnp.float32)[:, None], (0, place ^ flip, 0, 0)
+        )
+    return out.reshape(size * rows, width)
+
+
+def all_sum(vector, axis):
+    total = vector
+    for flip in range(1, lax.axis_size(axis)):
+        total = total + partner(vector, axis, flip)
+    return total
+
+
+def plane_local(
+    tokens,
+    segment_ids,
+    positions,
+    attention_gain,
+    attention_shift,
+    feedforward_gain,
+    feedforward_shift,
+    joint_weight,
+    joint_bias,
+    output_weight,
+    output_bias,
+    up_weight,
+    up_bias,
+    down_weight,
+    down_bias,
+    cotangent,
+):
+    f32 = jnp.float32
+    bf16 = jnp.bfloat16
+    me, place, core = lax.axis_index("fsdp"), lax.axis_index("ctx"), lax.axis_index("tp")
+    size = lax.axis_size("fsdp")
+    count, model = tokens.shape[1:]
+    rows = tokens[0].astype(f32)
+    cot = cotangent[0]
+
+    small = jnp.concatenate(
+        [
+            attention_gain,
+            attention_shift,
+            feedforward_gain,
+            feedforward_shift,
+            output_bias,
+            down_bias,
+        ]
+    ).reshape(6, -1)
+    full_small = jnp.zeros((6, model), bf16)
+    for flip, block in enumerate(plane_gather(small)):
+        full_small = put(full_small, block, me ^ flip, 1)
+    params = full_small.astype(f32)
+    ids = jnp.concatenate([segment_ids, positions], 0)
+    ids_plane = plane_gather(ids)
+    pos_plane = jnp.concatenate([block[1] for block in ids_plane])
+    seg_plane = jnp.concatenate([block[0] for block in ids_plane])
+
+    plane_tokens = chip_gather(tokens[0])
+    width = joint_weight.shape[2] // size
+    joint_w = exchange(joint_weight, "fsdp", 2, 0)
+    cot_b = chip_gather(cot.astype(bf16))
+    output_w = exchange(output_weight, "fsdp", 0, 1)
+    up_w = exchange(up_weight, "fsdp", 1, 0)
+    down_w = exchange(down_weight, "fsdp", 0, 1)
+
+    normed, _ = normalize(plane_tokens.astype(f32))
+    first = (normed * params[0] + params[1]).astype(bf16)
+    second = (normed * params[2] + params[3]).astype(bf16)
+
+    lane = jnp.arange(width, dtype=jnp.int32) % HD
+    half = ROT // 2
+    freq = jnp.where(
+        lane < ROT, ROPE_BASE ** (-((lane % half).astype(f32) * 2.0 / ROT)), 0.0
+    )
+    angle = pos_plane.astype(f32)[:, None] * freq[None, :]
+    cosine = jnp.cos(angle)
+    sine = jnp.sin(angle) * jnp.where(lane < half, -1.0, 1.0)[None, :]
+    source = jnp.arange(width, dtype=jnp.int32)
+    source = jnp.where(lane < half, source + half, jnp.where(lane < ROT, source - half, -1))
+    swap = (jnp.arange(width, dtype=jnp.int32)[:, None] == source[None, :]).astype(bf16)
+
+    joint_flat = joint_w.reshape(model, 3 * width)
+    bias = joint_bias.astype(f32)
+    joint = jnp.dot(first, joint_flat, preferred_element_type=f32) + bias.reshape(-1)[None]
+    swapped_w = jnp.einsum("dpe,ef->dpf", joint_w[:, :2], swap, preferred_element_type=bf16)
+    swapped_b = jnp.dot(joint_bias[:2], swap, preferred_element_type=f32)
+    swapped = (
+        jnp.dot(first, swapped_w.reshape(model, 2 * width), preferred_element_type=f32)
+        + swapped_b.reshape(-1)[None]
+    )
+    scale = HD ** (-0.5)
+    queries = (joint[:, :width] * cosine + swapped[:, :width] * sine) * scale
+    keys = joint[:, width : 2 * width] * cosine + swapped[:, width:] * sine
+    qkv = jnp.concatenate([queries, keys, joint[:, 2 * width :]], 1).astype(bf16)
+
+    def to_sequence(tensor):
+        out = jnp.zeros(tensor.shape, tensor.dtype)
+        for flip in range(size):
+            block = pick(tensor, me ^ place ^ flip, count)
+            if flip:
+                block = partner(block, "ctx", flip)
+            out = put(out, block, place ^ flip)
+        return out
+
+    def from_sequence(tensor):
+        out = jnp.zeros(tensor.shape, tensor.dtype)
+        for flip in range(size):
+            block = pick(tensor, place ^ flip, count)
+            if flip:
+                block = partner(block, "ctx", flip)
+            out = put(out, block, me ^ place ^ flip)
+        return out
+
+    seg_seq = to_sequence(seg_plane)
+    qkv_seq = to_sequence(qkv)
+    d_context = jnp.einsum("nd,wd->nw", cot_b, output_w, preferred_element_type=f32).astype(bf16)
+    dctx_seq = to_sequence(d_context)
+    ctx_seq, dq_seq, dkv_seq = attention(qkv_seq, dctx_seq, seg_seq)
+
+    upper = jnp.dot(second, up_w, preferred_element_type=f32) + up_bias.astype(f32)[None]
+    gelu, gelu_back = jax.vjp(lambda value: jax.nn.gelu(value, approximate=False), upper)
+    activated = gelu.astype(bf16)
+    d_act = jnp.einsum("nd,fd->nf", cot_b, down_w, preferred_element_type=f32)
+    d_upper = gelu_back(d_act)[0]
+    d_upper_b = d_upper.astype(bf16)
+    grad_up_b = jnp.sum(d_upper, 0)
+    grad_up_w = jnp.dot(second.T, d_upper_b, preferred_element_type=f32).astype(bf16)
+    grad_down_w = jnp.dot(activated.T, cot_b, preferred_element_type=f32).astype(bf16)
+    d_second = jnp.einsum("nf,df->nd", d_upper_b, up_w, preferred_element_type=f32)
+
+    context = from_sequence(ctx_seq)
+    mixed = jnp.dot(context, output_w, preferred_element_type=f32) + jnp.dot(
+        activated, down_w, preferred_element_type=f32
+    )
+    result = rows + chip_scatter(mixed, count) + params[4] + params[5]
+    grad_output_w = jnp.dot(context.T, cot_b, preferred_element_type=f32).astype(bf16)
+
+    dq = from_sequence(dq_seq)
+    dkv = from_sequence(dkv_seq)
+    dq_swapped = jnp.dot(dq, swap, preferred_element_type=f32)
+    dk_swapped = jnp.dot(dkv[:, :width], swap, preferred_element_type=f32)
+    d_joint = jnp.concatenate(
+        [
+            dq.astype(f32) * cosine - dq_swapped * sine,
+            dkv[:, :width].astype(f32) * cosine - dk_swapped * sine,
+            dkv[:, width:].astype(f32),
+        ],
+        1,
+    )
+    d_joint_b = d_joint.astype(bf16)
+    grad_joint_b = jnp.sum(d_joint, 0)
+    grad_joint_w = jnp.dot(first.T, d_joint_b, preferred_element_type=f32).astype(bf16)
+    d_first = jnp.einsum("ne,de->nd", d_joint_b, joint_flat, preferred_element_type=f32)
+    upstream = chip_scatter(d_first * params[0] + d_second * params[2], count)
+
+    normed_here, rstd = normalize(rows)
+    tokens_grad = cot + rstd * (
+        upstream
+        - jnp.mean(upstream, -1, keepdims=True)
+        - normed_here * jnp.mean(upstream * normed_here, -1, keepdims=True)
+    )
+    stats = jnp.stack(
+        [
+            jnp.sum(d_first * normed, 0),
+            jnp.sum(d_first, 0),
+            jnp.sum(d_second * normed, 0),
+            jnp.sum(d_second, 0),
+            jnp.sum(pick(cot, core, count // 2), 0),
+        ]
+    )
+    stats = spread_sum(stats.reshape(5, size, -1), "fsdp")
+    stats = all_sum(stats, "tp")
+    packed = jnp.concatenate([stats.reshape(-1), grad_joint_b, grad_up_b])
+    packed = all_sum(packed, "ctx")
+    owned = packed[: stats.size].reshape(stats.shape)
+    owned_jbias = packed[stats.size : stats.size + 3 * width].reshape(3, width)
+    owned_upbias = packed[stats.size + 3 * width :]
+
+    owned_up = share_rows(grad_up_w).reshape(up_weight.shape)
+    owned_down = share_cols(grad_down_w)
+    owned_output = share_cols(grad_output_w)
+    owned_joint = share_rows(grad_joint_w).reshape(model // size, size, 3, width)
+    owned_joint = owned_joint.transpose(0, 2, 1, 3).reshape(joint_weight.shape)
+    return (
+        result[None],
+        tokens_grad[None],
+        owned[0],
+        owned[1],
+        owned[2],
+        owned[3],
+        owned_joint,
+        owned_jbias,
+        owned_output,
+        owned[4],
+        owned_up,
+        owned_upbias,
+        owned_down,
+        owned[4],
+    )
+
+
+def splits_plane(mesh, tokens, joint_weight):
+    size, depth, cores = mesh.shape["fsdp"], mesh.shape["ctx"], mesh.shape["tp"]
+    width = joint_weight.shape[2] // (size * cores)
+    return (
+        size == depth == tokens.shape[0]
+        and size & (size - 1) == 0
+        and cores == 2
+        and width % 128 == 0
+        and tokens.shape[1] // depth % 256 == 0
+    )
+
+
 def solution(mesh):
     placed = (
         P("fsdp", "ctx", None),
@@ -310,25 +800,27 @@
         P("fsdp"),
         P("fsdp", "ctx", None),
     )
-    return jax.shard_map(
-        local,
-        mesh=mesh,
-        in_specs=placed,
-        out_specs=(
-            P("fsdp", "ctx", None),
-            P("fsdp", "ctx", None),
-            P("fsdp"),
-            P("fsdp"),
-            P("fsdp"),
-            P("fsdp"),
-            P("fsdp", None, "tp"),
-            P(None, ("tp", "fsdp")),
-            P("tp", "fsdp"),
-            P("fsdp"),
-            P("fsdp", "tp"),
-            P(("tp", "fsdp")),
-            P("tp", "fsdp"),
-            P("fsdp"),
-        ),
-        check_vma=False,
-    )
+    given = (
+        P("fsdp", "ctx", None),
+        P("fsdp", "ctx", None),
+        P("fsdp"),
+        P("fsdp"),
+        P("fsdp"),
+        P("fsdp"),
+        P("fsdp", None, "tp"),
+        P(None, ("tp", "fsdp")),
+        P("tp", "fsdp"),
+        P("fsdp"),
+        P("fsdp", "tp"),
+        P(("tp", "fsdp")),
+        P("tp", "fsdp"),
+        P("fsdp"),
+    )
+
+    def run(*args):
+        body = plane_local if splits_plane(mesh, args[0], args[7]) else gathered_local
+        return jax.shard_map(
+            body, mesh=mesh, in_specs=placed, out_specs=given, check_vma=False
+        )(*args)
+
+    return run

time: 1360 us -> 542 us (0.40)
  waiting for transfers between devices: 931 us -> 199 us
  blocking collectives: 134 us -> 0 us
  starting transfers between devices: 1.27 us -> 119 us
  matrix products: 161 us -> 60.4 us
  Pallas kernels: 0 us -> 45.2 us
    reduce_scatter x5 -> x0, waiting for transfers between devices: 588 us -> none  [the longest x1 182 us: local(): lax.psum_scatter(grad_down_w, ('fsdp', 'ctx'), scatter_dimension=1, tiled...]
    ppermute x0 -> x101, waiting for transfers between devices: none -> 199 us  [partner(): return lax.ppermute(tensor, axis, [(s, s ^ flip) for s in range(size)])]
    all_gather x9 -> x0, waiting for transfers between devices: 181 us -> none  [the longest x1 46.1 us: local(): lax.all_gather(share_down, 'ctx', axis=1, tiled=True)]
    unnamed x19 -> x0, waiting for transfers between devices: 124 us -> none
    ppermute x0 -> x101, starting transfers between devices: none -> 119 us  [partner(): return lax.ppermute(tensor, axis, [(s, s ^ flip) for s in range(size)])]
    dot_general x18 -> x17, matrix products: 161 us -> 60.4 us  [the longest x1 16.4 us: plane_local(): d_act = jnp.einsum('nd,fd->nf', cot_b, down_w, preferred_element_type=f32)]
    all_gather x8 -> x0, blocking collectives: 93 us -> none  [the longest x1 18.7 us: local(): lax.all_gather(share_output, 'ctx', axis=1, tiled=True)]
    pallas_call x0 -> x1, Pallas kernels: none -> 45.2 us  [attention(): pl.pallas_call(lambda *refs: attention_body(heads, *refs), grid=(count //...]
  transfers between devices with their start and end apart: 17 -> 101, of which waited for: 16 -> 39; matrix products, arithmetic and copies ran while one was open for 19% -> 25% of each run, Pallas kernels for 0% -> 8%
where the time goes in v1:
time: 542 us; the launch traced here: 537 us
  waiting for transfers between devices  199 us (37%)
  starting transfers between devices  119 us (22%)
  local copies, waits for them, and re-layouts  63.6 us (12%)
  matrix products  60.4 us (11%)
  other arithmetic  46.4 us (9%)
  Pallas kernels  45.2 us (8%)
    ppermute x101, waiting for transfers between devices, partner(): return lax.ppermute(tensor, axis, [(s, s ^ flip) for s in range(size)])  199 us
    ppermute x101, starting transfers between devices, partner(): return lax.ppermute(tensor, axis, [(s, s ^ flip) for s in range(size)])  119 us
    pallas_call x1, Pallas kernels, attention(): pl.pallas_call(lambda *refs: attention_body(heads, *refs), grid=(count //...  45.2 us
    dot_general x1, matrix products, plane_local(): d_act = jnp.einsum('nd,fd->nf', cot_b, down_w, preferred_element_type=f32)  16.4 us
    dynamic_update_slice x35, local copies, waits for them, and re-layouts, put(): lax.dynamic_update_slice_in_dim(buffer, block, index * block.shape[dim],...  16.3 us
    unnamed x114, local copies, waits for them, and re-layouts  13.4 us
  transfers between devices with their start and end apart: 101, of which 39 were waited for; matrix products, arithmetic and copies ran while one was open for 25% of the time, Pallas kernels for 8%

profile of v1, /device:TPU:8, one launch (start us, length us, event | category | flops | bytes accessed | tf_op | source)
XLA Modules:
  0.0 537.0 jit_solution(1166299207843288969)
XLA Ops:
  65.9 6.5 %collective-permute-done.10 = bf16[256,3,128]{2,0,1:T(8,128)(2,1)S(1)} collective-permute-done((bf16[256,3,128]{2,0,1:T(8,128)(2,1)S(1)}, bf16[256,3,128]{2,0,1:T(8,128)(2,1)S(1)}, u32[]{:S(2)}, u32[]{:S(2)}) %collective-permute-start.10) | collective-permute-done | bytes 196640 | tf_op jit(solution)/shard_map/ppermute | solution.py:461
  84.1 9.0 %collective-permute-done.39 = bf16[512,256]{1,0:T(8,128)(2,1)S(1)} collective-permute-done((bf16[512,256]{1,0:T(8,128)(2,1)}, bf16[512,256]{1,0:T(8,128)(2,1)S(1)}, u32[]{:S(2)}, u32[]{:S(2)}) %collective-permute-start.39) | collective-permute-done | bytes 262176 | tf_op jit(solution)/shard_map/ppermute | solution.py:461
  95.5 12.4 %collective-permute-done.40 = bf16[512,256]{1,0:T(8,128)(2,1)S(1)} collective-permute-done((bf16[512,256]{1,0:T(8,128)(2,1)}, bf16[512,256]{1,0:T(8,128)(2,1)S(1)}, u32[]{:S(2)}, u32[]{:S(2)}) %collective-permute-start.40) | collective-permute-done | bytes 262176 | tf_op jit(solution)/shard_map/ppermute | solution.py:461
  120.0 8.5 %collective-permute-done.20 = bf16[256,1024]{1,0:T(8,128)(2,1)S(1)} collective-permute-done((bf16[256,1024]{1,0:T(8,128)(2,1)}, bf16[256,1024]{1,0:T(8,128)(2,1)S(1)}, u32[]{:S(2)}, u32[]{:S(2)}) %collective-permute-start.20) | collective-permute-done | bytes 524320 | tf_op jit(solution)/shard_map/ppermute | solution.py:461
  136.9 4.4 fusion.105
  141.7 16.4 %fusion.95 = (f32[512]{0:T(512)}, bf16[2048,512]{1,0:T(8,128)(2,1)}, f32[2048,512]{1,0:T(8,128)S(1)}) fusion(f32[2048,512]{1,0:T(8,128)S(1)} %fusion.105, f32[512]{0:T(512)S(1)} %copy-done.34, bf16[2048,1024]{1,0:T(8,128)(2,1)S(1)} %select_dynamic-update-slice_fusion, bf16[512,1024]{1,0:T(8,128)(2,1)} %constant_dynamic-update-slice_fusion.15), kind=kOutput, calls=%fused_computation.332 | convolution fusion | flops 2225077760 | bytes 15732736 | tf_op jit(solution)/shard_map/nd,fd->nf/dot_general | solution.py:693
  161.6 3.7 fusion.106
  181.2 4.9 fusion.42
  191.6 10.3 %collective-permute-done.28 = bf16[512,128]{1,0:T(8,128)(2,1)S(1)} collective-permute-done((bf16[512,128]{1,0:T(8,128)(2,1)S(1)}, bf16[512,128]{1,0:T(8,128)(2,1)S(1)}, u32[]{:S(2)}, u32[]{:S(2)}) %collective-permute-start.28) | collective-permute-done | bytes 131104 | tf_op jit(solution)/shard_map/ppermute | solution.py:461
  210.6 3.9 collective-permute-done.83
  215.9 7.5 %collective-permute-done.84 = bf16[4,64,512]{2,1,0:T(8,128)(2,1)S(1)} collective-permute-done((bf16[4,64,512]{2,1,0:T(8,128)(2,1)S(1)}, bf16[4,64,512]{2,1,0:T(8,128)(2,1)S(1)}, u32[]{:S(2)}, u32[]{:S(2)}) %collective-permute-start.84) | collective-permute-done | bytes 262176 | tf_op jit(solution)/shard_map/ppermute | solution.py:461
  223.4 22.2 %collective-permute-done.85 = bf16[4,64,512]{2,1,0:T(8,128)(2,1)S(1)} collective-permute-done((bf16[4,64,512]{2,1,0:T(8,128)(2,1)S(1)}, bf16[4,64,512]{2,1,0:T(8,128)(2,1)S(1)}, u32[]{:S(2)}, u32[]{:S(2)}) %collective-permute-start.85) | collective-permute-done | bytes 262176 | tf_op jit(solution)/shard_map/ppermute | solution.py:461
  245.9 3.9 collective-permute-done.96
  255.4 3.9 collective-permute-done.88
  263.3 12.2 %collective-permute-done.17 = bf16[512,384]{1,0:T(8,128)(2,1)S(1)} collective-permute-done((bf16[512,384]{1,0:T(8,128)(2,1)S(1)}, bf16[512,384]{1,0:T(8,128)(2,1)S(1)}, u32[]{:S(2)}, u32[]{:S(2)}) %collective-permute-start.17) | collective-permute-done | bytes 393248 | tf_op jit(solution)/shard_map/ppermute | solution.py:461
  275.5 45.2 %attention.1 = (bf16[2048,128]{1,0:T(8,128)(2,1)S(1)}, bf16[2048,128]{1,0:T(8,128)(2,1)S(1)}, bf16[2048,256]{1,0:T(8,128)(2,1)S(1)}) custom-call(bf16[2048,384]{1,0:T(8,128)(2,1)S(1)} %constant_dynamic-update-slice_fusion.30.refs_0_.refs_1_.refs_2_, bf16[2048,384]{1,0:T(8,128)(2,1)S(1)} %constant_dynamic-update-slice_fusion.30.refs_0_.refs_1_.refs_2_, ...), custom_call_target="tpu_custom_call" | custom-call | flops 9059696640 | bytes 4194304 | tf_op jit(solution)/shard_map/attention/pallas_call | solution.py:422
  331.8 4.0 collective-permute-done.35
  339.3 3.8 collective-permute-done.48
  344.9 5.5 %collective-permute-done.49 = bf16[512,128]{1,0:T(8,128)(2,1)S(1)} collective-permute-done((bf16[512,128]{1,0:T(8,128)(2,1)S(1)}, bf16[512,128]{1,0:T(8,128)(2,1)S(1)}, u32[]{:S(2)}, u32[]{:S(2)}) %collective-permute-start.49) | collective-permute-done | bytes 131104 | tf_op jit(solution)/shard_map/ppermute | solution.py:461
  350.5 4.0 fusion.45
  363.9 6.3 %collective-permute-done.91 = bf16[64,4,512]{2,0,1:T(8,128)(2,1)S(1)} collective-permute-done((bf16[64,4,512]{2,0,1:T(8,128)(2,1)S(1)}, bf16[64,4,512]{2,0,1:T(8,128)(2,1)S(1)}, u32[]{:S(2)}, u32[]{:S(2)}) %collective-permute-start.91) | collective-permute-done | bytes 262176 | tf_op jit(solution)/shard_map/ppermute | solution.py:461
  380.1 4.7 collective-permute-done.76
  400.4 4.2 fusion.46
  410.3 7.9 %fusion.93 = (f32[1024]{0:T(1024)S(1)}, f32[1024]{0:T(1024)S(1)}, f32[2048,1024]{1,0:T(8,128)}, f32[1024]{0:T(1024)S(1)}, f32[1024]{0:T(1024)S(1)}) fusion(f32[2048]{0:T(1024)S(1)} %add_rsqrt_fusion, f32[2048]{0:T(1024)S(1)} %broadcast_multiply_fusion, bf16[2048,1024]{1,0:T(8,128)(2,1)S(1)} %select_dynamic-update-slice_fusion.6, f32[1024]{0:T(1024)S(1)} %bitcast.348, ...), kind=kOutput, calls=%fused_computation.330 | convolution fusion | flops 2172645376 | bytes 24158208 | tf_op jit(solution)/shard_map/nf,df->nd/dot_general | solution.py:699
  421.9 3.8 fusion.34
  443.2 9.0 %collective-permute-done.66 = bf16[4,64,384]{2,1,0:T(8,128)(2,1)S(1)} collective-permute-done((bf16[4,64,384]{2,1,0:T(8,128)(2,1)}, bf16[4,64,384]{2,1,0:T(8,128)(2,1)S(1)}, u32[]{:S(2)}, u32[]{:S(2)}) %collective-permute-start.66) | collective-permute-done | bytes 196640 | tf_op jit(solution)/shard_map/ppermute | solution.py:461
  452.2 6.1 %collective-permute-done.67 = bf16[4,64,384]{2,1,0:T(8,128)(2,1)S(1)} collective-permute-done((bf16[4,64,384]{2,1,0:T(8,128)(2,1)S(1)}, bf16[4,64,384]{2,1,0:T(8,128)(2,1)S(1)}, u32[]{:S(2)}, u32[]{:S(2)}) %collective-permute-start.67) | collective-permute-done | bytes 196640 | tf_op jit(solution)/shard_map/ppermute | solution.py:461
  464.1 3.8 fusion.98
  476.4 6.6 %collective-permute-done.43 = bf16[256,1024]{1,0:T(8,128)(2,1)S(1)} collective-permute-done((bf16[256,1024]{1,0:T(8,128)(2,1)S(1)}, bf16[256,1024]{1,0:T(8,128)(2,1)S(1)}, u32[]{:S(2)}, u32[]{:S(2)}) %collective-permute-start.43) | collective-permute-done | bytes 524320 | tf_op jit(solution)/shard_map/ppermute | solution.py:461
  485.9 9.9 %collective-permute-done.44 = bf16[256,1024]{1,0:T(8,128)(2,1)S(1)} collective-permute-done((bf16[256,1024]{1,0:T(8,128)(2,1)S(1)}, bf16[256,1024]{1,0:T(8,128)(2,1)S(1)}, u32[]{:S(2)}, u32[]{:S(2)}) %collective-permute-start.44) | collective-permute-done | bytes 524320 | tf_op jit(solution)/shard_map/ppermute | solution.py:461
  499.0 6.6 %collective-permute-done.54 = bf16[256,1024]{1,0:T(8,128)(2,1)S(1)} collective-permute-done((bf16[256,1024]{1,0:T(8,128)(2,1)S(1)}, bf16[256,1024]{1,0:T(8,128)(2,1)S(1)}, u32[]{:S(2)}, u32[]{:S(2)}) %collective-permute-start.54) | collective-permute-done | bytes 524320 | tf_op jit(solution)/shard_map/ppermute | solution.py:461
  506.0 9.5 %collective-permute-done.55 = bf16[256,1024]{1,0:T(8,128)(2,1)S(1)} collective-permute-done((bf16[256,1024]{1,0:T(8,128)(2,1)S(1)}, bf16[256,1024]{1,0:T(8,128)(2,1)S(1)}, u32[]{:S(2)}, u32[]{:S(2)}) %collective-permute-start.55) | collective-permute-done | bytes 524320 | tf_op jit(solution)/shard_map/ppermute | solution.py:461
  (489 shorter events, 263.8 us)
Async XLA Ops:
  5.8 29.1 %collective-permute-start.6 = (bf16[6,256]{1,0:T(8,128)(2,1)S(1)}, bf16[6,256]{1,0:T(8,128)(2,1)}, u32[]{:S(2)}, u32[]{:S(2)}) collective-permute-start(bf16[6,256]{1,0:T(8,128)(2,1)S(1)} %reshape.348), channel_id=1, source_target_pairs={{0,8},{8,0},{16,24},{24,16},{1,9},{9,1},{17,25},{25,17},{2,10},{10... | collective-permute-start | bytes 9224 | tf_op jit(solution)/shard_map/ppermute | solution.py:461
  7.4 29.3 %collective-permute-start.7 = (bf16[6,256]{1,0:T(8,128)(2,1)S(1)}, bf16[6,256]{1,0:T(8,128)(2,1)}, u32[]{:S(2)}, u32[]{:S(2)}) collective-permute-start(bf16[6,256]{1,0:T(8,128)(2,1)S(1)} %reshape.348), channel_id=1, source_target_pairs={{0,16},{8,24},{16,0},{24,8},{1,17},{9,25},{17,1},{25,9},{2,18},{10... | collective-permute-start | bytes 9224 | tf_op jit(solution)/shard_map/ppermute | solution.py:461
  8.9 30.5 %collective-permute-start.8 = (bf16[6,256]{1,0:T(8,128)(2,1)S(1)}, bf16[6,256]{1,0:T(8,128)(2,1)}, u32[]{:S(2)}, u32[]{:S(2)}) collective-permute-start(bf16[6,256]{1,0:T(8,128)(2,1)S(1)} %reshape.348), channel_id=1, source_target_pairs={{0,24},{8,16},{16,8},{24,0},{1,25},{9,17},{17,9},{25,1},{2,26},{10... | collective-permute-start | bytes 9224 | tf_op jit(solution)/shard_map/ppermute | solution.py:461
  10.7 30.5 %collective-permute-start.12 = (s32[2,512]{1,0:T(2,128)}, s32[2,512]{1,0:T(2,128)}, u32[]{:S(2)}, u32[]{:S(2)}) collective-permute-start(s32[2,512]{1,0:T(2,128)} %pad_add_fusion.1), channel_id=1, source_target_pairs={{0,8},{8,0},{16,24},{24,16},{1,9},{9,1},{17,25},{25,17},{2,10},{10... | collective-permute-start | bytes 12296 | tf_op jit(solution)/shard_map/ppermute | solution.py:461
  12.2 29.8 %collective-permute-start.13 = (s32[2,512]{1,0:T(2,128)}, s32[2,512]{1,0:T(2,128)}, u32[]{:S(2)}, u32[]{:S(2)}) collective-permute-start(s32[2,512]{1,0:T(2,128)} %pad_add_fusion.1), channel_id=1, source_target_pairs={{0,16},{8,24},{16,0},{24,8},{1,17},{9,25},{17,1},{25,9},{2,18},{10... | collective-permute-start | bytes 12296 | tf_op jit(solution)/shard_map/ppermute | solution.py:461
  36.7 40.5 %collective-permute-start.36 = (bf16[256,512]{1,0:T(8,128)(2,1)}, bf16[256,512]{1,0:T(8,128)(2,1)}, u32[]{:S(2)}, u32[]{:S(2)}) collective-permute-start(bf16[256,512]{1,0:T(8,128)(2,1)} %get-tuple-element.83), channel_id=1, source_target_pairs={{0,8},{8,0},{16,24},{24,16},{1,9},{9,1},{17,25},{25,17},{2,10},{10... | collective-permute-start | bytes 786440 | tf_op jit(solution)/shard_map/ppermute | solution.py:461
  49.0 28.2 %collective-permute-start.37 = (bf16[256,512]{1,0:T(8,128)(2,1)}, bf16[256,512]{1,0:T(8,128)(2,1)}, u32[]{:S(2)}, u32[]{:S(2)}) collective-permute-start(bf16[256,512]{1,0:T(8,128)(2,1)} %get-tuple-element.85), channel_id=1, source_target_pairs={{0,16},{8,24},{16,0},{24,8},{1,17},{9,25},{17,1},{25,9},{2,18},{10... | collective-permute-start | bytes 786440 | tf_op jit(solution)/shard_map/ppermute | solution.py:461
  72.4 38.7 %collective-permute-start = (bf16[256,1024]{1,0:T(8,128)(2,1)}, bf16[256,1024]{1,0:T(8,128)(2,1)}, u32[]{:S(2)}, u32[]{:S(2)}) collective-permute-start(bf16[256,1024]{1,0:T(8,128)(2,1)} %dynamic-slice_bitcast_fusion.1), channel_id=1, source_target_pairs={{0,8},{8,0},{16,24},{24,16},{1,9},{9,1},{17,25},{25,17},{2,10},{10... | collective-permute-start | bytes 1572872 | tf_op jit(solution)/shard_map/ppermute | solution.py:461
  72.9 38.4 %collective-permute-start.2 = (bf16[256,1024]{1,0:T(8,128)(2,1)}, bf16[256,1024]{1,0:T(8,128)(2,1)S(1)}, u32[]{:S(2)}, u32[]{:S(2)}) collective-permute-start(bf16[256,1024]{1,0:T(8,128)(2,1)} %dynamic-slice_bitcast_fusion.1), channel_id=1, source_target_pairs={{0,16},{8,24},{16,0},{24,8},{1,17},{9,25},{17,1},{25,9},{2,18},{10... | collective-permute-start | bytes 1572872 | tf_op jit(solution)/shard_map/ppermute | solution.py:461
  77.2 30.6 %collective-permute-start.40 = (bf16[512,256]{1,0:T(8,128)(2,1)}, bf16[512,256]{1,0:T(8,128)(2,1)S(1)}, u32[]{:S(2)}, u32[]{:S(2)}) collective-permute-start(bf16[512,256]{1,0:T(8,128)(2,1)} %get-tuple-element.89), channel_id=1, source_target_pairs={{0,16},{8,24},{16,0},{24,8},{1,17},{9,25},{17,1},{25,9},{2,18},{10... | collective-permute-start | bytes 786440 | tf_op jit(solution)/shard_map/ppermute | solution.py:461
  77.7 30.5 %collective-permute-start.41 = (bf16[512,256]{1,0:T(8,128)(2,1)}, bf16[512,256]{1,0:T(8,128)(2,1)S(1)}, u32[]{:S(2)}, u32[]{:S(2)}) collective-permute-start(bf16[512,256]{1,0:T(8,128)(2,1)} %get-tuple-element.86), channel_id=1, source_target_pairs={{0,24},{8,16},{16,8},{24,0},{1,25},{9,17},{17,9},{25,1},{2,26},{10... | collective-permute-start | bytes 786440 | tf_op jit(solution)/shard_map/ppermute | solution.py:461
  165.4 40.0 %collective-permute-start.92 = (bf16[1,128,1024]{2,1,0:T(8,128)(2,1)S(1)}, bf16[1,128,1024]{2,1,0:T(8,128)(2,1)S(1)}, u32[]{:S(2)}, u32[]{:S(2)}) collective-permute-start(bf16[1,128,1024]{2,1,0:T(8,128)(2,1)S(1)} %get-tuple-element.70), channel_id=1, source_target_pairs={{0,2},{2,0},{4,6},{6,4},{1,3},{3,1},{5,7},{7,5},{8,10},{10,8},{12,... | collective-permute-start | bytes 786440 | tf_op jit(solution)/shard_map/ppermute | solution.py:461
  166.5 39.9 %collective-permute-start.93 = (bf16[1,128,1024]{2,1,0:T(8,128)(2,1)S(1)}, bf16[1,128,1024]{2,1,0:T(8,128)(2,1)S(1)}, u32[]{:S(2)}, u32[]{:S(2)}) collective-permute-start(bf16[1,128,1024]{2,1,0:T(8,128)(2,1)S(1)} %get-tuple-element.72), channel_id=1, source_target_pairs={{0,4},{2,6},{4,0},{6,2},{1,5},{3,7},{5,1},{7,3},{8,12},{10,14},{12... | collective-permute-start | bytes 786440 | tf_op jit(solution)/shard_map/ppermute | solution.py:461
  169.8 38.9 %collective-permute-start.94 = (bf16[1,128,1024]{2,1,0:T(8,128)(2,1)S(1)}, bf16[1,128,1024]{2,1,0:T(8,128)(2,1)S(1)}, u32[]{:S(2)}, u32[]{:S(2)}) collective-permute-start(bf16[1,128,1024]{2,1,0:T(8,128)(2,1)S(1)} %get-tuple-element.71), channel_id=1, source_target_pairs={{0,6},{2,4},{4,2},{6,0},{1,7},{3,5},{5,3},{7,1},{8,14},{10,12},{12... | collective-permute-start | bytes 786440 | tf_op jit(solution)/shard_map/ppermute | solution.py:461
  175.2 26.6 %collective-permute-start.28 = (bf16[512,128]{1,0:T(8,128)(2,1)S(1)}, bf16[512,128]{1,0:T(8,128)(2,1)S(1)}, u32[]{:S(2)}, u32[]{:S(2)}) collective-permute-start(bf16[512,128]{1,0:T(8,128)(2,1)S(1)} %get-tuple-element.106), channel_id=1, source_target_pairs={{0,4},{2,6},{4,0},{6,2},{1,5},{3,7},{5,1},{7,3},{8,12},{10,14},{12... | collective-permute-start | bytes 393224 | tf_op jit(solution)/shard_map/ppermute | solution.py:461
  205.4 40.3 %collective-permute-start.85 = (bf16[4,64,512]{2,1,0:T(8,128)(2,1)S(1)}, bf16[4,64,512]{2,1,0:T(8,128)(2,1)S(1)}, u32[]{:S(2)}, u32[]{:S(2)}) collective-permute-start(bf16[4,64,512]{2,1,0:T(8,128)(2,1)S(1)} %get-tuple-element.74), channel_id=1, source_target_pairs={{0,6},{2,4},{4,2},{6,0},{1,7},{3,5},{5,3},{7,1},{8,14},{10,12},{12... | collective-permute-start | bytes 786440 | tf_op jit(solution)/shard_map/ppermute | solution.py:461
  206.5 54.2 %collective-permute-start.15 = (bf16[512,384]{1,0:T(8,128)(2,1)S(1)}, bf16[512,384]{1,0:T(8,128)(2,1)S(1)}, u32[]{:S(2)}, u32[]{:S(2)}) collective-permute-start(bf16[512,384]{1,0:T(8,128)(2,1)S(1)} %get-tuple-element.68), channel_id=1, source_target_pairs={{0,2},{2,0},{4,6},{6,4},{1,3},{3,1},{5,7},{7,5},{8,10},{10,8},{12,... | collective-permute-start | bytes 1179656 | tf_op jit(solution)/shard_map/ppermute | solution.py:461
  208.7 54.4 %collective-permute-start.16 = (bf16[512,384]{1,0:T(8,128)(2,1)S(1)}, bf16[512,384]{1,0:T(8,128)(2,1)S(1)}, u32[]{:S(2)}, u32[]{:S(2)}) collective-permute-start(bf16[512,384]{1,0:T(8,128)(2,1)S(1)} %get-tuple-element.67), channel_id=1, source_target_pairs={{0,4},{2,6},{4,0},{6,2},{1,5},{3,7},{5,1},{7,3},{8,12},{10,14},{12... | collective-permute-start | bytes 1179656 | tf_op jit(solution)/shard_map/ppermute | solution.py:461
  214.6 60.9 %collective-permute-start.17 = (bf16[512,384]{1,0:T(8,128)(2,1)S(1)}, bf16[512,384]{1,0:T(8,128)(2,1)S(1)}, u32[]{:S(2)}, u32[]{:S(2)}) collective-permute-start(bf16[512,384]{1,0:T(8,128)(2,1)S(1)} %get-tuple-element.66), channel_id=1, source_target_pairs={{0,6},{2,4},{4,2},{6,0},{1,7},{3,5},{5,3},{7,1},{8,14},{10,12},{12... | collective-permute-start | bytes 1179656 | tf_op jit(solution)/shard_map/ppermute | solution.py:461
  255.3 115.3 %collective-permute-start.98 = (bf16[4,128,256]{2,1,0:T(8,128)(2,1)S(1)}, bf16[4,128,256]{2,1,0:T(8,128)(2,1)}, u32[]{:S(2)}, u32[]{:S(2)}) collective-permute-start(bf16[4,128,256]{2,1,0:T(8,128)(2,1)S(1)} %bitcast_dynamic-update-slice_fusion.2), channel_id=1, source_target_pairs={{0,2},{2,0},{4,6},{6,4},{1,3},{3,1},{5,7},{7,5},{8,10},{10,8},{12,... | collective-permute-start | bytes 786440 | tf_op jit(solution)/shard_map/ppermute | solution.py:461
  259.3 113.9 %collective-permute-start.99 = (bf16[4,128,256]{2,1,0:T(8,128)(2,1)S(1)}, bf16[4,128,256]{2,1,0:T(8,128)(2,1)}, u32[]{:S(2)}, u32[]{:S(2)}) collective-permute-start(bf16[4,128,256]{2,1,0:T(8,128)(2,1)S(1)} %bitcast_dynamic-update-slice_fusion.2), channel_id=1, source_target_pairs={{0,4},{2,6},{4,0},{6,2},{1,5},{3,7},{5,1},{7,3},{8,12},{10,14},{12... | collective-permute-start | bytes 786440 | tf_op jit(solution)/shard_map/ppermute | solution.py:461
  260.6 124.7 %collective-permute-start.100 = (bf16[4,128,256]{2,1,0:T(8,128)(2,1)S(1)}, bf16[4,128,256]{2,1,0:T(8,128)(2,1)}, u32[]{:S(2)}, u32[]{:S(2)}) collective-permute-start(bf16[4,128,256]{2,1,0:T(8,128)(2,1)S(1)} %bitcast_dynamic-update-slice_fusion.2), channel_id=1, source_target_pairs={{0,6},{2,4},{4,2},{6,0},{1,7},{3,5},{5,3},{7,1},{8,14},{10,12},{12... | collective-permute-start | bytes 786440 | tf_op jit(solution)/shard_map/ppermute | solution.py:461
  360.5 39.7 %collective-permute-start.50 = (bf16[512,256]{1,0:T(8,128)(2,1)S(1)}, bf16[512,256]{1,0:T(8,128)(2,1)S(1)}, u32[]{:S(2)}, u32[]{:S(2)}) collective-permute-start(bf16[512,256]{1,0:T(8,128)(2,1)S(1)} %get-tuple-element.80), channel_id=1, source_target_pairs={{0,2},{2,0},{4,6},{6,4},{1,3},{3,1},{5,7},{7,5},{8,10},{10,8},{12,... | collective-permute-start | bytes 786440 | tf_op jit(solution)/shard_map/ppermute | solution.py:461
  384.8 79.3 %collective-permute-start.42 = (bf16[4,256,1024]{2,1,0:T(8,128)(2,1)}, bf16[4,256,1024]{2,1,0:T(8,128)(2,1)}, u32[]{:S(2)}, u32[]{:S(2)}) collective-permute-start(bf16[4,256,1024]{2,1,0:T(8,128)(2,1)} %fusion.33), channel_id=1, source_target_pairs={{0,1},{1,0},{2,3},{3,2},{4,5},{5,4},{6,7},{7,6},{8,9},{9,8},{10,11... | collective-permute-start | bytes 6291464 | tf_op jit(solution)/shard_map/ppermute | solution.py:461
  397.6 34.6 %collective-permute-start.80 = (bf16[4,32,256]{2,1,0:T(8,128)(2,1)S(1)}, bf16[4,32,256]{2,1,0:T(8,128)(2,1)S(1)}, u32[]{:S(2)}, u32[]{:S(2)}) collective-permute-start(bf16[4,32,256]{2,1,0:T(8,128)(2,1)S(1)} %constant_dynamic-update-slice_fusion.5), channel_id=1, source_target_pairs={{0,2},{2,0},{4,6},{6,4},{1,3},{3,1},{5,7},{7,5},{8,10},{10,8},{12,... | collective-permute-start | bytes 196616 | tf_op jit(solution)/shard_map/ppermute | solution.py:461
  441.4 30.3 %collective-permute-start.53 = (bf16[4,256,1024]{2,1,0:T(8,128)(2,1)}, bf16[4,256,1024]{2,1,0:T(8,128)(2,1)S(1)}, u32[]{:S(2)}, u32[]{:S(2)}) collective-permute-start(bf16[4,256,1024]{2,1,0:T(8,128)(2,1)} %fusion.34), channel_id=1, source_target_pairs={{0,1},{1,0},{2,3},{3,2},{4,5},{5,4},{6,7},{7,6},{8,9},{9,8},{10,11... | collective-permute-start | bytes 6291464 | tf_op jit(solution)/shard_map/ppermute | solution.py:461
  469.7 26.1 %collective-permute-start.44 = (bf16[256,1024]{1,0:T(8,128)(2,1)S(1)}, bf16[256,1024]{1,0:T(8,128)(2,1)S(1)}, u32[]{:S(2)}, u32[]{:S(2)}) collective-permute-start(bf16[256,1024]{1,0:T(8,128)(2,1)S(1)} %get-tuple-element.65), channel_id=1, source_target_pairs={{0,16},{8,24},{16,0},{24,8},{1,17},{9,25},{17,1},{25,9},{2,18},{10... | collective-permute-start | bytes 1572872 | tf_op jit(solution)/shard_map/ppermute | solution.py:461
  471.6 24.2 %collective-permute-start.45 = (bf16[256,1024]{1,0:T(8,128)(2,1)S(1)}, bf16[256,1024]{1,0:T(8,128)(2,1)S(1)}, u32[]{:S(2)}, u32[]{:S(2)}) collective-permute-start(bf16[256,1024]{1,0:T(8,128)(2,1)S(1)} %get-tuple-element.64), channel_id=1, source_target_pairs={{0,24},{8,16},{16,8},{24,0},{1,25},{9,17},{17,9},{25,1},{2,26},{10... | collective-permute-start | bytes 1572872 | tf_op jit(solution)/shard_map/ppermute | solution.py:461
  472.9 32.6 %collective-permute-start.54 = (bf16[256,1024]{1,0:T(8,128)(2,1)S(1)}, bf16[256,1024]{1,0:T(8,128)(2,1)S(1)}, u32[]{:S(2)}, u32[]{:S(2)}) collective-permute-start(bf16[256,1024]{1,0:T(8,128)(2,1)S(1)} %get-tuple-element.58), channel_id=1, source_target_pairs={{0,8},{8,0},{16,24},{24,16},{1,9},{9,1},{17,25},{25,17},{2,10},{10... | collective-permute-start | bytes 1572872 | tf_op jit(solution)/shard_map/ppermute | solution.py:461
  474.5 41.0 %collective-permute-start.55 = (bf16[256,1024]{1,0:T(8,128)(2,1)S(1)}, bf16[256,1024]{1,0:T(8,128)(2,1)S(1)}, u32[]{:S(2)}, u32[]{:S(2)}) collective-permute-start(bf16[256,1024]{1,0:T(8,128)(2,1)S(1)} %get-tuple-element.60), channel_id=1, source_target_pairs={{0,16},{8,24},{16,0},{24,8},{1,17},{9,25},{17,1},{25,9},{2,18},{10... | collective-permute-start | bytes 1572872 | tf_op jit(solution)/shard_map/ppermute | solution.py:461
  483.0 32.5 %collective-permute-start.56 = (bf16[256,1024]{1,0:T(8,128)(2,1)S(1)}, bf16[256,1024]{1,0:T(8,128)(2,1)S(1)}, u32[]{:S(2)}, u32[]{:S(2)}) collective-permute-start(bf16[256,1024]{1,0:T(8,128)(2,1)S(1)} %get-tuple-element.59), channel_id=1, source_target_pairs={{0,24},{8,16},{16,8},{24,0},{1,25},{9,17},{17,9},{25,1},{2,26},{10... | collective-permute-start | bytes 1572872 | tf_op jit(solution)/shard_map/ppermute | solution.py:461
  495.8 24.4 %collective-permute-start.72 = (bf16[64,4,384]{2,0,1:T(8,128)(2,1)S(1)}, bf16[64,4,384]{2,0,1:T(8,128)(2,1)S(1)}, u32[]{:S(2)}, u32[]{:S(2)}) collective-permute-start(bf16[64,4,384]{2,0,1:T(8,128)(2,1)S(1)} %bitcast_dynamic-update-slice_fusion.9), channel_id=1, source_target_pairs={{0,4},{2,6},{4,0},{6,2},{1,5},{3,7},{5,1},{7,3},{8,12},{10,14},{12... | collective-permute-start | bytes 589832 | tf_op jit(solution)/shard_map/ppermute | solution.py:461
  (118 other events, 1321.0 us)

commit v2 on v1

--- a/solution.py
+++ b/solution.py
@@ -297,18 +297,32 @@
 
 
 def attention_body(
-    heads, q_ref, k_ref, v_ref, dc_ref, qseg_ref, kseg_ref, ctx_ref, dq_ref, dkv_ref,
-    kt_ref, vt_ref, s_ref, e_ref, dk_acc, dv_acc,
+    heads, flips, place_ref, *refs,
 ):
     f32 = jnp.float32
     bf16 = jnp.bfloat16
+    ins, refs = refs[:flips], refs[flips:]
+    kseg_ref, qseg_ref, refs = refs[0], refs[1], refs[2:]
+    outs, refs = refs[:flips], refs[flips:]
+    x_ref, y_ref, kt_ref, vt_ref, s_ref, e_ref, dk_acc, dv_acc = refs
     step = pl.program_id(0)
-    rows, width = q_ref.shape
+    place = place_ref[0]
+    rows = s_ref.shape[2]
+    width = dk_acc.shape[1]
     chunks, _, chunk = kt_ref.shape
     hd = width // heads
+    span = ins[0].shape[0]
+
+    def spot(flip):
+        return pl.ds(pl.multiple_of((place ^ flip) * span, span), span)
+
+    k_ref = x_ref.at[:, width : 2 * width]
+    v_ref = x_ref.at[:, 2 * width : 3 * width]
 
     @pl.when(step == 0)
     def _():
+        for flip in range(flips):
+            x_ref[spot(flip), :] = ins[flip][...]
         for c in range(chunks):
             part = pl.ds(c * chunk, chunk)
             kt_ref[c] = k_ref[part, :].astype(f32).T.astype(bf16)
@@ -316,10 +330,11 @@
         dk_acc[...] = jnp.zeros_like(dk_acc)
         dv_acc[...] = jnp.zeros_like(dv_acc)
 
+    here = pl.ds(pl.multiple_of(step * rows, rows), rows)
     used = ((step + 1) * rows + chunk - 1) // chunk
-    q = q_ref[...]
+    q = x_ref[here, :width]
     q_t = q.astype(f32).T
-    dc_t = dc_ref[...].astype(f32).T
+    dc_t = x_ref[here, 3 * width :].astype(f32).T
     row_head = lax.broadcasted_iota(jnp.int32, (width, rows), 0) // hd
     lane_head = lax.broadcasted_iota(jnp.int32, (rows, width), 1) // hd
     q_heads_t = [jnp.where(row_head == h, q_t, 0.0).astype(bf16) for h in range(heads)]
@@ -375,7 +390,7 @@
         deltas.append(jnp.sum(ctx_h * dc_h, 0, keepdims=True) * inv)
         ctx_parts.append(ctx_h)
         dcn_parts.append(dc_h * inv)
-    ctx_ref[...] = jnp.concatenate(ctx_parts, 0).T.astype(bf16)
+    y_ref[here, :width] = jnp.concatenate(ctx_parts, 0).T.astype(bf16)
     dcn_t = jnp.concatenate(dcn_parts, 0)
     dcn = dcn_t.T
     dcn_heads_t = [jnp.where(row_head == h, dcn_t, 0.0).astype(bf16) for h in range(heads)]
@@ -405,55 +420,96 @@
     dq = lax.fori_loop(
         0, used, back, tuple(jnp.zeros((hd, rows), f32) for _ in range(heads))
     )
-    dq_ref[...] = (jnp.concatenate(dq, 0).T * HD ** (-0.5)).astype(bf16)
+    y_ref[here, width : 2 * width] = (jnp.concatenate(dq, 0).T * HD ** (-0.5)).astype(bf16)
 
     @pl.when(step == pl.num_programs(0) - 1)
     def _():
-        dkv_ref[:, :width] = dk_acc[...].astype(bf16)
-        dkv_ref[:, width:] = dv_acc[...].astype(bf16)
-
-
-def attention(qkv, dctx, seg, block=256, chunk=256):
-    count, width = dctx.shape
+        y_ref[:, 2 * width : 3 * width] = dk_acc[...].astype(bf16)
+        y_ref[:, 3 * width :] = dv_acc[...].astype(bf16)
+        for flip in range(flips):
+            outs[flip][...] = y_ref[spot(flip), :]
+
+
+def attention(blocks, seg, place, block=256, chunk=256):
+    flips = len(blocks)
+    span, columns = blocks[0].shape
+    count, width = span * flips, columns // 4
     heads = width // HD
     bf16 = jnp.bfloat16
     f32 = jnp.float32
     pairs = count * (count + block) // 2 * heads
+    whole = pl.BlockSpec((span, columns), lambda i, p: (0, 0))
     return pl.pallas_call(
-        lambda *refs: attention_body(heads, *refs),
-        grid=(count // block,),
-        in_specs=[
-            pl.BlockSpec((block, width), lambda i: (i, 0)),
-            pl.BlockSpec((count, width), lambda i: (0, 1)),
-            pl.BlockSpec((count, width), lambda i: (0, 2)),
-            pl.BlockSpec((block, width), lambda i: (i, 0)),
-            pl.BlockSpec((1, block), lambda i: (0, i)),
-            pl.BlockSpec((count, 1), lambda i: (0, 0)),
-        ],
-        out_specs=[
-            pl.BlockSpec((block, width), lambda i: (i, 0)),
-            pl.BlockSpec((block, width), lambda i: (i, 0)),
-            pl.BlockSpec((count, 2 * width), lambda i: (0, 0)),
-        ],
-        out_shape=[
-            jax.ShapeDtypeStruct((count, width), bf16),
-            jax.ShapeDtypeStruct((count, width), bf16),
-            jax.ShapeDtypeStruct((count, 2 * width), bf16),
-        ],
-        scratch_shapes=[
-            pltpu.VMEM((count // chunk, width, chunk), bf16),
-            pltpu.VMEM((count // chunk, width, chunk), bf16),
-            pltpu.VMEM((heads, count, block), f32),
-            pltpu.VMEM((heads, count, block), bf16),
-            pltpu.VMEM((count, width), f32),
-            pltpu.VMEM((count, width), f32),
-        ],
-        compiler_params=pltpu.CompilerParams(vmem_limit_bytes=40 * 1024 * 1024),
+        lambda *refs: attention_body(heads, flips, *refs),
+        grid_spec=pltpu.PrefetchScalarGridSpec(
+            num_scalar_prefetch=1,
+            grid=(count // block,),
+            in_specs=[whole] * flips
+            + [
+                pl.BlockSpec((count, 1), lambda i, p: (0, 0)),
+                pl.BlockSpec((1, block), lambda i, p: (0, i)),
+            ],
+            out_specs=[whole] * flips,
+            scratch_shapes=[
+                pltpu.VMEM((count, columns), bf16),
+                pltpu.VMEM((count, columns), bf16),
+                pltpu.VMEM((count // chunk, width, chunk), bf16),
+                pltpu.VMEM((count // chunk, width, chunk), bf16),
+                pltpu.VMEM((heads, count, block), f32),
+                pltpu.VMEM((heads, count, block), bf16),
+                pltpu.VMEM((count, width), f32),
+                pltpu.VMEM((count, width), f32),
+            ],
+        ),
+        out_shape=[jax.ShapeDtypeStruct((span, columns), bf16)] * flips,
+        compiler_params=pltpu.CompilerParams(vmem_limit_bytes=48 * 1024 * 1024),
         cost_estimate=pl.CostEstimate(
             flops=10 * pairs * HD * 3, bytes_accessed=count * width * 16, transcendentals=pairs
         ),
         name="attention",
-    )(qkv, qkv, qkv, dctx, seg[None, :], seg[:, None])
+    )(place.reshape(1), *blocks, seg[:, None], seg[None, :])
+
+
+def norm_body(core_ref, mine_ref, other_ref, params_ref, first_ref, second_ref, normed_ref):
+    core = core_ref[0]
+    f32 = jnp.float32
+    for source, slot in ((mine_ref, core), (other_ref, 1 - core)):
+        normed, _ = normalize(source[0].astype(f32))
+        normed_ref[0, slot] = normed.astype(jnp.bfloat16)
+        first_ref[0, slot] = (normed * params_ref[0:1] + params_ref[1:2]).astype(jnp.bfloat16)
+        second_ref[0, slot] = (normed * params_ref[2:3] + params_ref[3:4]).astype(jnp.bfloat16)
+
+
+def merge_body(core_ref, mine_ref, other_ref, out_ref):
+    core = core_ref[0]
+    out_ref[0, core] = mine_ref[0]
+    out_ref[0, 1 - core] = other_ref[0]
+
+
+def both_cores(body, mine, core, params, results):
+    size, half, cols = mine.shape
+    other = partner(mine, "tp", 1)
+    side = pl.BlockSpec((1, half, cols), lambda i, c: (i, 0, 0))
+    out = pl.BlockSpec((1, 2, half, cols), lambda i, c: (i, 0, 0, 0))
+    extra = [pl.BlockSpec(p.shape, lambda i, c: (0, 0)) for p in params]
+    made = pl.pallas_call(
+        body,
+        grid_spec=pltpu.PrefetchScalarGridSpec(
+            num_scalar_prefetch=1,
+            grid=(size,),
+            in_specs=[side, side] + extra,
+            out_specs=[out] * results,
+        ),
+        out_shape=[jax.ShapeDtypeStruct((size, 2, half, cols), mine.dtype)] * results,
+        compiler_params=pltpu.CompilerParams(vmem_limit_bytes=32 * 1024 * 1024),
+        cost_estimate=pl.CostEstimate(
+            flops=size * half * cols * 20,
+            bytes_accessed=size * half * cols * 4 * (1 + results),
+            transcendentals=0,
+        ),
+        name=body.__name__,
+    )(core.reshape(1), mine, other, *params)
+    return [x.reshape(size * 2 * half, cols) for x in made]
 
 
 def partner(tensor, axis, flip):
@@ -465,119 +521,195 @@
     return lax.dynamic_slice_in_dim(tensor, index * size, size, dim)
 
 
-def put(buffer, block, index, dim=0):
-    return lax.dynamic_update_slice_in_dim(buffer, block, index * block.shape[dim], dim)
-
-
-def exchange(tensor, axis, dim_from, dim_to):
-    size = lax.axis_size(axis)
-    me = lax.axis_index(axis)
-    part = tensor.shape[dim_from] // size
-    shape = list(tensor.shape)
-    shape[dim_from] = part
-    shape[dim_to] *= size
-    out = jnp.zeros(shape, tensor.dtype)
-    for flip in range(size):
-        block = pick(tensor, me ^ flip, part, dim_from)
-        if flip:
-            block = partner(block, axis, flip)
-        out = put(out, block, me ^ flip, dim_to)
-    return out
-
-
-def plane_gather(block, axis="fsdp"):
-    return [block] + [partner(block, axis, flip) for flip in range(1, lax.axis_size(axis))]
-
-
-def chip_gather(rows):
+def swap(tensor, axis):
+    return lax.all_to_all(tensor, axis, 0, 0)
+
+
+def gather(block, axis):
+    return swap(jnp.broadcast_to(block[None], (lax.axis_size(axis),) + block.shape), axis)
+
+
+def double_up(block, axis, order):
+    held = block[None]
+    bits = []
+    for bit in order:
+        held = jnp.stack([held, partner(held, axis, 1 << bit)], 0)
+        bits.insert(0, bit)
+    levels = len(order)
+    held = held.reshape((2,) * levels + block.shape)
+    turn = [bits.index(bit) for bit in reversed(range(levels))]
+    held = held.transpose(turn + list(range(levels, levels + block.ndim)))
+    return held.reshape((2**levels,) + block.shape)
+
+
+def chip_start(partial, size):
+    f32 = jnp.float32
     core = lax.axis_index("tp")
-    half = rows.shape[0] // 2
-    mine = pick(rows, core, half)
-    out = [rows]
-    for block in plane_gather(mine)[1:]:
-        other = partner(block, "tp", 1)
-        out.append(jnp.where(core == 0, block, other))
-        out.append(jnp.where(core == 0, other, block))
-    return jnp.concatenate(out, 0)
-
-
-def chip_scatter(partial, count):
+    halves = partial.reshape(size, 2, -1, partial.shape[1])
+    away = lax.dynamic_index_in_dim(halves, 1 - core, 1, keepdims=False)
+    kept = lax.dynamic_index_in_dim(halves, core, 1, keepdims=False)
+    return (kept.astype(f32) + partner(away, "tp", 1).astype(f32)).astype(partial.dtype)
+
+
+def chip_finish(sending):
+    f32 = jnp.float32
+    total = sending[0].astype(f32)
+    for flip in range(1, sending.shape[0]):
+        total = total + partner(sending[flip], "fsdp", flip).astype(f32)
+    return total
+
+
+def chip_join(mine):
+    core = lax.axis_index("tp")
+    other = partner(mine, "tp", 1)
+    low = jnp.where(core == 0, mine, other)
+    high = jnp.where(core == 0, other, mine)
+    return jnp.concatenate([low, high], 0)
+
+
+def pack_wide(up, down, out, low, chips, part):
+    span = down.shape[3] // chips
+    for chip in range(chips):
+        out[0, chip, :part, :] = up[chip, 0, low]
+        for half in range(2):
+            out[0, chip, part:, half * span : (half + 1) * span] = down[
+                0, low, half * part : (half + 1) * part, chip * span : (chip + 1) * span
+            ]
+
+
+def pack_heads(joint, outw, out, low, chips, part):
+    width = joint.shape[4]
+    span = outw.shape[3] // chips // 2
+    rows = part // 2
+    for chip in range(chips):
+        out[0, chip, :, :width] = joint[chip, 0, low]
+        for half in range(2):
+            begin = (2 * chip + half) * span
+            out[0, chip, half * rows : (half + 1) * rows, width:] = outw[
+                0, low, :, begin : begin + span
+            ]
+
+
+def pack(body, wide, tall, rows, chips, place):
+    bf16 = jnp.bfloat16
+    depth = 4
+    part = wide.shape[0] // chips // depth
+    cols = part * 8
+    wide = wide.reshape(chips, 2, 2, part, wide.shape[1])
+    tall = tall.reshape(2, 2, tall.shape[0] // depth, tall.shape[1])
+
+    def run(place_ref, wide_ref, tall_ref, kept_ref, away_ref):
+        side = place_ref[0] & 1
+        body(wide_ref, tall_ref, kept_ref, side, chips, part)
+        body(wide_ref, tall_ref, away_ref, 1 - side, chips, part)
+
+    made = jax.ShapeDtypeStruct((2, chips, rows, cols), bf16)
+    out = pl.BlockSpec((1, chips, rows, cols), lambda i, p: (i, 0, 0, 0))
+    return pl.pallas_call(
+        run,
+        grid_spec=pltpu.PrefetchScalarGridSpec(
+            num_scalar_prefetch=1,
+            grid=(2,),
+            in_specs=[
+                pl.BlockSpec(
+                    (chips, 1, 2, part, wide.shape[4]), lambda i, p: (0, i, 0, 0, 0)
+                ),
+                pl.BlockSpec((1,) + tall.shape[1:], lambda i, p: (i, 0, 0, 0)),
+            ],
+            out_specs=[out, out],
+        ),
+        out_shape=[made, made],
+        compiler_params=pltpu.CompilerParams(vmem_limit_bytes=24 * 1024 * 1024),
+        cost_estimate=pl.CostEstimate(
+            flops=0, bytes_accessed=16 * chips * rows * cols, transcendentals=0
+        ),
+        name=body.__name__,
+    )(place.reshape(1), wide, tall)
+
+
+def unpack_wide(x, up, down, chips, part):
+    f32 = jnp.float32
+    span = down.shape[3]
+    cols = x.shape[2]
+    for chip in range(chips):
+        up[:, chip * cols : (chip + 1) * cols] = x[chip, :part, :].astype(f32)
+        for half in range(2):
+            down[chip, 0, half * part : (half + 1) * part, :] = x[
+                chip, part:, half * span : (half + 1) * span
+            ].astype(f32)
+
+
+def unpack_heads(x, joint, outw, chips, part):
+    f32 = jnp.float32
+    span = outw.shape[3] // 2
+    rows = part // 2
+    width = joint.shape[2] // chips
+    for chip in range(chips):
+        for kind in range(3):
+            joint[kind, :, chip * width : (chip + 1) * width] = x[
+                chip, :, kind * width : (kind + 1) * width
+            ].astype(f32)
+        for half in range(2):
+            outw[chip, 0, :, half * span : (half + 1) * span] = x[
+                chip, half * rows : (half + 1) * rows, 3 * width :
+            ].astype(f32)
+
+
+def unpack(body, blocks, wide, wide_block, tall, tall_block, place):
+    f32 = jnp.float32
+    chips, rows, cols = blocks[0].shape
+    depth = len(blocks)
+    whole = pl.BlockSpec((chips, rows, cols), lambda i, p: (0, 0, 0))
+
+    def run(place_ref, *refs):
+        for k in range(depth):
+
+            @pl.when(pl.program_id(0) == k)
+            def _(k=k):
+                body(refs[k], refs[depth], refs[depth + 1], chips, cols // 8)
+
+    def at(dim, count):
+        return lambda i, p: tuple((p[0] ^ i) if d == dim else 0 for d in range(count))
+
+    dim = len(wide) - 2
+    return pl.pallas_call(
+        run,
+        grid_spec=pltpu.PrefetchScalarGridSpec(
+            num_scalar_prefetch=1,
+            grid=(depth,),
+            in_specs=[whole] * depth,
+            out_specs=[
+                pl.BlockSpec(wide_block, at(dim, len(wide))),
+                pl.BlockSpec(tall_block, at(1, len(tall))),
+            ],
+        ),
+        out_shape=[jax.ShapeDtypeStruct(wide, f32), jax.ShapeDtypeStruct(tall, f32)],
+        compiler_params=pltpu.CompilerParams(vmem_limit_bytes=24 * 1024 * 1024),
+        cost_estimate=pl.CostEstimate(
+            flops=0, bytes_accessed=6 * depth * chips * rows * cols, transcendentals=0
+        ),
+        name=body.__name__,
+    )(place.reshape(1), *blocks)
+
+
+def sum_slots(kept, away, gate=()):
     f32 = jnp.float32
     bf16 = jnp.bfloat16
-    core = lax.axis_index("tp")
-    size = partial.shape[0] // count
-    halves = partial.reshape(size, 2, count // 2, partial.shape[1])
-    away = lax.dynamic_index_in_dim(halves, 1 - core, 1, keepdims=False).astype(bf16)
-    kept = lax.dynamic_index_in_dim(halves, core, 1, keepdims=False)
-    summed = kept + partner(away, "tp", 1).astype(f32)
-    sending = summed.astype(bf16)
-    total = summed[0]
-    for flip in range(1, size):
-        total = total + partner(sending[flip], "fsdp", flip).astype(f32)
-    other = partner(total, "tp", 1)
-    low = jnp.where(core == 0, total, other)
-    high = jnp.where(core == 0, other, total)
-    return jnp.concatenate([low, high], 0)
-
-
-def spread_sum(parts, axis):
-    size = lax.axis_size(axis)
-    me = lax.axis_index(axis)
-    total = lax.dynamic_index_in_dim(parts, me, 1, keepdims=False).astype(jnp.float32)
-    for flip in range(1, size):
-        block = lax.dynamic_index_in_dim(parts, me ^ flip, 1, keepdims=False)
-        total = total + partner(block, axis, flip).astype(jnp.float32)
-    return total
-
-
-def share_rows(grad):
-    size, depth = lax.axis_size("fsdp"), lax.axis_size("ctx")
-    rows, cols = grad.shape
-    part = rows // size // depth
-    quarter = spread_sum(grad.reshape(size, depth, part, cols), "ctx").astype(jnp.bfloat16)
-    me, place = lax.axis_index("fsdp"), lax.axis_index("ctx")
-    held = jnp.zeros((part, size, cols), jnp.bfloat16)
-    for flip in range(size):
-        block = lax.dynamic_index_in_dim(quarter, me ^ flip, 0, keepdims=False)
-        if flip:
-            block = partner(block, "fsdp", flip)
-        held = lax.dynamic_update_slice(held, block[:, None], (0, me ^ flip, 0))
-    out = jnp.zeros((depth, part, size, cols), jnp.float32)
-    for flip in range(depth):
-        block = partner(held, "ctx", flip) if flip else held
-        out = lax.dynamic_update_slice(
-            out, block.astype(jnp.float32)[None], (place ^ flip, 0, 0, 0)
-        )
-    return out.reshape(rows // size, size, cols)
-
-
-def share_cols(grad):
-    size, depth = lax.axis_size("fsdp"), lax.axis_size("ctx")
-    rows, cols = grad.shape
-    part = rows // depth
-    width = cols // size
-    quarter = spread_sum(grad.reshape(1, depth, part, cols), "ctx")[0].astype(jnp.bfloat16)
-    me, place = lax.axis_index("fsdp"), lax.axis_index("ctx")
-    held = jnp.zeros((size, part, width), jnp.bfloat16)
-    for flip in range(size):
-        block = pick(quarter, me ^ flip, width, 1)
-        if flip:
-            block = partner(block, "fsdp", flip)
-        held = lax.dynamic_update_slice(held, block[None], (me ^ flip, 0, 0))
-    out = jnp.zeros((size, depth, part, width), jnp.float32)
-    for flip in range(depth):
-        block = partner(held, "ctx", flip) if flip else held
-        out = lax.dynamic_update_slice(
-            out, block.astype(jnp.float32)[:, None], (0, place ^ flip, 0, 0)
-        )
-    return out.reshape(size * rows, width)
-
-
-def all_sum(vector, axis):
-    total = vector
-    for flip in range(1, lax.axis_size(axis)):
-        total = total + partner(vector, axis, flip)
-    return total
+    side = lax.axis_index("ctx") >> 1
+    held = (kept.astype(f32) + partner(away, "ctx", 1).astype(f32)).astype(bf16)
+    held = after(held, *gate)
+    kept = lax.dynamic_index_in_dim(held, side, 0, keepdims=False)
+    away = lax.dynamic_index_in_dim(held, 1 - side, 0, keepdims=False)
+    return (kept.astype(f32) + partner(away, "ctx", 2).astype(f32)).astype(bf16)
+
+
+def spread(held):
+    far = partner(held, "ctx", 2)
+    return [held, partner(held, "ctx", 1), far, partner(far, "ctx", 1)]
+
+
+def after(tensor, *others):
+    return lax.optimization_barrier((tensor,) + others)[0]
 
 
 def plane_local(
@@ -602,10 +734,19 @@
     bf16 = jnp.bfloat16
     me, place, core = lax.axis_index("fsdp"), lax.axis_index("ctx"), lax.axis_index("tp")
     size = lax.axis_size("fsdp")
+    depth = lax.axis_size("ctx")
     count, model = tokens.shape[1:]
+    half_rows = count // 2
     rows = tokens[0].astype(f32)
     cot = cotangent[0]
-
+    levels = list(range(size.bit_length() - 1))
+
+    my_tokens = double_up(pick(tokens[0], core, half_rows), "fsdp", levels)
+    my_cot = double_up(pick(cot, core, half_rows).astype(bf16), "fsdp", levels[::-1])
+    width = joint_weight.shape[2] // size
+    joint_w = swap(
+        joint_weight.reshape(-1, 3, size, width).transpose(2, 0, 1, 3), "fsdp"
+    ).reshape(model, 3, width)
     small = jnp.concatenate(
         [
             attention_gain,
@@ -615,45 +756,48 @@
             output_bias,
             down_bias,
         ]
-    ).reshape(6, -1)
-    full_small = jnp.zeros((6, model), bf16)
-    for flip, block in enumerate(plane_gather(small)):
-        full_small = put(full_small, block, me ^ flip, 1)
-    params = full_small.astype(f32)
-    ids = jnp.concatenate([segment_ids, positions], 0)
-    ids_plane = plane_gather(ids)
-    pos_plane = jnp.concatenate([block[1] for block in ids_plane])
-    seg_plane = jnp.concatenate([block[0] for block in ids_plane])
-
-    plane_tokens = chip_gather(tokens[0])
-    width = joint_weight.shape[2] // size
-    joint_w = exchange(joint_weight, "fsdp", 2, 0)
-    cot_b = chip_gather(cot.astype(bf16))
-    output_w = exchange(output_weight, "fsdp", 0, 1)
-    up_w = exchange(up_weight, "fsdp", 1, 0)
-    down_w = exchange(down_weight, "fsdp", 0, 1)
-
-    normed, _ = normalize(plane_tokens.astype(f32))
-    first = (normed * params[0] + params[1]).astype(bf16)
-    second = (normed * params[2] + params[3]).astype(bf16)
+    ).astype(f32)
+    notes = jnp.concatenate([small, segment_ids[0].astype(f32), positions[0].astype(f32)])
+    packed = gather(
+        after(notes, joint_w),
+        ("fsdp", "ctx"),
+    ).reshape(size, depth, -1)
+    params = packed[:, 0, : small.size].reshape(size, 6, -1).transpose(1, 0, 2).reshape(6, model)
+    seg_seq = lax.dynamic_index_in_dim(packed, place, 0, keepdims=False)
+    seg_seq = seg_seq[:, small.size : small.size + count].reshape(-1)
+    pos_here = lax.dynamic_index_in_dim(packed, place, 1, keepdims=False)[:, small.size + count :]
+    pos_plane = jnp.concatenate(
+        [lax.dynamic_index_in_dim(pos_here, me ^ k, 0, keepdims=False) for k in range(size)]
+    )
+    output_w = swap(after(output_weight, packed).reshape(size, width, -1), "fsdp")
+    output_w = output_w.transpose(1, 0, 2).reshape(width, model)
+    first, second, normed = both_cores(norm_body, my_tokens, core, [params[:4]], 3)
+    (cot_b,) = both_cores(merge_body, my_cot, core, [], 1)
+    hidden = up_weight.shape[1] // size
+    up_send = up_weight.reshape(-1, size, hidden).transpose(1, 0, 2)
+    up_w = swap(after(up_send, output_w, first, cot_b), "fsdp")
+    up_w = up_w.reshape(model, hidden)
+    down_w = swap(after(down_weight, up_w).reshape(size, hidden, -1), "fsdp")
+    down_w = down_w.transpose(1, 0, 2).reshape(hidden, model)
+
 
     lane = jnp.arange(width, dtype=jnp.int32) % HD
     half = ROT // 2
     freq = jnp.where(
         lane < ROT, ROPE_BASE ** (-((lane % half).astype(f32) * 2.0 / ROT)), 0.0
     )
-    angle = pos_plane.astype(f32)[:, None] * freq[None, :]
+    angle = pos_plane[:, None] * freq[None, :]
     cosine = jnp.cos(angle)
     sine = jnp.sin(angle) * jnp.where(lane < half, -1.0, 1.0)[None, :]
     source = jnp.arange(width, dtype=jnp.int32)
     source = jnp.where(lane < half, source + half, jnp.where(lane < ROT, source - half, -1))
-    swap = (jnp.arange(width, dtype=jnp.int32)[:, None] == source[None, :]).astype(bf16)
+    turn = (jnp.arange(width, dtype=jnp.int32)[:, None] == source[None, :]).astype(bf16)
 
     joint_flat = joint_w.reshape(model, 3 * width)
     bias = joint_bias.astype(f32)
     joint = jnp.dot(first, joint_flat, preferred_element_type=f32) + bias.reshape(-1)[None]
-    swapped_w = jnp.einsum("dpe,ef->dpf", joint_w[:, :2], swap, preferred_element_type=bf16)
-    swapped_b = jnp.dot(joint_bias[:2], swap, preferred_element_type=f32)
+    swapped_w = jnp.einsum("dpe,ef->dpf", joint_w[:, :2], turn, preferred_element_type=bf16)
+    swapped_b = jnp.dot(joint_bias[:2], turn, preferred_element_type=f32)
     swapped = (
         jnp.dot(first, swapped_w.reshape(model, 2 * width), preferred_element_type=f32)
         + swapped_b.reshape(-1)[None]
@@ -661,31 +805,13 @@
     scale = HD ** (-0.5)
     queries = (joint[:, :width] * cosine + swapped[:, :width] * sine) * scale
     keys = joint[:, width : 2 * width] * cosine + swapped[:, width:] * sine
-    qkv = jnp.concatenate([queries, keys, joint[:, 2 * width :]], 1).astype(bf16)
-
-    def to_sequence(tensor):
-        out = jnp.zeros(tensor.shape, tensor.dtype)
-        for flip in range(size):
-            block = pick(tensor, me ^ place ^ flip, count)
-            if flip:
-                block = partner(block, "ctx", flip)
-            out = put(out, block, place ^ flip)
-        return out
-
-    def from_sequence(tensor):
-        out = jnp.zeros(tensor.shape, tensor.dtype)
-        for flip in range(size):
-            block = pick(tensor, place ^ flip, count)
-            if flip:
-                block = partner(block, "ctx", flip)
-            out = put(out, block, me ^ place ^ flip)
-        return out
-
-    seg_seq = to_sequence(seg_plane)
-    qkv_seq = to_sequence(qkv)
-    d_context = jnp.einsum("nd,wd->nw", cot_b, output_w, preferred_element_type=f32).astype(bf16)
-    dctx_seq = to_sequence(d_context)
-    ctx_seq, dq_seq, dkv_seq = attention(qkv_seq, dctx_seq, seg_seq)
+    d_context = jnp.einsum("nd,wd->nw", cot_b, output_w, preferred_element_type=f32)
+    sending = jnp.concatenate([queries, keys, joint[:, 2 * width :], d_context], 1).astype(bf16)
+    blocks = []
+    for flip in range(depth):
+        block = pick(sending, me ^ place ^ flip, count)
+        blocks.append(partner(block, "ctx", flip) if flip else block)
+    second, up_w = lax.optimization_barrier((second, up_w, sending))[:2]
 
     upper = jnp.dot(second, up_w, preferred_element_type=f32) + up_bias.astype(f32)[None]
     gelu, gelu_back = jax.vjp(lambda value: jax.nn.gelu(value, approximate=False), upper)
@@ -694,63 +820,112 @@
     d_upper = gelu_back(d_act)[0]
     d_upper_b = d_upper.astype(bf16)
     grad_up_b = jnp.sum(d_upper, 0)
-    grad_up_w = jnp.dot(second.T, d_upper_b, preferred_element_type=f32).astype(bf16)
+    moment_up = jnp.dot(normed.T, d_upper_b, preferred_element_type=f32)
+    d_upper_sum = jnp.sum(d_upper_b.astype(f32), 0)
+    grad_up_w = (
+        params[2][:, None] * moment_up + params[3][:, None] * d_upper_sum[None, :]
+    ).astype(bf16)
+    up_f32 = up_w.astype(f32)
+    gain_two_grad = jnp.sum(up_f32 * moment_up, 1)
+    shift_two_grad = jnp.sum(up_f32 * d_upper_sum[None, :], 1)
     grad_down_w = jnp.dot(activated.T, cot_b, preferred_element_type=f32).astype(bf16)
-    d_second = jnp.einsum("nf,df->nd", d_upper_b, up_w, preferred_element_type=f32)
-
-    context = from_sequence(ctx_seq)
-    mixed = jnp.dot(context, output_w, preferred_element_type=f32) + jnp.dot(
-        activated, down_w, preferred_element_type=f32
-    )
-    result = rows + chip_scatter(mixed, count) + params[4] + params[5]
+    part = model // size // depth
+    kept, away = pack(pack_wide, grad_up_w, grad_down_w, 2 * part, size, place)
+    held = (kept, away)
+    blocks = lax.optimization_barrier((tuple(blocks), kept, away))[0]
+    made = attention(blocks, seg_seq, place)
+    kept, away = held
+    held = swap(sum_slots(kept, away), "fsdp")
+    owned_up, owned_down = unpack(
+        unpack_wide,
+        spread(held),
+        (model // size, up_weight.shape[1]),
+        (part, up_weight.shape[1]),
+        (size, depth, 2 * part, 2 * width),
+        (size, 1, 2 * part, 2 * width),
+        place,
+    )
+    owned_down = owned_down.reshape(down_weight.shape)
+    gained = (up_f32 * params[2][:, None]).astype(bf16)
+    upstream_two = jnp.einsum("nf,df->nd", d_upper_b, gained, preferred_element_type=f32)
+    upstream_two = upstream_two.astype(bf16)
+    mixed_two = jnp.dot(activated, down_w, preferred_element_type=f32).astype(bf16)
+
+    back = jnp.zeros(sending.shape, bf16)
+    for flip in range(depth):
+        block = partner(made[flip], "ctx", flip) if flip else made[flip]
+        back = lax.dynamic_update_slice_in_dim(back, block, (me ^ place ^ flip) * count, 0)
+    context = back[:, :width]
+    d_qk = back[:, width : 3 * width]
     grad_output_w = jnp.dot(context.T, cot_b, preferred_element_type=f32).astype(bf16)
 
-    dq = from_sequence(dq_seq)
-    dkv = from_sequence(dkv_seq)
-    dq_swapped = jnp.dot(dq, swap, preferred_element_type=f32)
-    dk_swapped = jnp.dot(dkv[:, :width], swap, preferred_element_type=f32)
+    d_swapped = jnp.einsum(
+        "npe,ef->npf", d_qk.reshape(-1, 2, width), turn, preferred_element_type=f32
+    ).reshape(-1, 2 * width)
+    cosines = jnp.concatenate([cosine, cosine], 1)
+    sines = jnp.concatenate([sine, sine], 1)
     d_joint = jnp.concatenate(
-        [
-            dq.astype(f32) * cosine - dq_swapped * sine,
-            dkv[:, :width].astype(f32) * cosine - dk_swapped * sine,
-            dkv[:, width:].astype(f32),
-        ],
-        1,
+        [d_qk.astype(f32) * cosines - d_swapped * sines, back[:, 3 * width :].astype(f32)], 1
     )
     d_joint_b = d_joint.astype(bf16)
     grad_joint_b = jnp.sum(d_joint, 0)
-    grad_joint_w = jnp.dot(first.T, d_joint_b, preferred_element_type=f32).astype(bf16)
-    d_first = jnp.einsum("ne,de->nd", d_joint_b, joint_flat, preferred_element_type=f32)
-    upstream = chip_scatter(d_first * params[0] + d_second * params[2], count)
-
-    normed_here, rstd = normalize(rows)
-    tokens_grad = cot + rstd * (
-        upstream
-        - jnp.mean(upstream, -1, keepdims=True)
-        - normed_here * jnp.mean(upstream * normed_here, -1, keepdims=True)
+    moment_joint = jnp.dot(normed.T, d_joint_b, preferred_element_type=f32)
+    d_joint_sum = jnp.sum(d_joint_b.astype(f32), 0)
+    grad_joint_w = (
+        params[0][:, None] * moment_joint + params[1][:, None] * d_joint_sum[None, :]
+    ).astype(bf16)
+    kept, away = pack(pack_heads, grad_joint_w, grad_output_w, part, size, place)
+    context, d_joint_b = lax.optimization_barrier((context, d_joint_b, kept, away))[:2]
+    mixed = jnp.dot(context, output_w, preferred_element_type=f32) + mixed_two.astype(f32)
+    sending_result = chip_start(mixed.astype(bf16), size)
+    joint_f32 = joint_flat.astype(f32)
+    gained = (joint_f32 * params[0][:, None]).astype(bf16)
+    upstream = jnp.einsum("ne,de->nd", d_joint_b, gained, preferred_element_type=f32)
+    sending_up = chip_start((upstream + upstream_two.astype(f32)).astype(bf16), size)
+    held = sum_slots(kept, away, (sending_result, sending_up))
+    held = swap(held, "fsdp")
+    owned_joint, owned_output = unpack(
+        unpack_heads,
+        spread(held),
+        (3, model // size, joint_weight.shape[2]),
+        (3, part, joint_weight.shape[2]),
+        (size, depth, part // 2, 2 * width),
+        (size, 1, part // 2, 2 * width),
+        place,
+    )
+    owned_joint = owned_joint.transpose(1, 0, 2)
+    owned_output = owned_output.reshape(output_weight.shape)
+
+    my_rows = pick(rows, core, half_rows)
+    result = chip_join(my_rows + chip_finish(sending_result) + params[4] + params[5])
+    normed_here, rstd = normalize(my_rows)
+    upstream = chip_finish(sending_up)
+    tokens_grad = chip_join(
+        pick(cot, core, half_rows)
+        + rstd
+        * (
+            upstream
+            - jnp.mean(upstream, -1, keepdims=True)
+            - normed_here * jnp.mean(upstream * normed_here, -1, keepdims=True)
+        )
     )
     stats = jnp.stack(
         [
-            jnp.sum(d_first * normed, 0),
-            jnp.sum(d_first, 0),
-            jnp.sum(d_second * normed, 0),
-            jnp.sum(d_second, 0),
-            jnp.sum(pick(cot, core, count // 2), 0),
+            jnp.sum(joint_f32 * moment_joint, 1),
+            jnp.sum(joint_f32 * d_joint_sum[None, :], 1),
+            gain_two_grad,
+            shift_two_grad,
+            jnp.sum(pick(cot, core, half_rows), 0),
         ]
     )
-    stats = spread_sum(stats.reshape(5, size, -1), "fsdp")
-    stats = all_sum(stats, "tp")
+    stats = jnp.sum(swap(stats.reshape(5, size, -1).transpose(1, 0, 2), "fsdp"), 0)
     packed = jnp.concatenate([stats.reshape(-1), grad_joint_b, grad_up_b])
-    packed = all_sum(packed, "ctx")
-    owned = packed[: stats.size].reshape(stats.shape)
-    owned_jbias = packed[stats.size : stats.size + 3 * width].reshape(3, width)
-    owned_upbias = packed[stats.size + 3 * width :]
-
-    owned_up = share_rows(grad_up_w).reshape(up_weight.shape)
-    owned_down = share_cols(grad_down_w)
-    owned_output = share_cols(grad_output_w)
-    owned_joint = share_rows(grad_joint_w).reshape(model // size, size, 3, width)
-    owned_joint = owned_joint.transpose(0, 2, 1, 3).reshape(joint_weight.shape)
+    packed = gather(packed, ("ctx", "tp")).reshape(depth, 2, -1)
+    owned = jnp.sum(packed[:, :, : stats.size], (0, 1)).reshape(stats.shape)
+    biases = jnp.sum(packed[:, :, stats.size :], 0)
+    biases = lax.dynamic_index_in_dim(biases, core, 0, keepdims=False)
+    owned_jbias = biases[: 3 * width].reshape(3, width)
+    owned_upbias = biases[3 * width :]
     return (
         result[None],
         tokens_grad[None],
@@ -769,14 +944,15 @@
     )
 
 
-def splits_plane(mesh, tokens, joint_weight):
+def splits_plane(mesh, tokens, joint_weight, up_weight):
     size, depth, cores = mesh.shape["fsdp"], mesh.shape["ctx"], mesh.shape["tp"]
     width = joint_weight.shape[2] // (size * cores)
     return (
-        size == depth == tokens.shape[0]
-        and size & (size - 1) == 0
+        size == depth == tokens.shape[0] == 4
         and cores == 2
         and width % 128 == 0
+        and tokens.shape[2] == 2 * size * width
+        and up_weight.shape[1] == 4 * size * cores * width
         and tokens.shape[1] // depth % 256 == 0
     )
 
@@ -818,7 +994,7 @@
     )
 
     def run(*args):
-        body = plane_local if splits_plane(mesh, args[0], args[7]) else gathered_local
+        body = plane_local if splits_plane(mesh, args[0], args[7], args[11]) else gathered_local
         return jax.shard_map(
             body, mesh=mesh, in_specs=placed, out_specs=given, check_vma=False
         )(*args)

time: 542 us -> 442 us (0.82)
  the two profiles are of different devices: /device:TPU:8 before, /device:TPU:0 now
where the time goes in v2:
time: 442 us; the launch traced here: 435 us
  waiting for transfers between devices  151 us (34%)
  starting transfers between devices  80 us (18%)
  Pallas kernels  61 us (14%)
  matrix products  56.2 us (13%)
  local copies, waits for them, and re-layouts  45.3 us (10%)
  other arithmetic  39.6 us (9%)
    ppermute x32, waiting for transfers between devices, partner(): return lax.ppermute(tensor, axis, [(s, s ^ flip) for s in range(size)])  123 us
    pallas_call x1, Pallas kernels, attention(): pl.pallas_call(lambda *refs: attention_body(heads, flips, *refs), grid_sp...  46.7 us
    ppermute x32, starting transfers between devices, partner(): return lax.ppermute(tensor, axis, [(s, s ^ flip) for s in range(size)])  44.1 us
    all_to_all x9, starting transfers between devices, swap(): return lax.all_to_all(tensor, axis, 0, 0)  36 us
    all_to_all x9, waiting for transfers between devices, swap(): return lax.all_to_all(tensor, axis, 0, 0)  27.3 us
    unnamed x112, local copies, waits for them, and re-layouts  18.2 us
    dot_general x1, matrix products, plane_local(): jnp.dot(second, up_w, preferred_element_type=f32)  14.3 us
    dot_general x1, matrix products, plane_local(): d_act = jnp.einsum('nd,fd->nf', cot_b, down_w, preferred_element_type=f32)  9.09 us
  transfers between devices with their start and end apart: 41, of which 19 were waited for; matrix products, arithmetic and copies ran while one was open for 28% of the time, Pallas kernels for 13%

profile of v2, /device:TPU:0, one launch (start us, length us, event | category | flops | bytes accessed | tf_op | source)
XLA Modules:
  0.0 435.0 jit_solution(4553719365943848626)
XLA Ops:
  7.8 9.0 %collective-permute-done = bf16[1,256,1024]{2,1,0:T(8,128)(2,1)S(1)} collective-permute-done((bf16[1,256,1024]{2,1,0:T(8,128)(2,1)S(1)}, bf16[1,256,1024]{2,1,0:T(8,128)(2,1)S(1)}, u32[]{:S(2)}, u32[]{:S(2)}) %collective-permute-start) | collective-permute-done | bytes 524320 | tf_op jit(solution)/shard_map/ppermute | solution.py:517
  25.3 3.5 all-to-all-start
  30.4 13.8 %collective-permute-done.1 = bf16[2,1,256,1024]{3,2,1,0:T(8,128)(2,1)} collective-permute-done((bf16[2,1,256,1024]{3,2,1,0:T(8,128)(2,1)S(1)}, bf16[2,1,256,1024]{3,2,1,0:T(8,128)(2,1)}, u32[]{:S(2)}, u32[]{:S(2)}) %collective-permute-start.1) | collective-permute-done | bytes 1048608 | tf_op jit(solution)/shard_map/ppermute | solution.py:517
  56.9 6.8 %all-to-all-start.1 = ((f32[16,1,2560]{2,1,0:T(1,128)}), f32[16,1,2560]{2,1,0:T(1,128)S(1)}, u32[]{:S(2)}, u32[]{:S(2)}) async-start(f32[16,1,2560]{2,1,0:T(1,128)} %broadcast_in_dim.27), calls=%async_computation.1 | async-start | bytes 327680 | tf_op jit(solution)/shard_map/all_to_all | solution.py:525
  72.1 3.4 all-to-all-start.2
  76.1 4.8 %all-to-all-done.2 = bf16[4,128,256]{2,1,0:T(8,128)(2,1)S(1)} async-done(((bf16[4,128,256]{2,1,0:T(8,128)(2,1)}), bf16[4,128,256]{2,1,0:T(8,128)(2,1)S(1)}, u32[]{:S(2)}, u32[]{:S(2)}) %all-to-all-start.2) | async-done | bytes 262176 | tf_op jit(solution)/shard_map/all_to_all | solution.py:525
  87.7 5.1 %norm_body.1 = (bf16[4,2,256,1024]{3,2,1,0:T(8,128)(2,1)S(1)}, bf16[4,2,256,1024]{3,2,1,0:T(8,128)(2,1)S(1)}, bf16[4,2,256,1024]{3,2,1,0:T(8,128)(2,1)S(1)}) custom-call(s32[1]{0:T(128)} %bitcast.2.core_ref, bf16[4,256,1024]{2,1,0:T(8,128)(2,1)S(1)} %bitcast.226, bf16[4,256,1024]{2,1,0:T(8,128)(2,1)} %collective-permute-done.2.other_ref, f32[4,1024]{1,0:T(4,128)S(1)} %bitcast.232), custom_call_target="tpu_custom_call" | custom-call | flops 20971520 | bytes 16777216 | tf_op jit(solution)/shard_map/norm_body/pallas_call | solution.py:495
  98.8 4.0 all-to-all-start.3
  102.8 5.0 %convolution_add_fusion = f32[2048,384]{1,0:T(8,128)S(1)} fusion(bf16[2048,1024]{1,0:T(8,128)(2,1)} %bitcast.238, bf16[1024,384]{0,1:T(8,128)(2,1)} %bitcast.249, f32[384]{0:T(512)S(1)} %bitcast_convert_fusion), kind=kOutput, calls=%fused_computation.29 | convolution fusion | flops 1611399168 | bytes 8128000 | tf_op jit(solution)/shard_map/dot_general | solution.py:798
  109.2 5.7 %fusion.39 = (bf16[2048,128]{1,0:T(8,128)(2,1)S(1)}, bf16[2048,128]{1,0:T(8,128)(2,1)S(1)}, f32[2048,128]{1,0:T(8,128)}, f32[2048,128]{1,0:T(8,128)}) fusion(f32[2048,256]{1,0:T(8,128)S(1)} %convolution_add_fusion.1, f32[2048,384]{1,0:T(8,128)S(1)} %convolution_add_fusion, f32[128]{0:T(128)S(1)} %get-tuple-element.129, f32[128]{0:T(128)S(1)} %get-tuple-element.130, ...), kind=kLoop, calls=%fused_computation.89 | loop fusion | flops 2883584 | bytes 7349248 | tf_op jit(solution)/shard_map/convert.7 | solution.py:998
  122.4 4.3 all-to-all-start.4
  126.7 14.3 %multiply_convert_fusion = (bf16[2048,512]{1,0:T(8,128)(2,1)S(1)}, f32[2048,512]{1,0:T(8,128)}, f32[2048,512]{1,0:T(8,128)}) fusion(f32[512]{0:T(512)S(1)} %convert_element_type.217, bf16[2048,1024]{1,0:T(8,128)(2,1)} %bitcast.237, bf16[1024,512]{1,0:T(8,128)(2,1)S(1)} %bitcast.256), kind=kOutput, calls=%fused_computation.8 | convolution fusion | flops 2216689664 | bytes 15730688 | tf_op jit(solution)/shard_map/dot_general | solution.py:816
  146.0 9.1 %fusion.71 = (f32[512]{0:T(512)S(1)}, f32[512]{0:T(512)S(1)}, bf16[2048,512]{1,0:T(8,128)(2,1)S(1)}) fusion(f32[2048,512]{1,0:T(8,128)} %get-tuple-element.81, f32[2048,512]{1,0:T(8,128)} %get-tuple-element.128, f32[512]{0:T(512)S(1)} %convert_element_type.217, bf16[2048,1024]{1,0:T(8,128)(2,1)} %bitcast.221, bf16[512,1024]{0,1:T(8,128)(2,1)} %bitcast.259), kind=kOutput, calls=%fused_computation.184 | convolution fusion | flops 2167405568 | bytes 15734784 | tf_op jit(solution)/shard_map/nd,fd->nf/dot_general | solution.py:819
  159.7 4.5 %fusion.30 = bf16[2048,1024]{1,0:T(8,128)(2,1)} fusion(bf16[1024,512]{1,0:T(8,128)(2,1)S(1)} %bitcast.258, f32[1024]{0:T(1024)S(1)} %bitcast.283, bf16[2048,512]{1,0:T(8,128)(2,1)S(1)} %get-tuple-element.82), kind=kOutput, calls=%fused_computation.76 | convolution fusion | flops 2149056512 | bytes 7344128 | tf_op jit(solution)/shard_map/nf,df->nd/dot_general | solution.py:850
  164.3 46.7 %attention.1 = (bf16[512,512]{1,0:T(8,128)(2,1)S(1)}, bf16[512,512]{1,0:T(8,128)(2,1)S(1)}, bf16[512,512]{1,0:T(8,128)(2,1)S(1)}, bf16[512,512]{1,0:T(8,128)(2,1)S(1)}) custom-call(s32[1]{0:T(128)} %bitcast.1.place_ref.refs_0_, bf16[512,512]{1,0:T(8,128)(2,1)S(1)} %copy-done.4, bf16[512,512]{1,0:T(8,128)(2,1)} %collective-permute-done.6.refs_2_, ...), custom_call_target="tpu_custom_call" | custom-call | flops 9059696640 | bytes 4194304 | tf_op jit(solution)/shard_map/attention/pallas_call | solution.py:442
  215.4 4.4 %fusion.76 = bf16[2048,1024]{1,0:T(8,128)(2,1)} fusion(bf16[2048,512]{1,0:T(8,128)(2,1)S(1)} %copy-done.49, bf16[512,1024]{0,1:T(8,128)(2,1)S(1)} %bitcast.260), kind=kOutput, calls=%fused_computation.187 | convolution fusion | flops 2147483648 | bytes 7340032 | tf_op jit(solution)/shard_map/dot_general | solution.py:852
  220.0 8.3 %collective-permute-done.9 = bf16[512,512]{1,0:T(8,128)(2,1)S(1)} collective-permute-done((bf16[512,512]{1,0:T(8,128)(2,1)S(1)}, bf16[512,512]{1,0:T(8,128)(2,1)S(1)}, u32[]{:S(2)}, u32[]{:S(2)}) %collective-permute-start.9) | collective-permute-done | bytes 524320 | tf_op jit(solution)/shard_map/ppermute | solution.py:517
  228.4 21.8 %collective-permute-done.10 = bf16[512,512]{1,0:T(8,128)(2,1)S(1)} collective-permute-done((bf16[512,512]{1,0:T(8,128)(2,1)S(1)}, bf16[512,512]{1,0:T(8,128)(2,1)S(1)}, u32[]{:S(2)}, u32[]{:S(2)}) %collective-permute-start.10) | collective-permute-done | bytes 524320 | tf_op jit(solution)/shard_map/ppermute | solution.py:517
  277.7 7.6 %collective-permute-start.28 = (bf16[4,128,512]{2,1,0:T(8,128)(2,1)}, bf16[4,128,512]{2,1,0:T(8,128)(2,1)S(1)}, u32[]{:S(2)}, u32[]{:S(2)}) collective-permute-start(bf16[4,128,512]{2,1,0:T(8,128)(2,1)} %dynamic-slice_bitcast_fusion.2), channel_id=1, source_target_pairs={{0,4},{2,6},{4,0},{6,2},{1,5},{3,7},{5,1},{7,3},{8,12},{10,14},{12... | collective-permute-start | bytes 1572872 | tf_op jit(solution)/shard_map/ppermute | solution.py:517
  286.9 21.7 %collective-permute-done.28 = bf16[4,128,512]{2,1,0:T(8,128)(2,1)S(1)} collective-permute-done((bf16[4,128,512]{2,1,0:T(8,128)(2,1)}, bf16[4,128,512]{2,1,0:T(8,128)(2,1)S(1)}, u32[]{:S(2)}, u32[]{:S(2)}) %collective-permute-start.28) | collective-permute-done | bytes 524320 | tf_op jit(solution)/shard_map/ppermute | solution.py:517
  310.6 3.9 all-to-all-start.8
  315.6 6.5 %all-to-all-done.8.refs_0_ = bf16[4,128,512]{2,1,0:T(8,128)(2,1)S(1)} async-done(((bf16[4,128,512]{2,1,0:T(8,128)(2,1)}), bf16[4,128,512]{2,1,0:T(8,128)(2,1)S(1)}, u32[]{:S(2)}, u32[]{:S(2)}) %all-to-all-start.8) | async-done | bytes 524320 | tf_op jit(solution)/shard_map/all_to_all | solution.py:525
  325.4 3.4 fusion.1
  338.1 5.8 %collective-permute-done.18 = bf16[256,1024]{1,0:T(8,128)(2,1)S(1)} collective-permute-done((bf16[256,1024]{1,0:T(8,128)(2,1)S(1)}, bf16[256,1024]{1,0:T(8,128)(2,1)S(1)}, u32[]{:S(2)}, u32[]{:S(2)}) %collective-permute-start.18) | collective-permute-done | bytes 524320 | tf_op jit(solution)/shard_map/ppermute | solution.py:517
  345.8 8.7 %collective-permute-done.19 = bf16[256,1024]{1,0:T(8,128)(2,1)S(1)} collective-permute-done((bf16[256,1024]{1,0:T(8,128)(2,1)S(1)}, bf16[256,1024]{1,0:T(8,128)(2,1)S(1)}, u32[]{:S(2)}, u32[]{:S(2)}) %collective-permute-start.19) | collective-permute-done | bytes 524320 | tf_op jit(solution)/shard_map/ppermute | solution.py:517
  358.5 7.9 %collective-permute-done.13 = bf16[256,1024]{1,0:T(8,128)(2,1)S(1)} collective-permute-done((bf16[256,1024]{1,0:T(8,128)(2,1)S(1)}, bf16[256,1024]{1,0:T(8,128)(2,1)S(1)}, u32[]{:S(2)}, u32[]{:S(2)}) %collective-permute-start.13) | collective-permute-done | bytes 524320 | tf_op jit(solution)/shard_map/ppermute | solution.py:517
  366.4 9.7 %collective-permute-done.14 = bf16[256,1024]{1,0:T(8,128)(2,1)S(1)} collective-permute-done((bf16[256,1024]{1,0:T(8,128)(2,1)S(1)}, bf16[256,1024]{1,0:T(8,128)(2,1)S(1)}, u32[]{:S(2)}, u32[]{:S(2)}) %collective-permute-start.14) | collective-permute-done | bytes 524320 | tf_op jit(solution)/shard_map/ppermute | solution.py:517
  378.9 3.4 all-to-all-start.7
  383.0 5.5 %all-to-all-done.7.refs_0_ = bf16[4,64,512]{2,1,0:T(8,128)(2,1)S(1)} async-done(((bf16[4,64,512]{2,1,0:T(8,128)(2,1)}), bf16[4,64,512]{2,1,0:T(8,128)(2,1)S(1)}, u32[]{:S(2)}, u32[]{:S(2)}) %all-to-all-start.7) | async-done | bytes 262176 | tf_op jit(solution)/shard_map/all_to_all | solution.py:525
  397.1 8.6 %all-to-all-done.6 = f32[8,1,2176]{2,1,0:T(1,128)S(1)} async-done(((f32[8,1,2176]{2,1,0:T(1,128)}), f32[8,1,2176]{2,1,0:T(1,128)S(1)}, u32[]{:S(2)}, u32[]{:S(2)}) %all-to-all-start.6) | async-done | bytes 69664 | tf_op jit(solution)/shard_map/all_to_all | solution.py:525
  409.9 5.2 %collective-permute-done.31.refs_3_ = bf16[4,128,512]{2,1,0:T(8,128)(2,1)S(1)} collective-permute-done((bf16[4,128,512]{2,1,0:T(8,128)(2,1)S(1)}, bf16[4,128,512]{2,1,0:T(8,128)(2,1)S(1)}, u32[]{:S(2)}, u32[]{:S(2)}) %collective-permute-start.31) | collective-permute-done | bytes 524320 | tf_op jit(solution)/shard_map/ppermute | solution.py:517
  420.7 5.2 %collective-permute-done.26.refs_3_ = bf16[4,64,512]{2,1,0:T(8,128)(2,1)S(1)} collective-permute-done((bf16[4,64,512]{2,1,0:T(8,128)(2,1)S(1)}, bf16[4,64,512]{2,1,0:T(8,128)(2,1)S(1)}, u32[]{:S(2)}, u32[]{:S(2)}) %collective-permute-start.26) | collective-permute-done | bytes 262176 | tf_op jit(solution)/shard_map/ppermute | solution.py:517
  (273 shorter events, 155.3 us)
Async XLA Ops:
  17.9 26.2 %collective-permute-start.1 = (bf16[2,1,256,1024]{3,2,1,0:T(8,128)(2,1)S(1)}, bf16[2,1,256,1024]{3,2,1,0:T(8,128)(2,1)}, u32[]{:S(2)}, u32[]{:S(2)}) collective-permute-start(bf16[2,1,256,1024]{3,2,1,0:T(8,128)(2,1)S(1)} %get-tuple-element.106), channel_id=1, source_target_pairs={{0,16},{8,24},{16,0},{24,8},{1,17},{9,25},{17,1},{25,9},{2,18},{10... | collective-permute-start | bytes 3145736 | tf_op jit(solution)/shard_map/ppermute | solution.py:517
  22.5 26.4 %collective-permute-start.4 = (bf16[2,1,256,1024]{3,2,1,0:T(8,128)(2,1)}, bf16[2,1,256,1024]{3,2,1,0:T(8,128)(2,1)}, u32[]{:S(2)}, u32[]{:S(2)}) collective-permute-start(bf16[2,1,256,1024]{3,2,1,0:T(8,128)(2,1)} %get-tuple-element.108), channel_id=1, source_target_pairs={{0,8},{8,0},{16,24},{24,16},{1,9},{9,1},{17,25},{25,17},{2,10},{10... | collective-permute-start | bytes 3145736 | tf_op jit(solution)/shard_map/ppermute | solution.py:517
  25.3 29.7 %all-to-all-start = ((bf16[4,256,3,128]{1,3,2,0:T(8,128)(2,1)}), bf16[4,256,3,128]{1,3,2,0:T(8,128)(2,1)S(1)}, u32[]{:S(2)}, u32[]{:S(2)}) async-start(bf16[4,256,3,128]{1,3,2,0:T(8,128)(2,1)} %copy.138), calls=%async_computation | async-start | bytes 1572864 | tf_op jit(solution)/shard_map/all_to_all | solution.py:525
  45.8 41.9 %collective-permute-start.2 = (bf16[4,256,1024]{2,1,0:T(8,128)(2,1)S(1)}, bf16[4,256,1024]{2,1,0:T(8,128)(2,1)}, u32[]{:S(2)}, u32[]{:S(2)}) collective-permute-start(bf16[4,256,1024]{2,1,0:T(8,128)(2,1)S(1)} %bitcast.225), channel_id=1, source_target_pairs={{0,1},{1,0},{2,3},{3,2},{4,5},{5,4},{6,7},{7,6},{8,9},{9,8},{10,11... | collective-permute-start | bytes 6291464 | tf_op jit(solution)/shard_map/ppermute | solution.py:517
  52.2 30.5 %collective-permute-start.5 = (bf16[4,256,1024]{2,1,0:T(8,128)(2,1)}, bf16[4,256,1024]{2,1,0:T(8,128)(2,1)}, u32[]{:S(2)}, u32[]{:S(2)}) collective-permute-start(bf16[4,256,1024]{2,1,0:T(8,128)(2,1)} %bitcast.32.mine_ref), channel_id=1, source_target_pairs={{0,1},{1,0},{2,3},{3,2},{4,5},{5,4},{6,7},{7,6},{8,9},{9,8},{10,11... | collective-permute-start | bytes 6291464 | tf_op jit(solution)/shard_map/ppermute | solution.py:517
  98.8 23.5 %all-to-all-start.3 = ((bf16[4,256,512]{2,1,0:T(8,128)(2,1)}), bf16[4,256,512]{2,1,0:T(8,128)(2,1)S(1)}, u32[]{:S(2)}, u32[]{:S(2)}) async-start(bf16[4,256,512]{2,1,0:T(8,128)(2,1)} %bitcast.246), calls=%async_computation.3 | async-start | bytes 2097152 | tf_op jit(solution)/shard_map/all_to_all | solution.py:525
  118.0 46.3 %collective-permute-start.6 = (bf16[512,512]{1,0:T(8,128)(2,1)}, bf16[512,512]{1,0:T(8,128)(2,1)}, u32[]{:S(2)}, u32[]{:S(2)}) collective-permute-start(bf16[512,512]{1,0:T(8,128)(2,1)} %get-tuple-element.101), channel_id=1, source_target_pairs={{0,2},{2,0},{4,6},{6,4},{1,3},{3,1},{5,7},{7,5},{8,10},{10,8},{12,... | collective-permute-start | bytes 1572872 | tf_op jit(solution)/shard_map/ppermute | solution.py:517
  119.3 45.0 %collective-permute-start.7 = (bf16[512,512]{1,0:T(8,128)(2,1)}, bf16[512,512]{1,0:T(8,128)(2,1)}, u32[]{:S(2)}, u32[]{:S(2)}) collective-permute-start(bf16[512,512]{1,0:T(8,128)(2,1)} %get-tuple-element.100), channel_id=1, source_target_pairs={{0,4},{2,6},{4,0},{6,2},{1,5},{3,7},{5,1},{7,3},{8,12},{10,14},{12... | collective-permute-start | bytes 1572872 | tf_op jit(solution)/shard_map/ppermute | solution.py:517
  120.9 43.4 %collective-permute-start.8 = (bf16[512,512]{1,0:T(8,128)(2,1)}, bf16[512,512]{1,0:T(8,128)(2,1)}, u32[]{:S(2)}, u32[]{:S(2)}) collective-permute-start(bf16[512,512]{1,0:T(8,128)(2,1)} %get-tuple-element.99), channel_id=1, source_target_pairs={{0,6},{2,4},{4,2},{6,0},{1,7},{3,5},{5,3},{7,1},{8,14},{10,12},{12... | collective-permute-start | bytes 1572872 | tf_op jit(solution)/shard_map/ppermute | solution.py:517
  122.4 22.3 %all-to-all-start.4 = ((bf16[4,512,256]{2,1,0:T(8,128)(2,1)}), bf16[4,512,256]{2,1,0:T(8,128)(2,1)S(1)}, u32[]{:S(2)}, u32[]{:S(2)}) async-start(bf16[4,512,256]{2,1,0:T(8,128)(2,1)} %bitcast.42), calls=%async_computation.4 | async-start | bytes 2097152 | tf_op jit(solution)/shard_map/all_to_all | solution.py:525
  159.2 115.3 %collective-permute-start.27 = (bf16[2,4,128,512]{3,2,1,0:T(8,128)(2,1)}, bf16[2,4,128,512]{3,2,1,0:T(8,128)(2,1)}, u32[]{:S(2)}, u32[]{:S(2)}) collective-permute-start(bf16[2,4,128,512]{3,2,1,0:T(8,128)(2,1)} %get-tuple-element.52), channel_id=1, source_target_pairs={{0,2},{2,0},{4,6},{6,4},{1,3},{3,1},{5,7},{7,5},{8,10},{10,8},{12,... | collective-permute-start | bytes 3145736 | tf_op jit(solution)/shard_map/ppermute | solution.py:517
  211.0 17.3 %collective-permute-start.9 = (bf16[512,512]{1,0:T(8,128)(2,1)S(1)}, bf16[512,512]{1,0:T(8,128)(2,1)S(1)}, u32[]{:S(2)}, u32[]{:S(2)}) collective-permute-start(bf16[512,512]{1,0:T(8,128)(2,1)S(1)} %get-tuple-element.58), channel_id=1, source_target_pairs={{0,2},{2,0},{4,6},{6,4},{1,3},{3,1},{5,7},{7,5},{8,10},{10,8},{12,... | collective-permute-start | bytes 1572872 | tf_op jit(solution)/shard_map/ppermute | solution.py:517
  212.6 37.6 %collective-permute-start.10 = (bf16[512,512]{1,0:T(8,128)(2,1)S(1)}, bf16[512,512]{1,0:T(8,128)(2,1)S(1)}, u32[]{:S(2)}, u32[]{:S(2)}) collective-permute-start(bf16[512,512]{1,0:T(8,128)(2,1)S(1)} %get-tuple-element.59), channel_id=1, source_target_pairs={{0,4},{2,6},{4,0},{6,2},{1,5},{3,7},{5,1},{7,3},{8,12},{10,14},{12... | collective-permute-start | bytes 1572872 | tf_op jit(solution)/shard_map/ppermute | solution.py:517
  213.6 36.7 %collective-permute-start.11 = (bf16[512,512]{1,0:T(8,128)(2,1)S(1)}, bf16[512,512]{1,0:T(8,128)(2,1)S(1)}, u32[]{:S(2)}, u32[]{:S(2)}) collective-permute-start(bf16[512,512]{1,0:T(8,128)(2,1)S(1)} %get-tuple-element.60), channel_id=1, source_target_pairs={{0,6},{2,4},{4,2},{6,0},{1,7},{3,5},{5,3},{7,1},{8,14},{10,12},{12... | collective-permute-start | bytes 1572872 | tf_op jit(solution)/shard_map/ppermute | solution.py:517
  270.4 55.0 %collective-permute-start.17 = (bf16[4,256,1024]{2,1,0:T(8,128)(2,1)}, bf16[4,256,1024]{2,1,0:T(8,128)(2,1)}, u32[]{:S(2)}, u32[]{:S(2)}) collective-permute-start(bf16[4,256,1024]{2,1,0:T(8,128)(2,1)} %dynamic-slice_bitcast_fusion), channel_id=1, source_target_pairs={{0,1},{1,0},{2,3},{3,2},{4,5},{5,4},{6,7},{7,6},{8,9},{9,8},{10,11... | collective-permute-start | bytes 6291464 | tf_op jit(solution)/shard_map/ppermute | solution.py:517
  274.5 58.0 %collective-permute-start.12 = (bf16[4,256,1024]{2,1,0:T(8,128)(2,1)}, bf16[4,256,1024]{2,1,0:T(8,128)(2,1)}, u32[]{:S(2)}, u32[]{:S(2)}) collective-permute-start(bf16[4,256,1024]{2,1,0:T(8,128)(2,1)} %dynamic-slice_bitcast_fusion.1), channel_id=1, source_target_pairs={{0,1},{1,0},{2,3},{3,2},{4,5},{5,4},{6,7},{7,6},{8,9},{9,8},{10,11... | collective-permute-start | bytes 6291464 | tf_op jit(solution)/shard_map/ppermute | solution.py:517
  277.7 30.9 %collective-permute-start.28 = (bf16[4,128,512]{2,1,0:T(8,128)(2,1)}, bf16[4,128,512]{2,1,0:T(8,128)(2,1)S(1)}, u32[]{:S(2)}, u32[]{:S(2)}) collective-permute-start(bf16[4,128,512]{2,1,0:T(8,128)(2,1)} %dynamic-slice_bitcast_fusion.2), channel_id=1, source_target_pairs={{0,4},{2,6},{4,0},{6,2},{1,5},{3,7},{5,1},{7,3},{8,12},{10,14},{12... | collective-permute-start | bytes 1572872 | tf_op jit(solution)/shard_map/ppermute | solution.py:517
  285.5 29.9 %collective-permute-start.22 = (bf16[2,4,64,512]{3,2,1,0:T(8,128)(2,1)S(1)}, bf16[2,4,64,512]{3,2,1,0:T(8,128)(2,1)S(1)}, u32[]{:S(2)}, u32[]{:S(2)}) collective-permute-start(bf16[2,4,64,512]{3,2,1,0:T(8,128)(2,1)S(1)} %get-tuple-element.62), channel_id=1, source_target_pairs={{0,2},{2,0},{4,6},{6,4},{1,3},{3,1},{5,7},{7,5},{8,10},{10,8},{12,... | collective-permute-start | bytes 1572872 | tf_op jit(solution)/shard_map/ppermute | solution.py:517
  322.0 56.9 %all-to-all-start.5 = ((f32[4,5,256]{2,1,0:T(8,128)}), f32[4,5,256]{2,1,0:T(8,128)S(1)}, u32[]{:S(2)}, u32[]{:S(2)}) async-start(f32[4,5,256]{2,1,0:T(8,128)} %bitcast.78), calls=%async_computation.5 | async-start | bytes 65536 | tf_op jit(solution)/shard_map/all_to_all | solution.py:525
  325.3 70.1 %collective-permute-start.30 = (bf16[4,128,512]{2,1,0:T(8,128)(2,1)S(1)}, bf16[4,128,512]{2,1,0:T(8,128)(2,1)S(1)}, u32[]{:S(2)}, u32[]{:S(2)}) collective-permute-start(bf16[4,128,512]{2,1,0:T(8,128)(2,1)S(1)} %all-to-all-done.8.refs_0_), channel_id=1, source_target_pairs={{0,4},{2,6},{4,0},{6,2},{1,5},{3,7},{5,1},{7,3},{8,12},{10,14},{12... | collective-permute-start | bytes 1572872 | tf_op jit(solution)/shard_map/ppermute | solution.py:517
  330.9 23.5 %collective-permute-start.19 = (bf16[256,1024]{1,0:T(8,128)(2,1)S(1)}, bf16[256,1024]{1,0:T(8,128)(2,1)S(1)}, u32[]{:S(2)}, u32[]{:S(2)}) collective-permute-start(bf16[256,1024]{1,0:T(8,128)(2,1)S(1)} %get-tuple-element.91), channel_id=1, source_target_pairs={{0,16},{8,24},{16,0},{24,8},{1,17},{9,25},{17,1},{25,9},{2,18},{10... | collective-permute-start | bytes 1572872 | tf_op jit(solution)/shard_map/ppermute | solution.py:517
  332.4 24.7 %collective-permute-start.20 = (bf16[256,1024]{1,0:T(8,128)(2,1)S(1)}, bf16[256,1024]{1,0:T(8,128)(2,1)S(1)}, u32[]{:S(2)}, u32[]{:S(2)}) collective-permute-start(bf16[256,1024]{1,0:T(8,128)(2,1)S(1)} %get-tuple-element.90), channel_id=1, source_target_pairs={{0,24},{8,16},{16,8},{24,0},{1,25},{9,17},{17,9},{25,1},{2,26},{10... | collective-permute-start | bytes 1572872 | tf_op jit(solution)/shard_map/ppermute | solution.py:517
  335.1 43.0 %collective-permute-start.23 = (bf16[4,64,512]{2,1,0:T(8,128)(2,1)S(1)}, bf16[4,64,512]{2,1,0:T(8,128)(2,1)S(1)}, u32[]{:S(2)}, u32[]{:S(2)}) collective-permute-start(bf16[4,64,512]{2,1,0:T(8,128)(2,1)S(1)} %dynamic-slice_bitcast_fusion.3), channel_id=1, source_target_pairs={{0,4},{2,6},{4,0},{6,2},{1,5},{3,7},{5,1},{7,3},{8,12},{10,14},{12... | collective-permute-start | bytes 786440 | tf_op jit(solution)/shard_map/ppermute | solution.py:517
  343.9 22.5 %collective-permute-start.13 = (bf16[256,1024]{1,0:T(8,128)(2,1)S(1)}, bf16[256,1024]{1,0:T(8,128)(2,1)S(1)}, u32[]{:S(2)}, u32[]{:S(2)}) collective-permute-start(bf16[256,1024]{1,0:T(8,128)(2,1)S(1)} %get-tuple-element.94), channel_id=1, source_target_pairs={{0,8},{8,0},{16,24},{24,16},{1,9},{9,1},{17,25},{25,17},{2,10},{10... | collective-permute-start | bytes 1572872 | tf_op jit(solution)/shard_map/ppermute | solution.py:517
  354.4 21.6 %collective-permute-start.14 = (bf16[256,1024]{1,0:T(8,128)(2,1)S(1)}, bf16[256,1024]{1,0:T(8,128)(2,1)S(1)}, u32[]{:S(2)}, u32[]{:S(2)}) collective-permute-start(bf16[256,1024]{1,0:T(8,128)(2,1)S(1)} %get-tuple-element.96), channel_id=1, source_target_pairs={{0,16},{8,24},{16,0},{24,8},{1,17},{9,25},{17,1},{25,9},{2,18},{10... | collective-permute-start | bytes 1572872 | tf_op jit(solution)/shard_map/ppermute | solution.py:517
  357.1 19.0 %collective-permute-start.15 = (bf16[256,1024]{1,0:T(8,128)(2,1)S(1)}, bf16[256,1024]{1,0:T(8,128)(2,1)S(1)}, u32[]{:S(2)}, u32[]{:S(2)}) collective-permute-start(bf16[256,1024]{1,0:T(8,128)(2,1)S(1)} %get-tuple-element.95), channel_id=1, source_target_pairs={{0,24},{8,16},{16,8},{24,0},{1,25},{9,17},{17,9},{25,1},{2,26},{10... | collective-permute-start | bytes 1572872 | tf_op jit(solution)/shard_map/ppermute | solution.py:517
  378.1 49.7 %collective-permute-start.21 = (f32[256,1024]{1,0:T(8,128)}, f32[256,1024]{1,0:T(8,128)}, u32[]{:S(2)}, u32[]{:S(2)}) collective-permute-start(f32[256,1024]{1,0:T(8,128)} %get-tuple-element.109), channel_id=1, source_target_pairs={{0,1},{1,0},{2,3},{3,2},{4,5},{5,4},{6,7},{7,6},{8,9},{9,8},{10,11... | collective-permute-start | bytes 3145736 | tf_op jit(solution)/shard_map/ppermute | solution.py:517
  382.3 23.6 %collective-permute-start.29 = (bf16[4,128,512]{2,1,0:T(8,128)(2,1)S(1)}, bf16[4,128,512]{2,1,0:T(8,128)(2,1)S(1)}, u32[]{:S(2)}, u32[]{:S(2)}) collective-permute-start(bf16[4,128,512]{2,1,0:T(8,128)(2,1)S(1)} %all-to-all-done.8.refs_0_), channel_id=1, source_target_pairs={{0,2},{2,0},{4,6},{6,4},{1,3},{3,1},{5,7},{7,5},{8,10},{10,8},{12,... | collective-permute-start | bytes 1572872 | tf_op jit(solution)/shard_map/ppermute | solution.py:517
  388.4 18.2 %collective-permute-start.25 = (bf16[4,64,512]{2,1,0:T(8,128)(2,1)S(1)}, bf16[4,64,512]{2,1,0:T(8,128)(2,1)S(1)}, u32[]{:S(2)}, u32[]{:S(2)}) collective-permute-start(bf16[4,64,512]{2,1,0:T(8,128)(2,1)S(1)} %all-to-all-done.7.refs_0_), channel_id=1, source_target_pairs={{0,4},{2,6},{4,0},{6,2},{1,5},{3,7},{5,1},{7,3},{8,12},{10,14},{12... | collective-permute-start | bytes 786440 | tf_op jit(solution)/shard_map/ppermute | solution.py:517
  395.0 36.1 %collective-permute-start.16 = (f32[256,1024]{1,0:T(8,128)}, f32[256,1024]{1,0:T(8,128)}, u32[]{:S(2)}, u32[]{:S(2)}) collective-permute-start(f32[256,1024]{1,0:T(8,128)} %get-tuple-element.110), channel_id=1, source_target_pairs={{0,1},{1,0},{2,3},{3,2},{4,5},{5,4},{6,7},{7,6},{8,9},{9,8},{10,11... | collective-permute-start | bytes 3145736 | tf_op jit(solution)/shard_map/ppermute | solution.py:517
  395.4 19.7 %collective-permute-start.31 = (bf16[4,128,512]{2,1,0:T(8,128)(2,1)S(1)}, bf16[4,128,512]{2,1,0:T(8,128)(2,1)S(1)}, u32[]{:S(2)}, u32[]{:S(2)}) collective-permute-start(bf16[4,128,512]{2,1,0:T(8,128)(2,1)S(1)} %collective-permute-done.30.refs_2_), channel_id=1, source_target_pairs={{0,2},{2,0},{4,6},{6,4},{1,3},{3,1},{5,7},{7,5},{8,10},{10,8},{12,... | collective-permute-start | bytes 1572872 | tf_op jit(solution)/shard_map/ppermute | solution.py:517
  406.7 19.2 %collective-permute-start.26 = (bf16[4,64,512]{2,1,0:T(8,128)(2,1)S(1)}, bf16[4,64,512]{2,1,0:T(8,128)(2,1)S(1)}, u32[]{:S(2)}, u32[]{:S(2)}) collective-permute-start(bf16[4,64,512]{2,1,0:T(8,128)(2,1)S(1)} %collective-permute-done.25.refs_2_), channel_id=1, source_target_pairs={{0,2},{2,0},{4,6},{6,4},{1,3},{3,1},{5,7},{7,5},{8,10},{10,8},{12,... | collective-permute-start | bytes 786440 | tf_op jit(solution)/shard_map/ppermute | solution.py:517
  (59 other events, 692.0 us)

commit v3 on v2

--- a/solution.py
+++ b/solution.py
@@ -301,7 +301,7 @@
 ):
     f32 = jnp.float32
     bf16 = jnp.bfloat16
-    ins, refs = refs[:flips], refs[flips:]
+    ins, refs = refs[: 2 * flips], refs[2 * flips :]
     kseg_ref, qseg_ref, refs = refs[0], refs[1], refs[2:]
     outs, refs = refs[:flips], refs[flips:]
     x_ref, y_ref, kt_ref, vt_ref, s_ref, e_ref, dk_acc, dv_acc = refs
@@ -322,7 +322,8 @@
     @pl.when(step == 0)
     def _():
         for flip in range(flips):
-            x_ref[spot(flip), :] = ins[flip][...]
+            x_ref[spot(flip), : 3 * width] = ins[flip][...]
+            x_ref[spot(flip), 3 * width :] = ins[flips + flip][...]
         for c in range(chunks):
             part = pl.ds(c * chunk, chunk)
             kt_ref[c] = k_ref[part, :].astype(f32).T.astype(bf16)
@@ -431,9 +432,9 @@
 
 
 def attention(blocks, seg, place, block=256, chunk=256):
-    flips = len(blocks)
-    span, columns = blocks[0].shape
-    count, width = span * flips, columns // 4
+    flips = len(blocks) // 2
+    span, width = blocks[-1].shape
+    count, columns = span * flips, 4 * width
     heads = width // HD
     bf16 = jnp.bfloat16
     f32 = jnp.float32
@@ -444,7 +445,7 @@
         grid_spec=pltpu.PrefetchScalarGridSpec(
             num_scalar_prefetch=1,
             grid=(count // block,),
-            in_specs=[whole] * flips
+            in_specs=[pl.BlockSpec(block.shape, lambda i, p: (0, 0)) for block in blocks]
             + [
                 pl.BlockSpec((count, 1), lambda i, p: (0, 0)),
                 pl.BlockSpec((1, block), lambda i, p: (0, i)),
@@ -470,45 +471,59 @@
     )(place.reshape(1), *blocks, seg[:, None], seg[None, :])
 
 
-def norm_body(core_ref, mine_ref, other_ref, params_ref, first_ref, second_ref, normed_ref):
-    core = core_ref[0]
-    f32 = jnp.float32
-    for source, slot in ((mine_ref, core), (other_ref, 1 - core)):
-        normed, _ = normalize(source[0].astype(f32))
-        normed_ref[0, slot] = normed.astype(jnp.bfloat16)
-        first_ref[0, slot] = (normed * params_ref[0:1] + params_ref[1:2]).astype(jnp.bfloat16)
-        second_ref[0, slot] = (normed * params_ref[2:3] + params_ref[3:4]).astype(jnp.bfloat16)
-
-
-def merge_body(core_ref, mine_ref, other_ref, out_ref):
-    core = core_ref[0]
-    out_ref[0, core] = mine_ref[0]
-    out_ref[0, 1 - core] = other_ref[0]
-
-
-def both_cores(body, mine, core, params, results):
-    size, half, cols = mine.shape
-    other = partner(mine, "tp", 1)
-    side = pl.BlockSpec((1, half, cols), lambda i, c: (i, 0, 0))
-    out = pl.BlockSpec((1, 2, half, cols), lambda i, c: (i, 0, 0, 0))
-    extra = [pl.BlockSpec(p.shape, lambda i, c: (0, 0)) for p in params]
+def norm_rows(x, slot, params_ref, outs):
+    bf16 = jnp.bfloat16
+    first_ref, second_ref, normed_ref = outs
+    normed, _ = normalize(x.astype(jnp.float32))
+    normed_ref[0, slot] = normed.astype(bf16)
+    first_ref[0, slot] = (normed * params_ref[0:1] + params_ref[1:2]).astype(bf16)
+    second_ref[0, slot] = (normed * params_ref[2:3] + params_ref[3:4]).astype(bf16)
+
+
+def merge_rows(x, slot, params_ref, outs):
+    outs[0][0, slot] = x
+
+
+def both_cores(rows_body, own, mine, other, core, params, results):
+    size = len(mine) + 1
+    half, cols = mine[0].shape
+
+    def run(core_ref, *refs):
+        own_ref, refs = refs[0], refs[1:]
+        ins, params_ref, outs = refs[: 2 * size - 2], refs[2 * size - 2], refs[2 * size - 1 :]
+        core = core_ref[0]
+
+        @pl.when(pl.program_id(0) == 0)
+        def _():
+            for slot in range(2):
+                rows_body(own_ref[slot * half : (slot + 1) * half, :], slot, params_ref, outs)
+
+        for chip in range(1, size):
+
+            @pl.when(pl.program_id(0) == chip)
+            def _(chip=chip):
+                rows_body(ins[chip - 1][...], core, params_ref, outs)
+                rows_body(ins[size + chip - 2][...], 1 - core, params_ref, outs)
+
     made = pl.pallas_call(
-        body,
+        run,
         grid_spec=pltpu.PrefetchScalarGridSpec(
             num_scalar_prefetch=1,
             grid=(size,),
-            in_specs=[side, side] + extra,
-            out_specs=[out] * results,
-        ),
-        out_shape=[jax.ShapeDtypeStruct((size, 2, half, cols), mine.dtype)] * results,
+            in_specs=[pl.BlockSpec(own.shape, lambda i, c: (0, 0))]
+            + [pl.BlockSpec((half, cols), lambda i, c: (0, 0))] * (2 * size - 2)
+            + [pl.BlockSpec(params.shape, lambda i, c: (0, 0))],
+            out_specs=[pl.BlockSpec((1, 2, half, cols), lambda i, c: (i, 0, 0, 0))] * results,
+        ),
+        out_shape=[jax.ShapeDtypeStruct((size, 2, half, cols), own.dtype)] * results,
         compiler_params=pltpu.CompilerParams(vmem_limit_bytes=32 * 1024 * 1024),
         cost_estimate=pl.CostEstimate(
             flops=size * half * cols * 20,
             bytes_accessed=size * half * cols * 4 * (1 + results),
             transcendentals=0,
         ),
-        name=body.__name__,
-    )(core.reshape(1), mine, other, *params)
+        name=rows_body.__name__,
+    )(core.reshape(1), own, *mine, *other, params)
     return [x.reshape(size * 2 * half, cols) for x in made]
 
 
@@ -527,19 +542,6 @@
 
 def gather(block, axis):
     return swap(jnp.broadcast_to(block[None], (lax.axis_size(axis),) + block.shape), axis)
-
-
-def double_up(block, axis, order):
-    held = block[None]
-    bits = []
-    for bit in order:
-        held = jnp.stack([held, partner(held, axis, 1 << bit)], 0)
-        bits.insert(0, bit)
-    levels = len(order)
-    held = held.reshape((2,) * levels + block.shape)
-    turn = [bits.index(bit) for bit in reversed(range(levels))]
-    held = held.transpose(turn + list(range(levels, levels + block.ndim)))
-    return held.reshape((2**levels,) + block.shape)
 
 
 def chip_start(partial, size):
@@ -551,29 +553,20 @@
     return (kept.astype(f32) + partner(away, "tp", 1).astype(f32)).astype(partial.dtype)
 
 
-def chip_finish(sending):
-    f32 = jnp.float32
-    total = sending[0].astype(f32)
-    for flip in range(1, sending.shape[0]):
-        total = total + partner(sending[flip], "fsdp", flip).astype(f32)
-    return total
-
-
-def chip_join(mine):
+def chip_join(mine, other):
     core = lax.axis_index("tp")
-    other = partner(mine, "tp", 1)
     low = jnp.where(core == 0, mine, other)
     high = jnp.where(core == 0, other, mine)
     return jnp.concatenate([low, high], 0)
 
 
-def pack_wide(up, down, out, low, chips, part):
-    span = down.shape[3] // chips
+def pack_wide(up, down, out, chips, part):
+    span = down.shape[2] // chips
     for chip in range(chips):
-        out[0, chip, :part, :] = up[chip, 0, low]
+        out[0, chip, :part, :] = up[chip, 0]
         for half in range(2):
             out[0, chip, part:, half * span : (half + 1) * span] = down[
-                0, low, half * part : (half + 1) * part, chip * span : (chip + 1) * span
+                0, half * part : (half + 1) * part, chip * span : (chip + 1) * span
             ]
 
 
@@ -588,43 +581,6 @@
             out[0, chip, half * rows : (half + 1) * rows, width:] = outw[
                 0, low, :, begin : begin + span
             ]
-
-
-def pack(body, wide, tall, rows, chips, place):
-    bf16 = jnp.bfloat16
-    depth = 4
-    part = wide.shape[0] // chips // depth
-    cols = part * 8
-    wide = wide.reshape(chips, 2, 2, part, wide.shape[1])
-    tall = tall.reshape(2, 2, tall.shape[0] // depth, tall.shape[1])
-
-    def run(place_ref, wide_ref, tall_ref, kept_ref, away_ref):
-        side = place_ref[0] & 1
-        body(wide_ref, tall_ref, kept_ref, side, chips, part)
-        body(wide_ref, tall_ref, away_ref, 1 - side, chips, part)
-
-    made = jax.ShapeDtypeStruct((2, chips, rows, cols), bf16)
-    out = pl.BlockSpec((1, chips, rows, cols), lambda i, p: (i, 0, 0, 0))
-    return pl.pallas_call(
-        run,
-        grid_spec=pltpu.PrefetchScalarGridSpec(
-            num_scalar_prefetch=1,
-            grid=(2,),
-            in_specs=[
-                pl.BlockSpec(
-                    (chips, 1, 2, part, wide.shape[4]), lambda i, p: (0, i, 0, 0, 0)
-                ),
-                pl.BlockSpec((1,) + tall.shape[1:], lambda i, p: (i, 0, 0, 0)),
-            ],
-            out_specs=[out, out],
-        ),
-        out_shape=[made, made],
-        compiler_params=pltpu.CompilerParams(vmem_limit_bytes=24 * 1024 * 1024),
-        cost_estimate=pl.CostEstimate(
-            flops=0, bytes_accessed=16 * chips * rows * cols, transcendentals=0
-        ),
-        name=body.__name__,
-    )(place.reshape(1), wide, tall)
 
 
 def unpack_wide(x, up, down, chips, part):
@@ -692,24 +648,132 @@
     )(place.reshape(1), *blocks)
 
 
-def sum_slots(kept, away, gate=()):
+def pack_slots(body, wide, tall, rows, chips, place):
+    depth = 4
+    part = wide.shape[0] // chips // depth
+    cols = part * 8
+    wide = wide.reshape(chips, 1, depth, part, wide.shape[1])
+    tall = tall.reshape(1, depth, tall.shape[0] // depth, tall.shape[1])
+
+    def run(place_ref, wide_ref, tall_ref, *outs):
+        for k in range(depth):
+            body(wide_ref, tall_ref, outs[k], place_ref[0] ^ k, chips, part)
+
+    return pl.pallas_call(
+        run,
+        grid_spec=pltpu.PrefetchScalarGridSpec(
+            num_scalar_prefetch=1,
+            grid=(1,),
+            in_specs=[
+                pl.BlockSpec(wide.shape, lambda i, p: (0, 0, 0, 0, 0)),
+                pl.BlockSpec(tall.shape, lambda i, p: (0, 0, 0, 0)),
+            ],
+            out_specs=[pl.BlockSpec((1, chips, rows, cols), lambda i, p: (0, 0, 0, 0))] * depth,
+        ),
+        out_shape=[jax.ShapeDtypeStruct((1, chips, rows, cols), jnp.bfloat16)] * depth,
+        compiler_params=pltpu.CompilerParams(vmem_limit_bytes=24 * 1024 * 1024),
+        cost_estimate=pl.CostEstimate(
+            flops=0, bytes_accessed=16 * chips * rows * cols, transcendentals=0
+        ),
+        name=body.__name__,
+    )(place.reshape(1), wide, tall)
+
+
+def pack_all(body, wide, tall, rows, chips):
+    depth = 4
+    part = wide.shape[0] // chips // depth
+    cols = part * 8
+    wide = wide.reshape(chips, depth, part, wide.shape[1])
+    tall = tall.reshape(depth, tall.shape[0] // depth, tall.shape[1])
+
+    def run(wide_ref, tall_ref, out):
+        body(wide_ref, tall_ref, out, chips, part)
+
+    return pl.pallas_call(
+        run,
+        grid=(depth,),
+        in_specs=[
+            pl.BlockSpec((chips, 1, part, wide.shape[3]), lambda i: (0, i, 0, 0)),
+            pl.BlockSpec((1,) + tall.shape[1:], lambda i: (i, 0, 0)),
+        ],
+        out_specs=pl.BlockSpec((1, chips, rows, cols), lambda i: (i, 0, 0, 0)),
+        out_shape=jax.ShapeDtypeStruct((depth, chips, rows, cols), jnp.bfloat16),
+        compiler_params=pltpu.CompilerParams(vmem_limit_bytes=24 * 1024 * 1024),
+        cost_estimate=pl.CostEstimate(
+            flops=0, bytes_accessed=4 * depth * chips * rows * cols, transcendentals=0
+        ),
+        name="pack_wide",
+    )(wide, tall)
+
+
+def add_slots(slots):
+    total = slots[0][0].astype(jnp.float32)
+    for slot in slots[1:]:
+        total = total + slot[0].astype(jnp.float32)
+    return total.astype(jnp.bfloat16)
+
+
+def send_slots(slots):
+    return [slots[0]] + [partner(slots[k], "ctx", k) for k in range(1, len(slots))]
+
+
+def after(tensor, *others):
+    return lax.optimization_barrier((tensor,) + others)[0]
+
+
+def hidden_body(second_ref, cot_ref, up_ref, down_ref, bias_ref, act_ref, dup_ref, sum_ref):
     f32 = jnp.float32
     bf16 = jnp.bfloat16
-    side = lax.axis_index("ctx") >> 1
-    held = (kept.astype(f32) + partner(away, "ctx", 1).astype(f32)).astype(bf16)
-    held = after(held, *gate)
-    kept = lax.dynamic_index_in_dim(held, side, 0, keepdims=False)
-    away = lax.dynamic_index_in_dim(held, 1 - side, 0, keepdims=False)
-    return (kept.astype(f32) + partner(away, "ctx", 2).astype(f32)).astype(bf16)
-
-
-def spread(held):
-    far = partner(held, "ctx", 2)
-    return [held, partner(held, "ctx", 1), far, partner(far, "ctx", 1)]
-
-
-def after(tensor, *others):
-    return lax.optimization_barrier((tensor,) + others)[0]
+    upper = jnp.dot(second_ref[...], up_ref[...], preferred_element_type=f32)
+    upper = upper + bias_ref[...]
+    share = 0.5 + 0.5 * lax.erf(upper * 0.5**0.5)
+    act_ref[...] = (upper * share).astype(bf16)
+    d_act = lax.dot_general(
+        cot_ref[...], down_ref[...], (((1,), (1,)), ((), ())), preferred_element_type=f32
+    )
+    bell = jnp.exp(-0.5 * upper * upper) * (0.5 / jnp.pi) ** 0.5
+    d_upper = d_act * (share + upper * bell)
+    dup_ref[...] = d_upper.astype(bf16)
+
+    @pl.when(pl.program_id(0) == 0)
+    def _():
+        sum_ref[...] = jnp.zeros_like(sum_ref)
+
+    sum_ref[...] += jnp.sum(d_upper, 0, keepdims=True)
+
+
+def hidden_layer(second, cot_b, up_w, down_w, up_bias, block=256):
+    f32 = jnp.float32
+    bf16 = jnp.bfloat16
+    count, model = second.shape
+    hidden = up_w.shape[1]
+    rows = pl.BlockSpec((block, model), lambda i: (i, 0))
+    made = pl.BlockSpec((block, hidden), lambda i: (i, 0))
+    act, dup, total = pl.pallas_call(
+        hidden_body,
+        grid=(count // block,),
+        in_specs=[
+            rows,
+            rows,
+            pl.BlockSpec((model, hidden), lambda i: (0, 0)),
+            pl.BlockSpec((hidden, model), lambda i: (0, 0)),
+            pl.BlockSpec((1, hidden), lambda i: (0, 0)),
+        ],
+        out_specs=[made, made, pl.BlockSpec((1, hidden), lambda i: (0, 0))],
+        out_shape=[
+            jax.ShapeDtypeStruct((count, hidden), bf16),
+            jax.ShapeDtypeStruct((count, hidden), bf16),
+            jax.ShapeDtypeStruct((1, hidden), f32),
+        ],
+        compiler_params=pltpu.CompilerParams(vmem_limit_bytes=32 * 1024 * 1024),
+        cost_estimate=pl.CostEstimate(
+            flops=4 * count * model * hidden,
+            bytes_accessed=4 * count * (model + hidden) + 4 * model * hidden,
+            transcendentals=2 * count * hidden,
+        ),
+        name="hidden_layer",
+    )(second, cot_b, up_w, down_w, up_bias.astype(f32)[None])
+    return act, dup, total[0]
 
 
 def plane_local(
@@ -739,14 +803,13 @@
     half_rows = count // 2
     rows = tokens[0].astype(f32)
     cot = cotangent[0]
-    levels = list(range(size.bit_length() - 1))
-
-    my_tokens = double_up(pick(tokens[0], core, half_rows), "fsdp", levels)
-    my_cot = double_up(pick(cot, core, half_rows).astype(bf16), "fsdp", levels[::-1])
+
+    half = pick(tokens[0], core, half_rows)
+    my_tokens = [partner(half, "fsdp", k) for k in range(1, size)]
+    cot_half, _ = lax.optimization_barrier((cot.astype(bf16), tuple(my_tokens)))
+    half = pick(cot_half, core, half_rows)
+    my_cot = [partner(half, "fsdp", k) for k in range(1, size)]
     width = joint_weight.shape[2] // size
-    joint_w = swap(
-        joint_weight.reshape(-1, 3, size, width).transpose(2, 0, 1, 3), "fsdp"
-    ).reshape(model, 3, width)
     small = jnp.concatenate(
         [
             attention_gain,
@@ -759,9 +822,13 @@
     ).astype(f32)
     notes = jnp.concatenate([small, segment_ids[0].astype(f32), positions[0].astype(f32)])
     packed = gather(
-        after(notes, joint_w),
+        notes,
         ("fsdp", "ctx"),
     ).reshape(size, depth, -1)
+    joint_send = joint_weight.reshape(-1, 3, size, width).transpose(2, 0, 1, 3)
+    tokens_other = [partner(block, "tp", 1) for block in my_tokens]
+    joint_w = swap(after(joint_send, packed), "fsdp")
+    joint_w = after(joint_w, *tokens_other).reshape(model, 3, width)
     params = packed[:, 0, : small.size].reshape(size, 6, -1).transpose(1, 0, 2).reshape(6, model)
     seg_seq = lax.dynamic_index_in_dim(packed, place, 0, keepdims=False)
     seg_seq = seg_seq[:, small.size : small.size + count].reshape(-1)
@@ -769,10 +836,13 @@
     pos_plane = jnp.concatenate(
         [lax.dynamic_index_in_dim(pos_here, me ^ k, 0, keepdims=False) for k in range(size)]
     )
-    output_w = swap(after(output_weight, packed).reshape(size, width, -1), "fsdp")
+    first, second, normed = both_cores(
+        norm_rows, tokens[0], my_tokens, tokens_other, core, params[:4], 3
+    )
+    output_w = swap(after(output_weight, first).reshape(size, width, -1), "fsdp")
     output_w = output_w.transpose(1, 0, 2).reshape(width, model)
-    first, second, normed = both_cores(norm_body, my_tokens, core, [params[:4]], 3)
-    (cot_b,) = both_cores(merge_body, my_cot, core, [], 1)
+    cot_other = [partner(block, "tp", 1) for block in my_cot]
+    (cot_b,) = both_cores(merge_rows, cot_half, my_cot, cot_other, core, params[:4], 1)
     hidden = up_weight.shape[1] // size
     up_send = up_weight.reshape(-1, size, hidden).transpose(1, 0, 2)
     up_w = swap(after(up_send, output_w, first, cot_b), "fsdp")
@@ -806,20 +876,15 @@
     queries = (joint[:, :width] * cosine + swapped[:, :width] * sine) * scale
     keys = joint[:, width : 2 * width] * cosine + swapped[:, width:] * sine
     d_context = jnp.einsum("nd,wd->nw", cot_b, output_w, preferred_element_type=f32)
-    sending = jnp.concatenate([queries, keys, joint[:, 2 * width :], d_context], 1).astype(bf16)
+    sending = jnp.concatenate([queries, keys, joint[:, 2 * width :]], 1).astype(bf16)
     blocks = []
-    for flip in range(depth):
-        block = pick(sending, me ^ place ^ flip, count)
-        blocks.append(partner(block, "ctx", flip) if flip else block)
+    for tensor in (sending, d_context.astype(bf16)):
+        for flip in range(depth):
+            block = pick(tensor, me ^ place ^ flip, count)
+            blocks.append(partner(block, "ctx", flip) if flip else block)
     second, up_w = lax.optimization_barrier((second, up_w, sending))[:2]
 
-    upper = jnp.dot(second, up_w, preferred_element_type=f32) + up_bias.astype(f32)[None]
-    gelu, gelu_back = jax.vjp(lambda value: jax.nn.gelu(value, approximate=False), upper)
-    activated = gelu.astype(bf16)
-    d_act = jnp.einsum("nd,fd->nf", cot_b, down_w, preferred_element_type=f32)
-    d_upper = gelu_back(d_act)[0]
-    d_upper_b = d_upper.astype(bf16)
-    grad_up_b = jnp.sum(d_upper, 0)
+    activated, d_upper_b, grad_up_b = hidden_layer(second, cot_b, up_w, down_w, up_bias)
     moment_up = jnp.dot(normed.T, d_upper_b, preferred_element_type=f32)
     d_upper_sum = jnp.sum(d_upper_b.astype(f32), 0)
     grad_up_w = (
@@ -830,34 +895,25 @@
     shift_two_grad = jnp.sum(up_f32 * d_upper_sum[None, :], 1)
     grad_down_w = jnp.dot(activated.T, cot_b, preferred_element_type=f32).astype(bf16)
     part = model // size // depth
-    kept, away = pack(pack_wide, grad_up_w, grad_down_w, 2 * part, size, place)
-    held = (kept, away)
-    blocks = lax.optimization_barrier((tuple(blocks), kept, away))[0]
+    packed_wide = pack_all(pack_wide, grad_up_w, grad_down_w, 2 * part, size)
+    blocks, packed_wide = lax.optimization_barrier((tuple(blocks), packed_wide))
     made = attention(blocks, seg_seq, place)
-    kept, away = held
-    held = swap(sum_slots(kept, away), "fsdp")
-    owned_up, owned_down = unpack(
-        unpack_wide,
-        spread(held),
-        (model // size, up_weight.shape[1]),
-        (part, up_weight.shape[1]),
-        (size, depth, 2 * part, 2 * width),
-        (size, 1, 2 * part, 2 * width),
-        place,
-    )
-    owned_down = owned_down.reshape(down_weight.shape)
+    made, packed_wide = lax.optimization_barrier((tuple(made), swap(packed_wide, "ctx")))
+    held_wide = swap(jnp.sum(packed_wide.astype(f32), 0).astype(bf16), "fsdp")
     gained = (up_f32 * params[2][:, None]).astype(bf16)
     upstream_two = jnp.einsum("nf,df->nd", d_upper_b, gained, preferred_element_type=f32)
     upstream_two = upstream_two.astype(bf16)
     mixed_two = jnp.dot(activated, down_w, preferred_element_type=f32).astype(bf16)
 
-    back = jnp.zeros(sending.shape, bf16)
+    back = jnp.zeros((size * count, 4 * width), bf16)
+    made = [made[0]] + [partner(made[k], "ctx", k) for k in range(1, depth)]
+    made, held_wide = lax.optimization_barrier((tuple(made), held_wide))
+    near_far = partner(held_wide, "ctx", 1), partner(held_wide, "ctx", 2)
     for flip in range(depth):
-        block = partner(made[flip], "ctx", flip) if flip else made[flip]
+        block = made[flip]
         back = lax.dynamic_update_slice_in_dim(back, block, (me ^ place ^ flip) * count, 0)
     context = back[:, :width]
     d_qk = back[:, width : 3 * width]
-    grad_output_w = jnp.dot(context.T, cot_b, preferred_element_type=f32).astype(bf16)
 
     d_swapped = jnp.einsum(
         "npe,ef->npf", d_qk.reshape(-1, 2, width), turn, preferred_element_type=f32
@@ -868,47 +924,26 @@
         [d_qk.astype(f32) * cosines - d_swapped * sines, back[:, 3 * width :].astype(f32)], 1
     )
     d_joint_b = d_joint.astype(bf16)
+    joint_f32 = joint_flat.astype(f32)
+    gained = (joint_f32 * params[0][:, None]).astype(bf16)
+    mixed = jnp.dot(context, output_w, preferred_element_type=f32) + mixed_two.astype(f32)
+    mixed = mixed.astype(bf16)
+    upstream = jnp.einsum("ne,de->nd", d_joint_b, gained, preferred_element_type=f32)
+    upstream = (upstream + upstream_two.astype(f32)).astype(bf16)
+    d_joint_b, context = lax.optimization_barrier((d_joint_b, context, mixed, upstream))[:2]
+    sending_result = chip_start(mixed, size)
+    sending_up = chip_start(upstream, size)
+    got_result = partner(sending_result[2:], "fsdp", 2)
+    got_up = partner(sending_up[1::2], "fsdp", 1)
     grad_joint_b = jnp.sum(d_joint, 0)
     moment_joint = jnp.dot(normed.T, d_joint_b, preferred_element_type=f32)
     d_joint_sum = jnp.sum(d_joint_b.astype(f32), 0)
     grad_joint_w = (
         params[0][:, None] * moment_joint + params[1][:, None] * d_joint_sum[None, :]
     ).astype(bf16)
-    kept, away = pack(pack_heads, grad_joint_w, grad_output_w, part, size, place)
-    context, d_joint_b = lax.optimization_barrier((context, d_joint_b, kept, away))[:2]
-    mixed = jnp.dot(context, output_w, preferred_element_type=f32) + mixed_two.astype(f32)
-    sending_result = chip_start(mixed.astype(bf16), size)
-    joint_f32 = joint_flat.astype(f32)
-    gained = (joint_f32 * params[0][:, None]).astype(bf16)
-    upstream = jnp.einsum("ne,de->nd", d_joint_b, gained, preferred_element_type=f32)
-    sending_up = chip_start((upstream + upstream_two.astype(f32)).astype(bf16), size)
-    held = sum_slots(kept, away, (sending_result, sending_up))
-    held = swap(held, "fsdp")
-    owned_joint, owned_output = unpack(
-        unpack_heads,
-        spread(held),
-        (3, model // size, joint_weight.shape[2]),
-        (3, part, joint_weight.shape[2]),
-        (size, depth, part // 2, 2 * width),
-        (size, 1, part // 2, 2 * width),
-        place,
-    )
-    owned_joint = owned_joint.transpose(1, 0, 2)
-    owned_output = owned_output.reshape(output_weight.shape)
-
-    my_rows = pick(rows, core, half_rows)
-    result = chip_join(my_rows + chip_finish(sending_result) + params[4] + params[5])
-    normed_here, rstd = normalize(my_rows)
-    upstream = chip_finish(sending_up)
-    tokens_grad = chip_join(
-        pick(cot, core, half_rows)
-        + rstd
-        * (
-            upstream
-            - jnp.mean(upstream, -1, keepdims=True)
-            - normed_here * jnp.mean(upstream * normed_here, -1, keepdims=True)
-        )
-    )
+    grad_output_w = jnp.dot(context.T, cot_b, preferred_element_type=f32).astype(bf16)
+    slots = pack_slots(pack_heads, grad_joint_w, grad_output_w, part, size, place)
+    slots = send_slots(slots)
     stats = jnp.stack(
         [
             jnp.sum(joint_f32 * moment_joint, 1),
@@ -918,14 +953,69 @@
             jnp.sum(pick(cot, core, half_rows), 0),
         ]
     )
-    stats = jnp.sum(swap(stats.reshape(5, size, -1).transpose(1, 0, 2), "fsdp"), 0)
-    packed = jnp.concatenate([stats.reshape(-1), grad_joint_b, grad_up_b])
-    packed = gather(packed, ("ctx", "tp")).reshape(depth, 2, -1)
-    owned = jnp.sum(packed[:, :, : stats.size], (0, 1)).reshape(stats.shape)
-    biases = jnp.sum(packed[:, :, stats.size :], 0)
-    biases = lax.dynamic_index_in_dim(biases, core, 0, keepdims=False)
+    stats = stats.reshape(5, size, 1, -1).transpose(1, 2, 0, 3).reshape(size, 1, -1)
+    biases = jnp.concatenate([grad_joint_b, grad_up_b])
+    biases = jnp.broadcast_to(biases[None, None], (size, 1, 3 * width + hidden))
+    stats_size = stats.shape[2]
+    packed = jnp.concatenate([stats, biases], 2)
+    packed = jnp.broadcast_to(packed, (size, 2 * depth, packed.shape[2]))
+    packed = swap(packed.reshape(2 * size * depth, 1, -1), ("fsdp", "ctx", "tp"))
+    got_result, got_up = lax.optimization_barrier((got_result, got_up))
+    half_result = sending_result[:2].astype(f32) + got_result.astype(f32)
+    half_up = sending_up[::2].astype(f32) + got_up.astype(f32)
+    got_result = partner(half_result[1].astype(bf16), "fsdp", 1)
+    got_up = partner(half_up[1].astype(bf16), "fsdp", 2)
+    slots, near_far, got_result, got_up, packed = lax.optimization_barrier(
+        (tuple(slots), near_far, got_result, got_up, packed)
+    )
+
+    held = swap(add_slots(slots), "fsdp")
+    last = partner(near_far[1], "ctx", 1)
+    my_rows = pick(rows, core, half_rows)
+    result = my_rows + half_result[0] + got_result.astype(f32) + params[4] + params[5]
+    normed_here, rstd = normalize(my_rows)
+    upstream = half_up[0] + got_up.astype(f32)
+    tokens_grad = pick(cot, core, half_rows) + rstd * (
+        upstream
+        - jnp.mean(upstream, -1, keepdims=True)
+        - normed_here * jnp.mean(upstream * normed_here, -1, keepdims=True)
+    )
+    other_result = partner(result, "tp", 1)
+    other_grad = partner(tokens_grad, "tp", 1)
+    held, last, other_result, other_grad = lax.optimization_barrier(
+        (held, last, other_result, other_grad)
+    )
+
+    slots = send_slots([held[None]] * depth)
+    result = chip_join(result, other_result)
+    tokens_grad = chip_join(tokens_grad, other_grad)
+    packed = packed.reshape(size, depth, 2, -1)
+    owned = jnp.sum(packed[..., :stats_size], (0, 1, 2)).reshape(5, -1)
+    biases = lax.dynamic_index_in_dim(packed[..., stats_size:], me, 0, keepdims=False)
+    biases = jnp.sum(lax.dynamic_index_in_dim(biases, core, 1, keepdims=False), 0)
     owned_jbias = biases[: 3 * width].reshape(3, width)
     owned_upbias = biases[3 * width :]
+    owned_up, owned_down = unpack(
+        unpack_wide,
+        (held_wide, near_far[0], near_far[1], last),
+        (model // size, up_weight.shape[1]),
+        (part, up_weight.shape[1]),
+        (size, depth, 2 * part, 2 * width),
+        (size, 1, 2 * part, 2 * width),
+        place,
+    )
+    owned_down = owned_down.reshape(down_weight.shape)
+    owned_joint, owned_output = unpack(
+        unpack_heads,
+        [slot[0] for slot in slots],
+        (3, model // size, joint_weight.shape[2]),
+        (3, part, joint_weight.shape[2]),
+        (size, depth, part // 2, 2 * width),
+        (size, 1, part // 2, 2 * width),
+        place,
+    )
+    owned_joint = owned_joint.transpose(1, 0, 2)
+    owned_output = owned_output.reshape(output_weight.shape)
     return (
         result[None],
         tokens_grad[None],

time: 442 us -> 429 us (0.971)
  the two profiles are of different devices: /device:TPU:0 before, /device:TPU:8 now
where the time goes in v3:
time: 429 us; the launch traced here: 421 us
  waiting for transfers between devices  115 us (27%)
  local copies, waits for them, and re-layouts  73.2 us (17%)
  starting transfers between devices  72.1 us (17%)
  Pallas kernels  66.7 us (16%)
  other arithmetic  49.1 us (11%)
  matrix products  43.4 us (10%)
    ppermute x38, waiting for transfers between devices, partner(): return lax.ppermute(tensor, axis, [(s, s ^ flip) for s in range(size)])  100 us
    pallas_call x1, Pallas kernels, attention(): pl.pallas_call(lambda *refs: attention_body(heads, flips, *refs), grid_sp...  46.6 us
    all_to_all x9, starting transfers between devices, swap(): return lax.all_to_all(tensor, axis, 0, 0)  38.9 us
    unnamed x152, local copies, waits for them, and re-layouts  35.2 us
    ppermute x38, starting transfers between devices, partner(): return lax.ppermute(tensor, axis, [(s, s ^ flip) for s in range(size)])  33.2 us
    all_to_all x9, waiting for transfers between devices, swap(): return lax.all_to_all(tensor, axis, 0, 0)  14.7 us
  transfers between devices with their start and end apart: 47, of which 19 were waited for; matrix products, arithmetic and copies ran while one was open for 27% of the time, Pallas kernels for 15%

profile of v3, /device:TPU:8, one launch (start us, length us, event | category | flops | bytes accessed | tf_op | source)
XLA Modules:
  0.0 421.1 jit_solution(12865377868052674851)
XLA Ops:
  13.3 7.2 %all-to-all-start = ((f32[16,1,2560]{2,1,0:T(1,128)}), f32[16,1,2560]{2,1,0:T(1,128)S(1)}, u32[]{:S(2)}, u32[]{:S(2)}) async-start(f32[16,1,2560]{2,1,0:T(1,128)} %broadcast_in_dim.66), calls=%async_computation | async-start | bytes 327680 | tf_op jit(solution)/shard_map/all_to_all | solution.py:540
  24.8 5.9 %all-to-all-done = f32[16,1,2560]{2,1,0:T(1,128)S(1)} async-done(((f32[16,1,2560]{2,1,0:T(1,128)}), f32[16,1,2560]{2,1,0:T(1,128)S(1)}, u32[]{:S(2)}, u32[]{:S(2)}) %all-to-all-start) | async-done | bytes 163872 | tf_op jit(solution)/shard_map/all_to_all | solution.py:540
  33.4 4.2 all-to-all-start.1
  45.0 5.6 %norm_rows.1 = (bf16[4,2,256,1024]{3,2,1,0:T(8,128)(2,1)S(1)}, bf16[4,2,256,1024]{3,2,1,0:T(8,128)(2,1)S(1)}, bf16[4,2,256,1024]{3,2,1,0:T(8,128)(2,1)S(1)}) custom-call(s32[1]{0:T(128)} %bitcast.2.core_ref, bf16[512,1024]{1,0:T(8,128)(2,1)S(1)} %bitcast.173, bf16[256,1024]{1,0:T(8,128)(2,1)S(1)} %collective-permute-done.refs_1_, ...), custom_call_target="tpu_custom_call" | custom-call | flops 20971520 | bytes 16777216 | tf_op jit(solution)/shard_map/norm_rows/pallas_call | solution.py:508
  56.6 4.4 %all-to-all-start.2 = ((bf16[4,128,256]{2,1,0:T(8,128)(2,1)}), bf16[4,128,256]{2,1,0:T(8,128)(2,1)S(1)}, u32[]{:S(2)}, u32[]{:S(2)}) async-start(bf16[4,128,256]{2,1,0:T(8,128)(2,1)} %bitcast.223), calls=%async_computation.2 | async-start | bytes 524288 | tf_op jit(solution)/shard_map/all_to_all | solution.py:540
  63.5 9.8 %collective-permute-done.11.refs_3_ = bf16[256,1024]{1,0:T(8,128)(2,1)} collective-permute-done((bf16[256,1024]{1,0:T(8,128)(2,1)}, bf16[256,1024]{1,0:T(8,128)(2,1)}, u32[]{:S(2)}, u32[]{:S(2)}) %collective-permute-start.11) | collective-permute-done | bytes 524320 | tf_op jit(solution)/shard_map/ppermute | solution.py:532
  73.3 6.2 %convolution_add_fusion = f32[2048,384]{1,0:T(8,128)} fusion(bf16[2048,1024]{1,0:T(8,128)(2,1)} %bitcast.203, bf16[1024,384]{0,1:T(8,128)(2,1)S(1)} %bitcast.212, f32[384]{0:T(512)S(1)} %bitcast_convert_fusion), kind=kOutput, calls=%fused_computation.12 | convolution fusion | flops 1611399168 | bytes 8128000 | tf_op jit(solution)/shard_map/dot_general | solution.py:868
  88.8 3.6 all-to-all-start.3
  92.5 3.7 convolution_add_fusion.1
  97.0 5.7 %fusion.33 = (bf16[2048,128]{1,0:T(8,128)(2,1)}, bf16[2048,128]{1,0:T(8,128)(2,1)}, f32[2048,128]{1,0:T(8,128)}, f32[2048,128]{1,0:T(8,128)}) fusion(f32[2048,256]{1,0:T(8,128)S(1)} %convolution_add_fusion.1, f32[2048,384]{1,0:T(8,128)S(1)} %copy-done.44, f32[128]{0:T(128)S(1)} %get-tuple-element.180, f32[128]{0:T(128)S(1)} %get-tuple-element.181, ...), kind=kLoop, calls=%fused_computation.76 | loop fusion | flops 2883584 | bytes 7349248 | tf_op jit(solution)/shard_map/convert.8 | solution.py:1088
  102.8 4.2 %all-to-all-done.3 = bf16[4,256,512]{2,1,0:T(8,128)(2,1)S(1)} async-done(((bf16[4,256,512]{2,1,0:T(8,128)(2,1)}), bf16[4,256,512]{2,1,0:T(8,128)(2,1)S(1)}, u32[]{:S(2)}, u32[]{:S(2)}) %all-to-all-start.3) | async-done | bytes 1048608 | tf_op jit(solution)/shard_map/all_to_all | solution.py:540
  107.0 3.8 all-to-all-start.4
  130.7 6.2 %hidden_layer.1 = (bf16[2048,512]{1,0:T(8,128)(2,1)S(1)}, bf16[2048,512]{1,0:T(8,128)(2,1)S(1)}, f32[1,512]{1,0:T(1,128)S(1)}) custom-call(bf16[2048,1024]{1,0:T(8,128)(2,1)S(1)} %bitcast.202, bf16[2048,1024]{1,0:T(8,128)(2,1)S(1)} %bitcast.171, bf16[1024,512]{1,0:T(8,128)(2,1)S(1)} %bitcast.179, bf16[512,1024]{1,0:T(8,128)(2,1)S(1)} %bitcast.181, ...), custom_call_target="tpu_custom_call" | custom-call | flops 4294967296 | bytes 14680064 | tf_op jit(solution)/shard_map/hidden_layer/pallas_call | solution.py:752
  146.5 11.9 %collective-permute-done.8.refs_4_ = bf16[512,384]{1,0:T(8,128)(2,1)} collective-permute-done((bf16[512,384]{1,0:T(8,128)(2,1)}, bf16[512,384]{1,0:T(8,128)(2,1)}, u32[]{:S(2)}, u32[]{:S(2)}) %collective-permute-start.8) | collective-permute-done | bytes 393248 | tf_op jit(solution)/shard_map/ppermute | solution.py:532
  163.0 5.0 %all-to-all-start.5 = ((bf16[4,4,128,512]{3,2,1,0:T(8,128)(2,1)}), bf16[4,4,128,512]{3,2,1,0:T(8,128)(2,1)}, u32[]{:S(2)}, u32[]{:S(2)}) async-start(bf16[4,4,128,512]{3,2,1,0:T(8,128)(2,1)} %pack_wide.1), calls=%async_computation.5 | async-start | bytes 4194304 | tf_op jit(solution)/shard_map/all_to_all | solution.py:540
  175.5 46.6 %attention.1 = (bf16[512,512]{1,0:T(8,128)(2,1)S(1)}, bf16[512,512]{1,0:T(8,128)(2,1)S(1)}, bf16[512,512]{1,0:T(8,128)(2,1)S(1)}, bf16[512,512]{1,0:T(8,128)(2,1)S(1)}) custom-call(s32[1]{0:T(128)} %bitcast.1.refs_0_.place_ref, bf16[512,384]{1,0:T(8,128)(2,1)S(1)} %get-tuple-element.89.refs_1_, bf16[512,384]{1,0:T(8,128)(2,1)} %collective-permute-done.6.refs_2_, ...), custom_call_target="tpu_custom_call" | custom-call | flops 9059696640 | bytes 4194304 | tf_op jit(solution)/shard_map/attention/pallas_call | solution.py:443
  228.8 5.8 %fusion.23 = bf16[2048,1024]{1,0:T(8,128)(2,1)} fusion(bf16[2048,512]{1,0:T(8,128)(2,1)S(1)} %get-tuple-element.87, bf16[1024,512]{1,0:T(8,128)(2,1)} %bitcast.178, f32[1024]{0:T(1024)} %bitcast.242), kind=kOutput, calls=%fused_computation.58 | convolution fusion | flops 2149056512 | bytes 7344128 | tf_op jit(solution)/shard_map/nf,df->nd/dot_general | solution.py:904
  237.5 3.9 all-to-all-start.6
  241.4 5.9 %fusion.58 = bf16[2048,1024]{1,0:T(8,128)(2,1)} fusion(bf16[2048,512]{1,0:T(8,128)(2,1)} %copy-done.25, bf16[512,1024]{1,0:T(8,128)(2,1)S(1)} %bitcast.182), kind=kOutput, calls=%fused_computation.154 | convolution fusion | flops 2147483648 | bytes 7340032 | tf_op jit(solution)/shard_map/dot_general | solution.py:906
  248.0 15.4 %collective-permute-done.19 = bf16[512,512]{1,0:T(8,128)(2,1)} collective-permute-done((bf16[512,512]{1,0:T(8,128)(2,1)}, bf16[512,512]{1,0:T(8,128)(2,1)}, u32[]{:S(2)}, u32[]{:S(2)}) %collective-permute-start.19) | collective-permute-done | bytes 524320 | tf_op jit(solution)/shard_map/ppermute | solution.py:532
  263.4 9.1 %collective-permute-done.20 = bf16[512,512]{1,0:T(8,128)(2,1)} collective-permute-done((bf16[512,512]{1,0:T(8,128)(2,1)}, bf16[512,512]{1,0:T(8,128)(2,1)}, u32[]{:S(2)}, u32[]{:S(2)}) %collective-permute-start.20) | collective-permute-done | bytes 524320 | tf_op jit(solution)/shard_map/ppermute | solution.py:532
  279.0 3.4 copy.93
  282.4 3.6 fusion.7
  324.2 3.4 all-to-all-start.7
  331.3 11.4 %collective-permute-done.24 = bf16[2,256,1024]{2,1,0:T(8,128)(2,1)} collective-permute-done((bf16[2,256,1024]{2,1,0:T(8,128)(2,1)}, bf16[2,256,1024]{2,1,0:T(8,128)(2,1)}, u32[]{:S(2)}, u32[]{:S(2)}) %collective-permute-start.24) | collective-permute-done | bytes 1048608 | tf_op jit(solution)/shard_map/ppermute | solution.py:532
  343.1 4.7 %collective-permute-done.22 = bf16[2,256,1024]{2,1,0:T(8,128)(2,1)} collective-permute-done((bf16[2,256,1024]{2,1,0:T(8,128)(2,1)}, bf16[2,256,1024]{2,1,0:T(8,128)(2,1)}, u32[]{:S(2)}, u32[]{:S(2)}) %collective-permute-start.22) | collective-permute-done | bytes 1048608 | tf_op jit(solution)/shard_map/ppermute | solution.py:532
  355.9 11.1 %collective-permute-done.27 = bf16[1,4,64,512]{3,2,1,0:T(8,128)(2,1)S(1)} collective-permute-done((bf16[1,4,64,512]{3,2,1,0:T(8,128)(2,1)S(1)}, bf16[1,4,64,512]{3,2,1,0:T(8,128)(2,1)S(1)}, u32[]{:S(2)}, u32[]{:S(2)}) %collective-permute-start.27) | collective-permute-done | bytes 262176 | tf_op jit(solution)/shard_map/ppermute | solution.py:532
  369.6 3.6 fusion.17
  375.7 3.4 all-to-all-start.8
  384.8 8.1 %collective-permute-done.32.refs_3_ = bf16[4,128,512]{2,1,0:T(8,128)(2,1)S(1)} collective-permute-done((bf16[4,128,512]{2,1,0:T(8,128)(2,1)S(1)}, bf16[4,128,512]{2,1,0:T(8,128)(2,1)S(1)}, u32[]{:S(2)}, u32[]{:S(2)}) %collective-permute-start.32) | collective-permute-done | bytes 524320 | tf_op jit(solution)/shard_map/ppermute | solution.py:532
  405.7 7.6 %collective-permute-done.36 = bf16[1,4,64,512]{3,2,1,0:T(8,128)(2,1)S(1)} collective-permute-done((bf16[1,4,64,512]{3,2,1,0:T(8,128)(2,1)S(1)}, bf16[1,4,64,512]{3,2,1,0:T(8,128)(2,1)S(1)}, u32[]{:S(2)}, u32[]{:S(2)}) %collective-permute-start.36) | collective-permute-done | bytes 262176 | tf_op jit(solution)/shard_map/ppermute | solution.py:532
  413.3 5.1 %collective-permute-done.37 = bf16[1,4,64,512]{3,2,1,0:T(8,128)(2,1)S(1)} collective-permute-done((bf16[1,4,64,512]{3,2,1,0:T(8,128)(2,1)S(1)}, bf16[1,4,64,512]{3,2,1,0:T(8,128)(2,1)S(1)}, u32[]{:S(2)}, u32[]{:S(2)}) %collective-permute-start.37) | collective-permute-done | bytes 262176 | tf_op jit(solution)/shard_map/ppermute | solution.py:532
  (326 shorter events, 179.6 us)
Async XLA Ops:
  2.7 22.1 %collective-permute-start = (bf16[256,1024]{1,0:T(8,128)(2,1)}, bf16[256,1024]{1,0:T(8,128)(2,1)S(1)}, u32[]{:S(2)}, u32[]{:S(2)}) collective-permute-start(bf16[256,1024]{1,0:T(8,128)(2,1)} %dynamic-slice_bitcast_fusion.2), channel_id=1, source_target_pairs={{0,8},{8,0},{16,24},{24,16},{1,9},{9,1},{17,25},{25,17},{2,10},{10... | collective-permute-start | bytes 1572872 | tf_op jit(solution)/shard_map/ppermute | solution.py:532
  4.2 33.5 %collective-permute-start.1 = (bf16[256,1024]{1,0:T(8,128)(2,1)}, bf16[256,1024]{1,0:T(8,128)(2,1)S(1)}, u32[]{:S(2)}, u32[]{:S(2)}) collective-permute-start(bf16[256,1024]{1,0:T(8,128)(2,1)} %dynamic-slice_bitcast_fusion.2), channel_id=1, source_target_pairs={{0,16},{8,24},{16,0},{24,8},{1,17},{9,25},{17,1},{25,9},{2,18},{10... | collective-permute-start | bytes 1572872 | tf_op jit(solution)/shard_map/ppermute | solution.py:532
  5.7 31.9 %collective-permute-start.2 = (bf16[256,1024]{1,0:T(8,128)(2,1)}, bf16[256,1024]{1,0:T(8,128)(2,1)}, u32[]{:S(2)}, u32[]{:S(2)}) collective-permute-start(bf16[256,1024]{1,0:T(8,128)(2,1)} %dynamic-slice_bitcast_fusion.2), channel_id=1, source_target_pairs={{0,24},{8,16},{16,8},{24,0},{1,25},{9,17},{17,9},{25,1},{2,26},{10... | collective-permute-start | bytes 1572872 | tf_op jit(solution)/shard_map/ppermute | solution.py:532
  33.4 23.3 %all-to-all-start.1 = ((bf16[4,256,3,128]{1,3,2,0:T(8,128)(2,1)}), bf16[4,256,3,128]{1,3,2,0:T(8,128)(2,1)}, u32[]{:S(2)}, u32[]{:S(2)}) async-start(bf16[4,256,3,128]{1,3,2,0:T(8,128)(2,1)} %copy.77), calls=%async_computation.1 | async-start | bytes 1572864 | tf_op jit(solution)/shard_map/all_to_all | solution.py:540
  38.5 24.4 %collective-permute-start.9 = (bf16[256,1024]{1,0:T(8,128)(2,1)}, bf16[256,1024]{1,0:T(8,128)(2,1)}, u32[]{:S(2)}, u32[]{:S(2)}) collective-permute-start(bf16[256,1024]{1,0:T(8,128)(2,1)} %constant_dynamic-slice_fusion.4), channel_id=1, source_target_pairs={{0,8},{8,0},{16,24},{24,16},{1,9},{9,1},{17,25},{25,17},{2,10},{10... | collective-permute-start | bytes 1572872 | tf_op jit(solution)/shard_map/ppermute | solution.py:532
  40.4 22.6 %collective-permute-start.10 = (bf16[256,1024]{1,0:T(8,128)(2,1)}, bf16[256,1024]{1,0:T(8,128)(2,1)}, u32[]{:S(2)}, u32[]{:S(2)}) collective-permute-start(bf16[256,1024]{1,0:T(8,128)(2,1)} %constant_dynamic-slice_fusion.4), channel_id=1, source_target_pairs={{0,16},{8,24},{16,0},{24,8},{1,17},{9,25},{17,1},{25,9},{2,18},{10... | collective-permute-start | bytes 1572872 | tf_op jit(solution)/shard_map/ppermute | solution.py:532
  41.9 31.4 %collective-permute-start.11 = (bf16[256,1024]{1,0:T(8,128)(2,1)}, bf16[256,1024]{1,0:T(8,128)(2,1)}, u32[]{:S(2)}, u32[]{:S(2)}) collective-permute-start(bf16[256,1024]{1,0:T(8,128)(2,1)} %constant_dynamic-slice_fusion.4), channel_id=1, source_target_pairs={{0,24},{8,16},{16,8},{24,0},{1,25},{9,17},{17,9},{25,1},{2,26},{10... | collective-permute-start | bytes 1572872 | tf_op jit(solution)/shard_map/ppermute | solution.py:532
  56.6 27.3 %all-to-all-start.2 = ((bf16[4,128,256]{2,1,0:T(8,128)(2,1)}), bf16[4,128,256]{2,1,0:T(8,128)(2,1)S(1)}, u32[]{:S(2)}, u32[]{:S(2)}) async-start(bf16[4,128,256]{2,1,0:T(8,128)(2,1)} %bitcast.223), calls=%async_computation.2 | async-start | bytes 524288 | tf_op jit(solution)/shard_map/all_to_all | solution.py:540
  62.9 21.9 %collective-permute-start.12 = (bf16[256,1024]{1,0:T(8,128)(2,1)}, bf16[256,1024]{1,0:T(8,128)(2,1)S(1)}, u32[]{:S(2)}, u32[]{:S(2)}) collective-permute-start(bf16[256,1024]{1,0:T(8,128)(2,1)} %collective-permute-done.9.refs_1_), channel_id=1, source_target_pairs={{0,1},{1,0},{2,3},{3,2},{4,5},{5,4},{6,7},{7,6},{8,9},{9,8},{10,11... | collective-permute-start | bytes 1572872 | tf_op jit(solution)/shard_map/ppermute | solution.py:532
  63.0 21.8 %collective-permute-start.13 = (bf16[256,1024]{1,0:T(8,128)(2,1)}, bf16[256,1024]{1,0:T(8,128)(2,1)S(1)}, u32[]{:S(2)}, u32[]{:S(2)}) collective-permute-start(bf16[256,1024]{1,0:T(8,128)(2,1)} %collective-permute-done.10.refs_2_), channel_id=1, source_target_pairs={{0,1},{1,0},{2,3},{3,2},{4,5},{5,4},{6,7},{7,6},{8,9},{9,8},{10,11... | collective-permute-start | bytes 1572872 | tf_op jit(solution)/shard_map/ppermute | solution.py:532
  88.8 18.2 %all-to-all-start.3 = ((bf16[4,256,512]{2,1,0:T(8,128)(2,1)}), bf16[4,256,512]{2,1,0:T(8,128)(2,1)S(1)}, u32[]{:S(2)}, u32[]{:S(2)}) async-start(bf16[4,256,512]{2,1,0:T(8,128)(2,1)} %bitcast.210), calls=%async_computation.3 | async-start | bytes 2097152 | tf_op jit(solution)/shard_map/all_to_all | solution.py:540
  107.0 17.5 %all-to-all-start.4 = ((bf16[4,512,256]{2,1,0:T(8,128)(2,1)}), bf16[4,512,256]{2,1,0:T(8,128)(2,1)S(1)}, u32[]{:S(2)}, u32[]{:S(2)}) async-start(bf16[4,512,256]{2,1,0:T(8,128)(2,1)} %bitcast.220), calls=%async_computation.4 | async-start | bytes 2097152 | tf_op jit(solution)/shard_map/all_to_all | solution.py:540
  113.6 27.2 %collective-permute-start.6 = (bf16[512,384]{1,0:T(8,128)(2,1)}, bf16[512,384]{1,0:T(8,128)(2,1)}, u32[]{:S(2)}, u32[]{:S(2)}) collective-permute-start(bf16[512,384]{1,0:T(8,128)(2,1)} %get-tuple-element.155), channel_id=1, source_target_pairs={{0,2},{2,0},{4,6},{6,4},{1,3},{3,1},{5,7},{7,5},{8,10},{10,8},{12,... | collective-permute-start | bytes 1179656 | tf_op jit(solution)/shard_map/ppermute | solution.py:532
  114.0 32.5 %collective-permute-start.7 = (bf16[512,384]{1,0:T(8,128)(2,1)}, bf16[512,384]{1,0:T(8,128)(2,1)}, u32[]{:S(2)}, u32[]{:S(2)}) collective-permute-start(bf16[512,384]{1,0:T(8,128)(2,1)} %get-tuple-element.154), channel_id=1, source_target_pairs={{0,4},{2,6},{4,0},{6,2},{1,5},{3,7},{5,1},{7,3},{8,12},{10,14},{12... | collective-permute-start | bytes 1179656 | tf_op jit(solution)/shard_map/ppermute | solution.py:532
  116.4 41.9 %collective-permute-start.8 = (bf16[512,384]{1,0:T(8,128)(2,1)}, bf16[512,384]{1,0:T(8,128)(2,1)}, u32[]{:S(2)}, u32[]{:S(2)}) collective-permute-start(bf16[512,384]{1,0:T(8,128)(2,1)} %get-tuple-element.153), channel_id=1, source_target_pairs={{0,6},{2,4},{4,2},{6,0},{1,7},{3,5},{5,3},{7,1},{8,14},{10,12},{12... | collective-permute-start | bytes 1179656 | tf_op jit(solution)/shard_map/ppermute | solution.py:532
  119.2 39.1 %collective-permute-start.15 = (bf16[512,128]{1,0:T(8,128)(2,1)}, bf16[512,128]{1,0:T(8,128)(2,1)}, u32[]{:S(2)}, u32[]{:S(2)}) collective-permute-start(bf16[512,128]{1,0:T(8,128)(2,1)} %get-tuple-element.161), channel_id=1, source_target_pairs={{0,2},{2,0},{4,6},{6,4},{1,3},{3,1},{5,7},{7,5},{8,10},{10,8},{12,... | collective-permute-start | bytes 393224 | tf_op jit(solution)/shard_map/ppermute | solution.py:532
  120.5 39.5 %collective-permute-start.16 = (bf16[512,128]{1,0:T(8,128)(2,1)}, bf16[512,128]{1,0:T(8,128)(2,1)}, u32[]{:S(2)}, u32[]{:S(2)}) collective-permute-start(bf16[512,128]{1,0:T(8,128)(2,1)} %get-tuple-element.160), channel_id=1, source_target_pairs={{0,4},{2,6},{4,0},{6,2},{1,5},{3,7},{5,1},{7,3},{8,12},{10,14},{12... | collective-permute-start | bytes 393224 | tf_op jit(solution)/shard_map/ppermute | solution.py:532
  140.8 21.5 %collective-permute-start.17 = (bf16[512,128]{1,0:T(8,128)(2,1)S(1)}, bf16[512,128]{1,0:T(8,128)(2,1)S(1)}, u32[]{:S(2)}, u32[]{:S(2)}) collective-permute-start(bf16[512,128]{1,0:T(8,128)(2,1)S(1)} %copy-done.56), channel_id=1, source_target_pairs={{0,6},{2,4},{4,2},{6,0},{1,7},{3,5},{5,3},{7,1},{8,14},{10,12},{12... | collective-permute-start | bytes 393224 | tf_op jit(solution)/shard_map/ppermute | solution.py:532
  163.0 62.4 %all-to-all-start.5 = ((bf16[4,4,128,512]{3,2,1,0:T(8,128)(2,1)}), bf16[4,4,128,512]{3,2,1,0:T(8,128)(2,1)}, u32[]{:S(2)}, u32[]{:S(2)}) async-start(bf16[4,4,128,512]{3,2,1,0:T(8,128)(2,1)} %pack_wide.1), calls=%async_computation.5 | async-start | bytes 4194304 | tf_op jit(solution)/shard_map/all_to_all | solution.py:540
  225.3 22.7 %collective-permute-start.18 = (bf16[512,512]{1,0:T(8,128)(2,1)}, bf16[512,512]{1,0:T(8,128)(2,1)}, u32[]{:S(2)}, u32[]{:S(2)}) collective-permute-start(bf16[512,512]{1,0:T(8,128)(2,1)} %copy-done.22), channel_id=1, source_target_pairs={{0,2},{2,0},{4,6},{6,4},{1,3},{3,1},{5,7},{7,5},{8,10},{10,8},{12,... | collective-permute-start | bytes 1572872 | tf_op jit(solution)/shard_map/ppermute | solution.py:532
  225.4 38.1 %collective-permute-start.19 = (bf16[512,512]{1,0:T(8,128)(2,1)}, bf16[512,512]{1,0:T(8,128)(2,1)}, u32[]{:S(2)}, u32[]{:S(2)}) collective-permute-start(bf16[512,512]{1,0:T(8,128)(2,1)} %copy-done.21), channel_id=1, source_target_pairs={{0,4},{2,6},{4,0},{6,2},{1,5},{3,7},{5,1},{7,3},{8,12},{10,14},{12... | collective-permute-start | bytes 1572872 | tf_op jit(solution)/shard_map/ppermute | solution.py:532
  228.2 44.3 %collective-permute-start.20 = (bf16[512,512]{1,0:T(8,128)(2,1)}, bf16[512,512]{1,0:T(8,128)(2,1)}, u32[]{:S(2)}, u32[]{:S(2)}) collective-permute-start(bf16[512,512]{1,0:T(8,128)(2,1)} %copy-done.20), channel_id=1, source_target_pairs={{0,6},{2,4},{4,2},{6,0},{1,7},{3,5},{5,3},{7,1},{8,14},{10,12},{12... | collective-permute-start | bytes 1572872 | tf_op jit(solution)/shard_map/ppermute | solution.py:532
  301.3 65.7 %collective-permute-start.28 = (bf16[4,128,512]{2,1,0:T(8,128)(2,1)S(1)}, bf16[4,128,512]{2,1,0:T(8,128)(2,1)S(1)}, u32[]{:S(2)}, u32[]{:S(2)}) collective-permute-start(bf16[4,128,512]{2,1,0:T(8,128)(2,1)S(1)} %all-to-all-done.6.refs_0_), channel_id=1, source_target_pairs={{0,2},{2,0},{4,6},{6,4},{1,3},{3,1},{5,7},{7,5},{8,10},{10,8},{12,... | collective-permute-start | bytes 1572872 | tf_op jit(solution)/shard_map/ppermute | solution.py:532
  301.4 66.3 %collective-permute-start.29 = (bf16[4,128,512]{2,1,0:T(8,128)(2,1)S(1)}, bf16[4,128,512]{2,1,0:T(8,128)(2,1)S(1)}, u32[]{:S(2)}, u32[]{:S(2)}) collective-permute-start(bf16[4,128,512]{2,1,0:T(8,128)(2,1)S(1)} %all-to-all-done.6.refs_0_), channel_id=1, source_target_pairs={{0,4},{2,6},{4,0},{6,2},{1,5},{3,7},{5,1},{7,3},{8,12},{10,14},{12... | collective-permute-start | bytes 1572872 | tf_op jit(solution)/shard_map/ppermute | solution.py:532
  314.8 27.9 %collective-permute-start.24 = (bf16[2,256,1024]{2,1,0:T(8,128)(2,1)}, bf16[2,256,1024]{2,1,0:T(8,128)(2,1)}, u32[]{:S(2)}, u32[]{:S(2)}) collective-permute-start(bf16[2,256,1024]{2,1,0:T(8,128)(2,1)} %slice.162), channel_id=1, source_target_pairs={{0,8},{8,0},{16,24},{24,16},{1,9},{9,1},{17,25},{25,17},{2,10},{10... | collective-permute-start | bytes 3145736 | tf_op jit(solution)/shard_map/ppermute | solution.py:532
  319.9 27.8 %collective-permute-start.22 = (bf16[2,256,1024]{2,1,0:T(8,128)(2,1)}, bf16[2,256,1024]{2,1,0:T(8,128)(2,1)}, u32[]{:S(2)}, u32[]{:S(2)}) collective-permute-start(bf16[2,256,1024]{2,1,0:T(8,128)(2,1)} %slice.194), channel_id=1, source_target_pairs={{0,16},{8,24},{16,0},{24,8},{1,17},{9,25},{17,1},{25,9},{2,18},{10... | collective-permute-start | bytes 3145736 | tf_op jit(solution)/shard_map/ppermute | solution.py:532
  324.2 43.5 %all-to-all-start.7 = ((f32[32,1,2176]{2,1,0:T(1,128)}), f32[32,1,2176]{2,1,0:T(1,128)}, u32[]{:S(2)}, u32[]{:S(2)}) async-start(f32[32,1,2176]{2,1,0:T(1,128)} %reshape.295), calls=%async_computation.7 | async-start | bytes 557056 | tf_op jit(solution)/shard_map/all_to_all | solution.py:540
  331.0 23.4 %collective-permute-start.25 = (bf16[1,4,64,512]{3,2,1,0:T(8,128)(2,1)S(1)}, bf16[1,4,64,512]{3,2,1,0:T(8,128)(2,1)S(1)}, u32[]{:S(2)}, u32[]{:S(2)}) collective-permute-start(bf16[1,4,64,512]{3,2,1,0:T(8,128)(2,1)S(1)} %get-tuple-element.115), channel_id=1, source_target_pairs={{0,2},{2,0},{4,6},{6,4},{1,3},{3,1},{5,7},{7,5},{8,10},{10,8},{12,... | collective-permute-start | bytes 786440 | tf_op jit(solution)/shard_map/ppermute | solution.py:532
  373.2 19.8 %collective-permute-start.33 = (f32[256,1024]{1,0:T(8,128)}, f32[256,1024]{1,0:T(8,128)}, u32[]{:S(2)}, u32[]{:S(2)}) collective-permute-start(f32[256,1024]{1,0:T(8,128)} %get-tuple-element.158), channel_id=1, source_target_pairs={{0,1},{1,0},{2,3},{3,2},{4,5},{5,4},{6,7},{7,6},{8,9},{9,8},{10,11... | collective-permute-start | bytes 3145736 | tf_op jit(solution)/shard_map/ppermute | solution.py:532
  373.2 19.8 %collective-permute-start.34 = (f32[256,1024]{1,0:T(8,128)}, f32[256,1024]{1,0:T(8,128)}, u32[]{:S(2)}, u32[]{:S(2)}) collective-permute-start(f32[256,1024]{1,0:T(8,128)} %get-tuple-element.157), channel_id=1, source_target_pairs={{0,1},{1,0},{2,3},{3,2},{4,5},{5,4},{6,7},{7,6},{8,9},{9,8},{10,11... | collective-permute-start | bytes 3145736 | tf_op jit(solution)/shard_map/ppermute | solution.py:532
  393.3 20.1 %collective-permute-start.36 = (bf16[1,4,64,512]{3,2,1,0:T(8,128)(2,1)S(1)}, bf16[1,4,64,512]{3,2,1,0:T(8,128)(2,1)S(1)}, u32[]{:S(2)}, u32[]{:S(2)}) collective-permute-start(bf16[1,4,64,512]{3,2,1,0:T(8,128)(2,1)S(1)} %bitcast.186), channel_id=1, source_target_pairs={{0,4},{2,6},{4,0},{6,2},{1,5},{3,7},{5,1},{7,3},{8,12},{10,14},{12... | collective-permute-start | bytes 786440 | tf_op jit(solution)/shard_map/ppermute | solution.py:532
  395.3 23.1 %collective-permute-start.37 = (bf16[1,4,64,512]{3,2,1,0:T(8,128)(2,1)S(1)}, bf16[1,4,64,512]{3,2,1,0:T(8,128)(2,1)S(1)}, u32[]{:S(2)}, u32[]{:S(2)}) collective-permute-start(bf16[1,4,64,512]{3,2,1,0:T(8,128)(2,1)S(1)} %bitcast.187), channel_id=1, source_target_pairs={{0,6},{2,4},{4,2},{6,0},{1,7},{3,5},{5,3},{7,1},{8,14},{10,12},{12... | collective-permute-start | bytes 786440 | tf_op jit(solution)/shard_map/ppermute | solution.py:532
  (85 other events, 778.2 us)

commit v4 on v3

--- a/solution.py
+++ b/solution.py
@@ -847,8 +847,6 @@
     up_send = up_weight.reshape(-1, size, hidden).transpose(1, 0, 2)
     up_w = swap(after(up_send, output_w, first, cot_b), "fsdp")
     up_w = up_w.reshape(model, hidden)
-    down_w = swap(after(down_weight, up_w).reshape(size, hidden, -1), "fsdp")
-    down_w = down_w.transpose(1, 0, 2).reshape(hidden, model)
 
 
     lane = jnp.arange(width, dtype=jnp.int32) % HD
@@ -882,6 +880,8 @@
         for flip in range(depth):
             block = pick(tensor, me ^ place ^ flip, count)
             blocks.append(partner(block, "ctx", flip) if flip else block)
+    down_w = swap(after(down_weight, up_w, blocks[2]).reshape(size, hidden, -1), "fsdp")
+    down_w = down_w.transpose(1, 0, 2).reshape(hidden, model)
     second, up_w = lax.optimization_barrier((second, up_w, sending))[:2]
 
     activated, d_upper_b, grad_up_b = hidden_layer(second, cot_b, up_w, down_w, up_bias)

time: 429 us -> 418 us (0.974)
  waiting for transfers between devices: 115 us -> 105 us
  matrix products: 43.4 us -> 38.2 us
    all_to_all x9, waiting for transfers between devices: 14.7 us -> 8.23 us  [swap(): return lax.all_to_all(tensor, axis, 0, 0)]
    unnamed x152 -> x150, local copies, waits for them, and re-layouts: 35.2 us -> 33.5 us
  transfers between devices with their start and end apart: 47 -> 47, of which waited for: 19 -> 14; matrix products, arithmetic and copies ran while one was open for 27% -> 27% of each run, Pallas kernels for 15% -> 15%
where the time goes in v4:
time: 418 us; the launch traced here: 410 us
  waiting for transfers between devices  105 us (25%)
  starting transfers between devices  75.4 us (18%)
  local copies, waits for them, and re-layouts  73.2 us (18%)
  Pallas kernels  66.6 us (16%)
  other arithmetic  49.3 us (12%)
  matrix products  38.2 us (9%)
    ppermute x38, waiting for transfers between devices, partner(): return lax.ppermute(tensor, axis, [(s, s ^ flip) for s in range(size)])  97.2 us
    pallas_call x1, Pallas kernels, attention(): pl.pallas_call(lambda *refs: attention_body(heads, flips, *refs), grid_sp...  46.5 us
    all_to_all x9, starting transfers between devices, swap(): return lax.all_to_all(tensor, axis, 0, 0)  40.7 us
    ppermute x38, starting transfers between devices, partner(): return lax.ppermute(tensor, axis, [(s, s ^ flip) for s in range(size)])  34.7 us
    unnamed x150, local copies, waits for them, and re-layouts  33.5 us
  transfers between devices with their start and end apart: 47, of which 14 were waited for; matrix products, arithmetic and copies ran while one was open for 27% of the time, Pallas kernels for 15%

profile of v4, /device:TPU:8, one launch (start us, length us, event | category | flops | bytes accessed | tf_op | source)
XLA Modules:
  0.0 410.0 jit_solution(2538230870612191293)
XLA Ops:
  13.3 7.2 %all-to-all-start = ((f32[16,1,2560]{2,1,0:T(1,128)}), f32[16,1,2560]{2,1,0:T(1,128)S(1)}, u32[]{:S(2)}, u32[]{:S(2)}) async-start(f32[16,1,2560]{2,1,0:T(1,128)} %broadcast_in_dim.66), calls=%async_computation | async-start | bytes 327680 | tf_op jit(solution)/shard_map/all_to_all | solution.py:540
  26.1 4.6 %all-to-all-done = f32[16,1,2560]{2,1,0:T(1,128)S(1)} async-done(((f32[16,1,2560]{2,1,0:T(1,128)}), f32[16,1,2560]{2,1,0:T(1,128)S(1)}, u32[]{:S(2)}, u32[]{:S(2)}) %all-to-all-start) | async-done | bytes 163872 | tf_op jit(solution)/shard_map/all_to_all | solution.py:540
  33.4 4.2 %all-to-all-start.1 = ((bf16[4,256,3,128]{1,3,2,0:T(8,128)(2,1)}), bf16[4,256,3,128]{1,3,2,0:T(8,128)(2,1)}, u32[]{:S(2)}, u32[]{:S(2)}) async-start(bf16[4,256,3,128]{1,3,2,0:T(8,128)(2,1)} %copy.77), calls=%async_computation.1 | async-start | bytes 1572864 | tf_op jit(solution)/shard_map/all_to_all | solution.py:540
  42.9 5.6 %norm_rows.1 = (bf16[4,2,256,1024]{3,2,1,0:T(8,128)(2,1)S(1)}, bf16[4,2,256,1024]{3,2,1,0:T(8,128)(2,1)S(1)}, bf16[4,2,256,1024]{3,2,1,0:T(8,128)(2,1)S(1)}) custom-call(s32[1]{0:T(128)} %bitcast.2.core_ref, bf16[512,1024]{1,0:T(8,128)(2,1)S(1)} %bitcast.173, bf16[256,1024]{1,0:T(8,128)(2,1)S(1)} %collective-permute-done.refs_1_, ...), custom_call_target="tpu_custom_call" | custom-call | flops 20971520 | bytes 16777216 | tf_op jit(solution)/shard_map/norm_rows/pallas_call | solution.py:508
  54.6 4.3 %all-to-all-start.2 = ((bf16[4,128,256]{2,1,0:T(8,128)(2,1)}), bf16[4,128,256]{2,1,0:T(8,128)(2,1)S(1)}, u32[]{:S(2)}, u32[]{:S(2)}) async-start(bf16[4,128,256]{2,1,0:T(8,128)(2,1)} %bitcast.222), calls=%async_computation.2 | async-start | bytes 524288 | tf_op jit(solution)/shard_map/all_to_all | solution.py:540
  67.3 6.0 %collective-permute-done.11.refs_3_ = bf16[256,1024]{1,0:T(8,128)(2,1)} collective-permute-done((bf16[256,1024]{1,0:T(8,128)(2,1)}, bf16[256,1024]{1,0:T(8,128)(2,1)}, u32[]{:S(2)}, u32[]{:S(2)}) %collective-permute-start.11) | collective-permute-done | bytes 524320 | tf_op jit(solution)/shard_map/ppermute | solution.py:532
  73.3 5.8 %fusion.33 = (bf16[2048,128]{1,0:T(8,128)(2,1)}, bf16[2048,128]{1,0:T(8,128)(2,1)}, f32[2048,128]{1,0:T(8,128)}, f32[2048,128]{1,0:T(8,128)}) fusion(f32[2048,256]{1,0:T(8,128)S(1)} %convolution_add_fusion.1, f32[2048,384]{1,0:T(8,128)S(1)} %convolution_add_fusion, f32[128]{0:T(128)S(1)} %get-tuple-element.180, f32[128]{0:T(128)S(1)} %get-tuple-element.181, ...), kind=kLoop, calls=%fused_computation.76 | loop fusion | flops 2883584 | bytes 7349248 | tf_op jit(solution)/shard_map/convert.8 | solution.py:1088
  84.7 3.6 all-to-all-start.3
  93.3 17.2 %collective-permute-done.7.refs_3_ = bf16[512,384]{1,0:T(8,128)(2,1)S(1)} collective-permute-done((bf16[512,384]{1,0:T(8,128)(2,1)S(1)}, bf16[512,384]{1,0:T(8,128)(2,1)S(1)}, u32[]{:S(2)}, u32[]{:S(2)}) %collective-permute-start.7) | collective-permute-done | bytes 393248 | tf_op jit(solution)/shard_map/ppermute | solution.py:532
  110.5 4.5 %all-to-all-start.4 = ((bf16[4,512,256]{2,1,0:T(8,128)(2,1)}), bf16[4,512,256]{2,1,0:T(8,128)(2,1)}, u32[]{:S(2)}, u32[]{:S(2)}) async-start(bf16[4,512,256]{2,1,0:T(8,128)(2,1)} %bitcast.219), calls=%async_computation.4 | async-start | bytes 2097152 | tf_op jit(solution)/shard_map/all_to_all | solution.py:540
  120.5 3.4 convolution_convert_fusion
  135.4 6.2 %hidden_layer.1 = (bf16[2048,512]{1,0:T(8,128)(2,1)S(1)}, bf16[2048,512]{1,0:T(8,128)(2,1)S(1)}, f32[1,512]{1,0:T(1,128)S(1)}) custom-call(bf16[2048,1024]{1,0:T(8,128)(2,1)S(1)} %bitcast.202, bf16[2048,1024]{1,0:T(8,128)(2,1)S(1)} %bitcast.171, bf16[1024,512]{1,0:T(8,128)(2,1)S(1)} %bitcast.179, bf16[512,1024]{1,0:T(8,128)(2,1)S(1)} %bitcast.181, ...), custom_call_target="tpu_custom_call" | custom-call | flops 4294967296 | bytes 14680064 | tf_op jit(solution)/shard_map/hidden_layer/pallas_call | solution.py:752
  142.3 3.2 fusion.6
  149.8 6.6 %all-to-all-start.5 = ((bf16[4,4,128,512]{3,2,1,0:T(8,128)(2,1)}), bf16[4,4,128,512]{3,2,1,0:T(8,128)(2,1)}, u32[]{:S(2)}, u32[]{:S(2)}) async-start(bf16[4,4,128,512]{3,2,1,0:T(8,128)(2,1)} %pack_wide.1), calls=%async_computation.5 | async-start | bytes 4194304 | tf_op jit(solution)/shard_map/all_to_all | solution.py:540
  164.0 46.5 %attention.1 = (bf16[512,512]{1,0:T(8,128)(2,1)S(1)}, bf16[512,512]{1,0:T(8,128)(2,1)S(1)}, bf16[512,512]{1,0:T(8,128)(2,1)S(1)}, bf16[512,512]{1,0:T(8,128)(2,1)S(1)}) custom-call(s32[1]{0:T(128)} %bitcast.1.refs_0_.place_ref, bf16[512,384]{1,0:T(8,128)(2,1)S(1)} %get-tuple-element.89.refs_1_, bf16[512,384]{1,0:T(8,128)(2,1)} %collective-permute-done.6.refs_2_, ...), custom_call_target="tpu_custom_call" | custom-call | flops 9059696640 | bytes 4194304 | tf_op jit(solution)/shard_map/attention/pallas_call | solution.py:443
  217.2 5.8 %fusion.23 = bf16[2048,1024]{1,0:T(8,128)(2,1)} fusion(bf16[2048,512]{1,0:T(8,128)(2,1)S(1)} %get-tuple-element.87, bf16[1024,512]{1,0:T(8,128)(2,1)} %bitcast.178, f32[1024]{0:T(1024)} %bitcast.241), kind=kOutput, calls=%fused_computation.58 | convolution fusion | flops 2149056512 | bytes 7344128 | tf_op jit(solution)/shard_map/nf,df->nd/dot_general | solution.py:904
  225.9 3.5 all-to-all-start.6
  229.4 5.9 %fusion.58 = bf16[2048,1024]{1,0:T(8,128)(2,1)} fusion(bf16[2048,512]{1,0:T(8,128)(2,1)} %copy-done.25, bf16[512,1024]{1,0:T(8,128)(2,1)S(1)} %bitcast.182), kind=kOutput, calls=%fused_computation.154 | convolution fusion | flops 2147483648 | bytes 7340032 | tf_op jit(solution)/shard_map/dot_general | solution.py:906
  236.0 15.8 %collective-permute-done.19 = bf16[512,512]{1,0:T(8,128)(2,1)} collective-permute-done((bf16[512,512]{1,0:T(8,128)(2,1)}, bf16[512,512]{1,0:T(8,128)(2,1)}, u32[]{:S(2)}, u32[]{:S(2)}) %collective-permute-start.19) | collective-permute-done | bytes 524320 | tf_op jit(solution)/shard_map/ppermute | solution.py:532
  251.8 9.7 %collective-permute-done.20 = bf16[512,512]{1,0:T(8,128)(2,1)} collective-permute-done((bf16[512,512]{1,0:T(8,128)(2,1)}, bf16[512,512]{1,0:T(8,128)(2,1)}, u32[]{:S(2)}, u32[]{:S(2)}) %collective-permute-start.20) | collective-permute-done | bytes 524320 | tf_op jit(solution)/shard_map/ppermute | solution.py:532
  267.9 3.4 copy.93
  271.3 3.6 fusion.7
  312.7 3.4 all-to-all-start.7
  316.1 3.2 convolution_convert_fusion.2
  319.8 11.9 %collective-permute-done.24 = bf16[2,256,1024]{2,1,0:T(8,128)(2,1)} collective-permute-done((bf16[2,256,1024]{2,1,0:T(8,128)(2,1)}, bf16[2,256,1024]{2,1,0:T(8,128)(2,1)}, u32[]{:S(2)}, u32[]{:S(2)}) %collective-permute-start.24) | collective-permute-done | bytes 1048608 | tf_op jit(solution)/shard_map/ppermute | solution.py:532
  332.0 4.7 %collective-permute-done.22 = bf16[2,256,1024]{2,1,0:T(8,128)(2,1)} collective-permute-done((bf16[2,256,1024]{2,1,0:T(8,128)(2,1)}, bf16[2,256,1024]{2,1,0:T(8,128)(2,1)}, u32[]{:S(2)}, u32[]{:S(2)}) %collective-permute-start.22) | collective-permute-done | bytes 1048608 | tf_op jit(solution)/shard_map/ppermute | solution.py:532
  344.8 11.1 %collective-permute-done.27 = bf16[1,4,64,512]{3,2,1,0:T(8,128)(2,1)S(1)} collective-permute-done((bf16[1,4,64,512]{3,2,1,0:T(8,128)(2,1)S(1)}, bf16[1,4,64,512]{3,2,1,0:T(8,128)(2,1)S(1)}, u32[]{:S(2)}, u32[]{:S(2)}) %collective-permute-start.27) | collective-permute-done | bytes 262176 | tf_op jit(solution)/shard_map/ppermute | solution.py:532
  358.6 3.6 fusion.17
  364.6 3.4 all-to-all-start.8
  373.8 8.1 %collective-permute-done.32.refs_3_ = bf16[4,128,512]{2,1,0:T(8,128)(2,1)S(1)} collective-permute-done((bf16[4,128,512]{2,1,0:T(8,128)(2,1)S(1)}, bf16[4,128,512]{2,1,0:T(8,128)(2,1)S(1)}, u32[]{:S(2)}, u32[]{:S(2)}) %collective-permute-start.32) | collective-permute-done | bytes 524320 | tf_op jit(solution)/shard_map/ppermute | solution.py:532
  394.7 7.6 %collective-permute-done.36 = bf16[1,4,64,512]{3,2,1,0:T(8,128)(2,1)S(1)} collective-permute-done((bf16[1,4,64,512]{3,2,1,0:T(8,128)(2,1)S(1)}, bf16[1,4,64,512]{3,2,1,0:T(8,128)(2,1)S(1)}, u32[]{:S(2)}, u32[]{:S(2)}) %collective-permute-start.36) | collective-permute-done | bytes 262176 | tf_op jit(solution)/shard_map/ppermute | solution.py:532
  402.2 5.1 %collective-permute-done.37 = bf16[1,4,64,512]{3,2,1,0:T(8,128)(2,1)S(1)} collective-permute-done((bf16[1,4,64,512]{3,2,1,0:T(8,128)(2,1)S(1)}, bf16[1,4,64,512]{3,2,1,0:T(8,128)(2,1)S(1)}, u32[]{:S(2)}, u32[]{:S(2)}) %collective-permute-start.37) | collective-permute-done | bytes 262176 | tf_op jit(solution)/shard_map/ppermute | solution.py:532
  (324 shorter events, 169.4 us)
Async XLA Ops:
  2.7 34.9 %collective-permute-start = (bf16[256,1024]{1,0:T(8,128)(2,1)}, bf16[256,1024]{1,0:T(8,128)(2,1)S(1)}, u32[]{:S(2)}, u32[]{:S(2)}) collective-permute-start(bf16[256,1024]{1,0:T(8,128)(2,1)} %dynamic-slice_bitcast_fusion.2), channel_id=1, source_target_pairs={{0,8},{8,0},{16,24},{24,16},{1,9},{9,1},{17,25},{25,17},{2,10},{10... | collective-permute-start | bytes 1572872 | tf_op jit(solution)/shard_map/ppermute | solution.py:532
  4.2 33.5 %collective-permute-start.1 = (bf16[256,1024]{1,0:T(8,128)(2,1)}, bf16[256,1024]{1,0:T(8,128)(2,1)S(1)}, u32[]{:S(2)}, u32[]{:S(2)}) collective-permute-start(bf16[256,1024]{1,0:T(8,128)(2,1)} %dynamic-slice_bitcast_fusion.2), channel_id=1, source_target_pairs={{0,16},{8,24},{16,0},{24,8},{1,17},{9,25},{17,1},{25,9},{2,18},{10... | collective-permute-start | bytes 1572872 | tf_op jit(solution)/shard_map/ppermute | solution.py:532
  5.7 32.5 %collective-permute-start.2 = (bf16[256,1024]{1,0:T(8,128)(2,1)}, bf16[256,1024]{1,0:T(8,128)(2,1)}, u32[]{:S(2)}, u32[]{:S(2)}) collective-permute-start(bf16[256,1024]{1,0:T(8,128)(2,1)} %dynamic-slice_bitcast_fusion.2), channel_id=1, source_target_pairs={{0,24},{8,16},{16,8},{24,0},{1,25},{9,17},{17,9},{25,1},{2,26},{10... | collective-permute-start | bytes 1572872 | tf_op jit(solution)/shard_map/ppermute | solution.py:532
  13.3 17.5 %all-to-all-start = ((f32[16,1,2560]{2,1,0:T(1,128)}), f32[16,1,2560]{2,1,0:T(1,128)S(1)}, u32[]{:S(2)}, u32[]{:S(2)}) async-start(f32[16,1,2560]{2,1,0:T(1,128)} %broadcast_in_dim.66), calls=%async_computation | async-start | bytes 327680 | tf_op jit(solution)/shard_map/all_to_all | solution.py:540
  33.4 21.3 %all-to-all-start.1 = ((bf16[4,256,3,128]{1,3,2,0:T(8,128)(2,1)}), bf16[4,256,3,128]{1,3,2,0:T(8,128)(2,1)}, u32[]{:S(2)}, u32[]{:S(2)}) async-start(bf16[4,256,3,128]{1,3,2,0:T(8,128)(2,1)} %copy.77), calls=%async_computation.1 | async-start | bytes 1572864 | tf_op jit(solution)/shard_map/all_to_all | solution.py:540
  39.1 23.8 %collective-permute-start.9 = (bf16[256,1024]{1,0:T(8,128)(2,1)}, bf16[256,1024]{1,0:T(8,128)(2,1)}, u32[]{:S(2)}, u32[]{:S(2)}) collective-permute-start(bf16[256,1024]{1,0:T(8,128)(2,1)} %constant_dynamic-slice_fusion.4), channel_id=1, source_target_pairs={{0,8},{8,0},{16,24},{24,16},{1,9},{9,1},{17,25},{25,17},{2,10},{10... | collective-permute-start | bytes 1572872 | tf_op jit(solution)/shard_map/ppermute | solution.py:532
  41.2 23.1 %collective-permute-start.10 = (bf16[256,1024]{1,0:T(8,128)(2,1)}, bf16[256,1024]{1,0:T(8,128)(2,1)}, u32[]{:S(2)}, u32[]{:S(2)}) collective-permute-start(bf16[256,1024]{1,0:T(8,128)(2,1)} %constant_dynamic-slice_fusion.4), channel_id=1, source_target_pairs={{0,16},{8,24},{16,0},{24,8},{1,17},{9,25},{17,1},{25,9},{2,18},{10... | collective-permute-start | bytes 1572872 | tf_op jit(solution)/shard_map/ppermute | solution.py:532
  42.7 30.5 %collective-permute-start.11 = (bf16[256,1024]{1,0:T(8,128)(2,1)}, bf16[256,1024]{1,0:T(8,128)(2,1)}, u32[]{:S(2)}, u32[]{:S(2)}) collective-permute-start(bf16[256,1024]{1,0:T(8,128)(2,1)} %constant_dynamic-slice_fusion.4), channel_id=1, source_target_pairs={{0,24},{8,16},{16,8},{24,0},{1,25},{9,17},{17,9},{25,1},{2,26},{10... | collective-permute-start | bytes 1572872 | tf_op jit(solution)/shard_map/ppermute | solution.py:532
  54.6 25.2 %all-to-all-start.2 = ((bf16[4,128,256]{2,1,0:T(8,128)(2,1)}), bf16[4,128,256]{2,1,0:T(8,128)(2,1)S(1)}, u32[]{:S(2)}, u32[]{:S(2)}) async-start(bf16[4,128,256]{2,1,0:T(8,128)(2,1)} %bitcast.222), calls=%async_computation.2 | async-start | bytes 524288 | tf_op jit(solution)/shard_map/all_to_all | solution.py:540
  62.9 17.8 %collective-permute-start.12 = (bf16[256,1024]{1,0:T(8,128)(2,1)}, bf16[256,1024]{1,0:T(8,128)(2,1)S(1)}, u32[]{:S(2)}, u32[]{:S(2)}) collective-permute-start(bf16[256,1024]{1,0:T(8,128)(2,1)} %collective-permute-done.9.refs_1_), channel_id=1, source_target_pairs={{0,1},{1,0},{2,3},{3,2},{4,5},{5,4},{6,7},{7,6},{8,9},{9,8},{10,11... | collective-permute-start | bytes 1572872 | tf_op jit(solution)/shard_map/ppermute | solution.py:532
  84.7 25.7 %all-to-all-start.3 = ((bf16[4,256,512]{2,1,0:T(8,128)(2,1)}), bf16[4,256,512]{2,1,0:T(8,128)(2,1)S(1)}, u32[]{:S(2)}, u32[]{:S(2)}) async-start(bf16[4,256,512]{2,1,0:T(8,128)(2,1)} %bitcast.210), calls=%async_computation.3 | async-start | bytes 2097152 | tf_op jit(solution)/shard_map/all_to_all | solution.py:540
  90.7 19.7 %collective-permute-start.7 = (bf16[512,384]{1,0:T(8,128)(2,1)S(1)}, bf16[512,384]{1,0:T(8,128)(2,1)S(1)}, u32[]{:S(2)}, u32[]{:S(2)}) collective-permute-start(bf16[512,384]{1,0:T(8,128)(2,1)S(1)} %get-tuple-element.154), channel_id=1, source_target_pairs={{0,4},{2,6},{4,0},{6,2},{1,5},{3,7},{5,1},{7,3},{8,12},{10,14},{12... | collective-permute-start | bytes 1179656 | tf_op jit(solution)/shard_map/ppermute | solution.py:532
  110.5 18.7 %all-to-all-start.4 = ((bf16[4,512,256]{2,1,0:T(8,128)(2,1)}), bf16[4,512,256]{2,1,0:T(8,128)(2,1)}, u32[]{:S(2)}, u32[]{:S(2)}) async-start(bf16[4,512,256]{2,1,0:T(8,128)(2,1)} %bitcast.219), calls=%async_computation.4 | async-start | bytes 2097152 | tf_op jit(solution)/shard_map/all_to_all | solution.py:540
  116.6 33.2 %collective-permute-start.6 = (bf16[512,384]{1,0:T(8,128)(2,1)}, bf16[512,384]{1,0:T(8,128)(2,1)}, u32[]{:S(2)}, u32[]{:S(2)}) collective-permute-start(bf16[512,384]{1,0:T(8,128)(2,1)} %get-tuple-element.155), channel_id=1, source_target_pairs={{0,2},{2,0},{4,6},{6,4},{1,3},{3,1},{5,7},{7,5},{8,10},{10,8},{12,... | collective-permute-start | bytes 1179656 | tf_op jit(solution)/shard_map/ppermute | solution.py:532
  118.1 31.7 %collective-permute-start.8 = (bf16[512,384]{1,0:T(8,128)(2,1)}, bf16[512,384]{1,0:T(8,128)(2,1)}, u32[]{:S(2)}, u32[]{:S(2)}) collective-permute-start(bf16[512,384]{1,0:T(8,128)(2,1)} %get-tuple-element.153), channel_id=1, source_target_pairs={{0,6},{2,4},{4,2},{6,0},{1,7},{3,5},{5,3},{7,1},{8,14},{10,12},{12... | collective-permute-start | bytes 1179656 | tf_op jit(solution)/shard_map/ppermute | solution.py:532
  124.8 25.0 %collective-permute-start.15 = (bf16[512,128]{1,0:T(8,128)(2,1)}, bf16[512,128]{1,0:T(8,128)(2,1)}, u32[]{:S(2)}, u32[]{:S(2)}) collective-permute-start(bf16[512,128]{1,0:T(8,128)(2,1)} %get-tuple-element.161), channel_id=1, source_target_pairs={{0,2},{2,0},{4,6},{6,4},{1,3},{3,1},{5,7},{7,5},{8,10},{10,8},{12,... | collective-permute-start | bytes 393224 | tf_op jit(solution)/shard_map/ppermute | solution.py:532
  125.8 24.0 %collective-permute-start.16 = (bf16[512,128]{1,0:T(8,128)(2,1)}, bf16[512,128]{1,0:T(8,128)(2,1)}, u32[]{:S(2)}, u32[]{:S(2)}) collective-permute-start(bf16[512,128]{1,0:T(8,128)(2,1)} %get-tuple-element.160), channel_id=1, source_target_pairs={{0,4},{2,6},{4,0},{6,2},{1,5},{3,7},{5,1},{7,3},{8,12},{10,14},{12... | collective-permute-start | bytes 393224 | tf_op jit(solution)/shard_map/ppermute | solution.py:532
  126.3 23.5 %collective-permute-start.17 = (bf16[512,128]{1,0:T(8,128)(2,1)}, bf16[512,128]{1,0:T(8,128)(2,1)}, u32[]{:S(2)}, u32[]{:S(2)}) collective-permute-start(bf16[512,128]{1,0:T(8,128)(2,1)} %get-tuple-element.159), channel_id=1, source_target_pairs={{0,6},{2,4},{4,2},{6,0},{1,7},{3,5},{5,3},{7,1},{8,14},{10,12},{12... | collective-permute-start | bytes 393224 | tf_op jit(solution)/shard_map/ppermute | solution.py:532
  149.8 63.9 %all-to-all-start.5 = ((bf16[4,4,128,512]{3,2,1,0:T(8,128)(2,1)}), bf16[4,4,128,512]{3,2,1,0:T(8,128)(2,1)}, u32[]{:S(2)}, u32[]{:S(2)}) async-start(bf16[4,4,128,512]{3,2,1,0:T(8,128)(2,1)} %pack_wide.1), calls=%async_computation.5 | async-start | bytes 4194304 | tf_op jit(solution)/shard_map/all_to_all | solution.py:540
  213.7 22.3 %collective-permute-start.18 = (bf16[512,512]{1,0:T(8,128)(2,1)}, bf16[512,512]{1,0:T(8,128)(2,1)}, u32[]{:S(2)}, u32[]{:S(2)}) collective-permute-start(bf16[512,512]{1,0:T(8,128)(2,1)} %copy-done.22), channel_id=1, source_target_pairs={{0,2},{2,0},{4,6},{6,4},{1,3},{3,1},{5,7},{7,5},{8,10},{10,8},{12,... | collective-permute-start | bytes 1572872 | tf_op jit(solution)/shard_map/ppermute | solution.py:532
  213.7 38.1 %collective-permute-start.19 = (bf16[512,512]{1,0:T(8,128)(2,1)}, bf16[512,512]{1,0:T(8,128)(2,1)}, u32[]{:S(2)}, u32[]{:S(2)}) collective-permute-start(bf16[512,512]{1,0:T(8,128)(2,1)} %copy-done.21), channel_id=1, source_target_pairs={{0,4},{2,6},{4,0},{6,2},{1,5},{3,7},{5,1},{7,3},{8,12},{10,14},{12... | collective-permute-start | bytes 1572872 | tf_op jit(solution)/shard_map/ppermute | solution.py:532
  216.6 44.8 %collective-permute-start.20 = (bf16[512,512]{1,0:T(8,128)(2,1)}, bf16[512,512]{1,0:T(8,128)(2,1)}, u32[]{:S(2)}, u32[]{:S(2)}) collective-permute-start(bf16[512,512]{1,0:T(8,128)(2,1)} %copy-done.20), channel_id=1, source_target_pairs={{0,6},{2,4},{4,2},{6,0},{1,7},{3,5},{5,3},{7,1},{8,14},{10,12},{12... | collective-permute-start | bytes 1572872 | tf_op jit(solution)/shard_map/ppermute | solution.py:532
  290.2 65.7 %collective-permute-start.28 = (bf16[4,128,512]{2,1,0:T(8,128)(2,1)S(1)}, bf16[4,128,512]{2,1,0:T(8,128)(2,1)S(1)}, u32[]{:S(2)}, u32[]{:S(2)}) collective-permute-start(bf16[4,128,512]{2,1,0:T(8,128)(2,1)S(1)} %all-to-all-done.6.refs_0_), channel_id=1, source_target_pairs={{0,2},{2,0},{4,6},{6,4},{1,3},{3,1},{5,7},{7,5},{8,10},{10,8},{12,... | collective-permute-start | bytes 1572872 | tf_op jit(solution)/shard_map/ppermute | solution.py:532
  290.3 66.4 %collective-permute-start.29 = (bf16[4,128,512]{2,1,0:T(8,128)(2,1)S(1)}, bf16[4,128,512]{2,1,0:T(8,128)(2,1)S(1)}, u32[]{:S(2)}, u32[]{:S(2)}) collective-permute-start(bf16[4,128,512]{2,1,0:T(8,128)(2,1)S(1)} %all-to-all-done.6.refs_0_), channel_id=1, source_target_pairs={{0,4},{2,6},{4,0},{6,2},{1,5},{3,7},{5,1},{7,3},{8,12},{10,14},{12... | collective-permute-start | bytes 1572872 | tf_op jit(solution)/shard_map/ppermute | solution.py:532
  303.7 27.9 %collective-permute-start.24 = (bf16[2,256,1024]{2,1,0:T(8,128)(2,1)}, bf16[2,256,1024]{2,1,0:T(8,128)(2,1)}, u32[]{:S(2)}, u32[]{:S(2)}) collective-permute-start(bf16[2,256,1024]{2,1,0:T(8,128)(2,1)} %slice.162), channel_id=1, source_target_pairs={{0,8},{8,0},{16,24},{24,16},{1,9},{9,1},{17,25},{25,17},{2,10},{10... | collective-permute-start | bytes 3145736 | tf_op jit(solution)/shard_map/ppermute | solution.py:532
  308.8 27.8 %collective-permute-start.22 = (bf16[2,256,1024]{2,1,0:T(8,128)(2,1)}, bf16[2,256,1024]{2,1,0:T(8,128)(2,1)}, u32[]{:S(2)}, u32[]{:S(2)}) collective-permute-start(bf16[2,256,1024]{2,1,0:T(8,128)(2,1)} %slice.194), channel_id=1, source_target_pairs={{0,16},{8,24},{16,0},{24,8},{1,17},{9,25},{17,1},{25,9},{2,18},{10... | collective-permute-start | bytes 3145736 | tf_op jit(solution)/shard_map/ppermute | solution.py:532
  312.7 44.0 %all-to-all-start.7 = ((f32[32,1,2176]{2,1,0:T(1,128)}), f32[32,1,2176]{2,1,0:T(1,128)}, u32[]{:S(2)}, u32[]{:S(2)}) async-start(f32[32,1,2176]{2,1,0:T(1,128)} %reshape.295), calls=%async_computation.7 | async-start | bytes 557056 | tf_op jit(solution)/shard_map/all_to_all | solution.py:540
  319.5 23.5 %collective-permute-start.25 = (bf16[1,4,64,512]{3,2,1,0:T(8,128)(2,1)S(1)}, bf16[1,4,64,512]{3,2,1,0:T(8,128)(2,1)S(1)}, u32[]{:S(2)}, u32[]{:S(2)}) collective-permute-start(bf16[1,4,64,512]{3,2,1,0:T(8,128)(2,1)S(1)} %get-tuple-element.115), channel_id=1, source_target_pairs={{0,2},{2,0},{4,6},{6,4},{1,3},{3,1},{5,7},{7,5},{8,10},{10,8},{12,... | collective-permute-start | bytes 786440 | tf_op jit(solution)/shard_map/ppermute | solution.py:532
  362.1 19.8 %collective-permute-start.33 = (f32[256,1024]{1,0:T(8,128)}, f32[256,1024]{1,0:T(8,128)}, u32[]{:S(2)}, u32[]{:S(2)}) collective-permute-start(f32[256,1024]{1,0:T(8,128)} %get-tuple-element.158), channel_id=1, source_target_pairs={{0,1},{1,0},{2,3},{3,2},{4,5},{5,4},{6,7},{7,6},{8,9},{9,8},{10,11... | collective-permute-start | bytes 3145736 | tf_op jit(solution)/shard_map/ppermute | solution.py:532
  362.1 19.8 %collective-permute-start.34 = (f32[256,1024]{1,0:T(8,128)}, f32[256,1024]{1,0:T(8,128)}, u32[]{:S(2)}, u32[]{:S(2)}) collective-permute-start(f32[256,1024]{1,0:T(8,128)} %get-tuple-element.157), channel_id=1, source_target_pairs={{0,1},{1,0},{2,3},{3,2},{4,5},{5,4},{6,7},{7,6},{8,9},{9,8},{10,11... | collective-permute-start | bytes 3145736 | tf_op jit(solution)/shard_map/ppermute | solution.py:532
  382.2 20.0 %collective-permute-start.36 = (bf16[1,4,64,512]{3,2,1,0:T(8,128)(2,1)S(1)}, bf16[1,4,64,512]{3,2,1,0:T(8,128)(2,1)S(1)}, u32[]{:S(2)}, u32[]{:S(2)}) collective-permute-start(bf16[1,4,64,512]{3,2,1,0:T(8,128)(2,1)S(1)} %bitcast.186), channel_id=1, source_target_pairs={{0,4},{2,6},{4,0},{6,2},{1,5},{3,7},{5,1},{7,3},{8,12},{10,14},{12... | collective-permute-start | bytes 786440 | tf_op jit(solution)/shard_map/ppermute | solution.py:532
  384.2 23.1 %collective-permute-start.37 = (bf16[1,4,64,512]{3,2,1,0:T(8,128)(2,1)S(1)}, bf16[1,4,64,512]{3,2,1,0:T(8,128)(2,1)S(1)}, u32[]{:S(2)}, u32[]{:S(2)}) collective-permute-start(bf16[1,4,64,512]{3,2,1,0:T(8,128)(2,1)S(1)} %bitcast.187), channel_id=1, source_target_pairs={{0,6},{2,4},{4,2},{6,0},{1,7},{3,5},{5,3},{7,1},{8,14},{10,12},{12... | collective-permute-start | bytes 786440 | tf_op jit(solution)/shard_map/ppermute | solution.py:532
  (84 other events, 722.0 us)
